TPU v7x, 32 devices: a whole 2x2x4 slice. The times are simulated.
32 devices in a mesh: dp: 4 (over z), seq: 8 (over y, x, core).
Axes of the slice: x: 2, y: 2, z: 4, core: 2. Of those that a mesh axis runs over, the one named last changes fastest.
Arguments:
- hidden: bfloat16 [4, 2560, 2048], P('dp', 'seq'), may hold values from -6 to 6
- seg_ids: int32 [4, 2560], P('dp', 'seq'), may hold values from 0 to 1, as said below
- pad_mask: int32 [4, 2560], P('dp', 'seq'), may hold values from 0 to 1, as said below
- attn_gain: bfloat16 [2048], P(('dp', 'seq')), may hold values from 0.25 to 1.75
- gate_gap: bfloat16 [2048], P(('dp', 'seq')), may hold values from 0.0002 to 0.5
- out_gain: bfloat16 [2048], P(('dp', 'seq')), may hold values from 0.25 to 1.75
- w_query: bfloat16 [2048, 2048], P(('dp', 'seq')), may hold values from -0.125 to 0.125
- w_forget: bfloat16 [2048, 2048], P(('dp', 'seq')), may hold values from -0.125 to 0.125
- w_input: bfloat16 [2048, 2048], P(('dp', 'seq')), may hold values from -0.125 to 0.125
- w_output: bfloat16 [2048, 2048], P(('dp', 'seq')), may hold values from -0.125 to 0.125
- ffn_gain: bfloat16 [2048], P(('dp', 'seq')), may hold values from 0.25 to 1.75
- w_gate: bfloat16 [2048, 5632], P(('dp', 'seq')), may hold values from -0.125 to 0.125
- w_up: bfloat16 [2048, 5632], P(('dp', 'seq')), may hold values from -0.125 to 0.125
- w_down: bfloat16 [5632, 2048], P(('dp', 'seq')), may hold values from -0.078125 to 0.078125
- out_grad: bfloat16 [4, 2560, 2048], P('dp', 'seq'), may hold values from -6 to 6
Outputs:
- block_out: bfloat16 [4, 2560, 2048], P('dp', 'seq')
- hidden_grad: bfloat16 [4, 2560, 2048], P('dp', 'seq')
- grad_attn_gain: float32 [2048], P(('dp', 'seq'))
- grad_gate_gap: float32 [2048], P(('dp', 'seq'))
- grad_out_gain: float32 [2048], P(('dp', 'seq'))
- grad_query: float32 [2048, 2048], P(('dp', 'seq'))
- grad_forget: float32 [2048, 2048], P(('dp', 'seq'))
- grad_input: float32 [2048, 2048], P(('dp', 'seq'))
- grad_output: float32 [2048, 2048], P(('dp', 'seq'))
- grad_ffn_gain: float32 [2048], P(('dp', 'seq'))
- grad_gate: float32 [2048, 5632], P(('dp', 'seq'))
- grad_up: float32 [2048, 5632], P(('dp', 'seq'))
- grad_down: float32 [5632, 2048], P(('dp', 'seq'))
Inputs may be any that keep to these rules, and one draw needn't show every extreme that they name: `seg_ids`: in each row the numbers start at 0, never fall and rise by at most one from a token to the next; each sequence holds 1024 tokens or more. `pad_mask`: in each row, 1 on a leading run of tokens and 0 on the rest, which may be empty.
All inputs are finite; a program needn't handle non-finite values.
Results may differ from a plain program's by a relative error of at most 0.012.
Values may be sent and summed in bfloat16 or wider, within the bound.
A program may use at most 448 MiB of HBM per device.

v0:
```python
import jax
import jax.numpy as jnp
from jax import lax
from jax.sharding import PartitionSpec as P

HEADS = 16
BLOCK = 64


EPSILON = 1e-06
STRICT_ARITHMETIC = lax.Precision.HIGHEST


def entering(shard, axis, combine, identity):
    peers, mine = (lax.axis_size(axis), lax.axis_index(axis))
    everything = jax.tree.map(
        lambda part, kind: lax.all_gather(part.astype(kind), axis),
        shard,
        (jnp.bfloat16, jnp.bfloat16, jnp.bfloat16, jnp.bfloat16),
    )
    start = jax.tree.map(
        lambda part, zero: jnp.broadcast_to(jnp.asarray(zero, part.dtype), part.shape),
        shard,
        identity,
    )

    def step(k, before):
        reached = k < mine
        new = combine(
            before, jax.tree.map(lambda part, own: part[k].astype(own.dtype), everything, shard)
        )
        return jax.tree.map(lambda a, b: jnp.where(reached, a, b), new, before)

    return lax.fori_loop(0, peers, step, start)


def entering_2(shard, axis, combine, identity):
    peers, mine = (lax.axis_size(axis), lax.axis_index(axis))
    everything = jax.tree.map(
        lambda part, kind: lax.all_gather(part.astype(kind), axis),
        shard,
        jax.tree.map(lambda a: jnp.bfloat16 if a.dtype == jnp.float32 else a.dtype, shard),
    )
    start = jax.tree.map(
        lambda part, zero: jnp.broadcast_to(jnp.asarray(zero, part.dtype), part.shape),
        shard,
        identity,
    )

    def step(k, before):
        at = peers - 1 - k
        reached = at > mine
        new = combine(
            before, jax.tree.map(lambda part, own: part[at].astype(own.dtype), everything, shard)
        )
        return jax.tree.map(lambda a, b: jnp.where(reached, a, b), new, before)

    return lax.fori_loop(0, peers, step, start)


def normalize(value_rows):
    factor = lax.rsqrt(jnp.mean(value_rows * value_rows, axis=-1, keepdims=True) + EPSILON)
    return (value_rows * factor, factor)


def norm_back(grad_normed, normed, factor):
    return factor * (grad_normed - normed * jnp.mean(grad_normed * normed, axis=-1, keepdims=True))


def contract_last(left, right):
    return lax.dot_general(
        left, right, (((1,), (1,)), ((), ())), preferred_element_type=jnp.float32
    )


def contract_first(left, right):
    return lax.dot_general(
        left, right, (((0,), (0,)), ((), ())), preferred_element_type=jnp.float32
    )


def block_step(carried, inputs):
    present_memory, offset = carried
    probe_vectors, key_part, log_keep, value_rows, segment, before = inputs
    steps_here = probe_vectors.shape[0]
    prefix_accumulations = jnp.cumsum(log_keep, axis=0)
    centre = prefix_accumulations[steps_here // 2]
    scaled_query = probe_vectors * jnp.exp(prefix_accumulations - centre)
    scaled_key = key_part * jnp.exp(centre - prefix_accumulations)
    scores = jnp.einsum("thk,shk->hts", scaled_query, scaled_key, precision=STRICT_ARITHMETIC)
    places = jnp.arange(steps_here)
    allowed = (places[None, :] <= places[:, None]) & (segment[None, :] == segment[:, None])
    scores = jnp.where(allowed[None], scores, jnp.zeros_like(scores))
    inner_part = jnp.einsum("hts,shv->thv", scores, value_rows, precision=STRICT_ARITHMETIC)
    inherited_flag = (segment == before).astype(jnp.float32)
    rank_one_update = (
        jnp.einsum(
            "fsl,slu->fsu",
            probe_vectors * jnp.exp(prefix_accumulations),
            present_memory,
            precision=STRICT_ARITHMETIC,
        )
        * inherited_flag[:, None, None]
    )
    ending = prefix_accumulations[-1]
    tail_ok = (segment == segment[-1]).astype(jnp.float32)
    segment_ends = key_part * jnp.exp(ending - prefix_accumulations) * tail_ok[:, None, None]
    keep_product = jnp.exp(ending) * (segment[-1] == before).astype(jnp.float32)
    updated_state = present_memory * keep_product[:, :, None] + jnp.einsum(
        "ufe,ufc->fec", segment_ends, value_rows, precision=STRICT_ARITHMETIC
    )
    reach_part = probe_vectors * jnp.exp(prefix_accumulations + offset)
    return ((updated_state, offset + ending), (inner_part + rank_one_update, reach_part))


def mixer_local(query_pre, forget_pre, input_pre, gate_gap, segment, live_mask):
    row_tokens = query_pre.shape[0]
    head_width = query_pre.shape[1] // HEADS
    probe_vectors = query_pre * jax.nn.sigmoid(query_pre)
    key_part = gate_gap * jax.nn.sigmoid(-forget_pre)
    log_keep = jnp.log1p(-key_part)
    value_rows = input_pre * live_mask[:, None]
    blocks = row_tokens // BLOCK

    def to_blocks(array):
        return array.reshape(blocks, BLOCK, HEADS, head_width)

    earlier = jnp.concatenate([segment[:1], segment[:-1]])
    before = earlier.reshape(blocks, BLOCK)[:, 0]
    initial = (
        jnp.zeros((HEADS, head_width, head_width), jnp.float32),
        jnp.zeros((HEADS, head_width), jnp.float32),
    )
    (end_state, offset), (mixed_out, reach_query) = lax.scan(
        jax.checkpoint(block_step),
        initial,
        (
            to_blocks(probe_vectors),
            to_blocks(key_part),
            to_blocks(log_keep),
            to_blocks(value_rows),
            segment.reshape(blocks, BLOCK),
            before,
        ),
    )
    return (
        mixed_out.reshape(row_tokens, -1),
        reach_query.reshape(row_tokens, HEADS, head_width),
        end_state,
        jnp.exp(offset),
    )


def chain_forward(earlier, later):
    keep_early, state_early, first_early, last_early = earlier
    keep_late, state_late, first_late, last_late = later
    joined = ((last_early == first_late) | (last_early < 0) | (first_late < 0)).astype(jnp.float32)
    factor = keep_late * joined[:, None, None]
    return (
        keep_early * factor,
        state_late + factor[..., None] * state_early,
        jnp.where(first_early < 0, first_late, first_early),
        jnp.where(last_late < 0, last_early, last_late),
    )


def chain_backward(earlier, later):
    keep_early, grad_early = earlier
    keep_late, grad_late = later
    return (keep_late * keep_early, grad_late + keep_late[..., None] * grad_early)


def on_device(
    hidden,
    seg_ids,
    pad_mask,
    attn_gain,
    gate_gap,
    out_gain,
    w_query,
    w_forget,
    w_input,
    w_output,
    ffn_gain,
    w_gate,
    w_up,
    w_down,
    out_grad,
):
    row_count, row_tokens, model_width = hidden.shape
    all_tokens = row_count * row_tokens
    head_width = model_width // HEADS
    gain_mix, gap_full, gain_out, query_full, forget_full, input_full, output_full = (
        lax.all_gather(attn_gain, ("dp", "seq"), axis=0, tiled=True),
        lax.all_gather(gate_gap, ("dp", "seq"), axis=0, tiled=True),
        lax.all_gather(out_gain, ("dp", "seq"), axis=0, tiled=True),
        lax.all_gather(w_query, ("dp", "seq"), axis=0, tiled=True),
        lax.all_gather(w_forget, ("dp", "seq"), axis=0, tiled=True),
        lax.all_gather(w_input, ("dp", "seq"), axis=0, tiled=True),
        lax.all_gather(w_output, ("dp", "seq"), axis=0, tiled=True),
    )
    flat_input = hidden.reshape(all_tokens, model_width).astype(jnp.float32)
    normed_mix, factor_mix = normalize(flat_input)
    rounded_mix = (normed_mix * gain_mix.astype(jnp.float32)).astype(jnp.bfloat16)
    query_pre = jnp.dot(rounded_mix, query_full, preferred_element_type=jnp.float32)
    forget_pre = jnp.dot(rounded_mix, forget_full, preferred_element_type=jnp.float32)
    input_pre = jnp.dot(rounded_mix, input_full, preferred_element_type=jnp.float32)
    live_rows = pad_mask.astype(jnp.float32)

    def local_mixer(query_in, forget_in, input_in, gap_in):
        shaped = (row_count, row_tokens, model_width)
        return jax.vmap(mixer_local, in_axes=(0, 0, 0, None, 0, 0))(
            query_in.reshape(shaped),
            forget_in.reshape(shaped),
            input_in.reshape(shaped),
            gap_in,
            seg_ids,
            live_rows,
        )

    (mixed_local, reach_query, state_local, keep_local), mixer_pullback = jax.vjp(
        local_mixer, query_pre, forget_pre, input_pre, gap_full.astype(jnp.float32)
    )
    segment_float = seg_ids.astype(jnp.float32)
    first_seg = segment_float[:, 0]
    last_seg = segment_float[:, -1]
    whole_keep = keep_local * (first_seg == last_seg).astype(jnp.float32)[:, None, None]
    identity = (
        jnp.ones_like(whole_keep),
        jnp.zeros_like(state_local),
        jnp.full_like(first_seg, -1.0),
        jnp.full_like(last_seg, -1.0),
    )
    _, state_before, _, last_before = entering(
        (whole_keep, state_local, first_seg, last_seg), "seq", chain_forward, identity
    )
    prior_seg = jnp.where(last_before < 0, first_seg, last_before)
    inherited_flag = (segment_float == prior_seg[:, None]).astype(jnp.float32)[:, :, None, None]
    passing = keep_local * (last_seg == prior_seg).astype(jnp.float32)[:, None, None]
    carried_in = (
        jnp.einsum("rthk,rhkv->rthv", reach_query, state_before, precision=STRICT_ARITHMETIC)
        * inherited_flag
    )
    mixed_all = (mixed_local + carried_in.reshape(row_count, row_tokens, model_width)).reshape(
        all_tokens, model_width
    )
    normed_out, factor_out = normalize(mixed_all)
    mixed_low = (normed_out * gain_out.astype(jnp.float32)).astype(jnp.bfloat16)
    middle = flat_input + jnp.dot(mixed_low, output_full, preferred_element_type=jnp.float32)
    gain_ffn, gate_full, up_full, contraction_matrix = (
        lax.all_gather(ffn_gain, ("dp", "seq"), axis=0, tiled=True),
        lax.all_gather(w_gate, ("dp", "seq"), axis=0, tiled=True),
        lax.all_gather(w_up, ("dp", "seq"), axis=0, tiled=True),
        lax.all_gather(w_down, ("dp", "seq"), axis=0, tiled=True),
    )
    normed_ffn, factor_ffn = normalize(middle)
    rounded_ffn = (normed_ffn * gain_ffn.astype(jnp.float32)).astype(jnp.bfloat16)
    gate_pre = jnp.dot(rounded_ffn, gate_full, preferred_element_type=jnp.float32)
    up_pre = jnp.dot(rounded_ffn, up_full, preferred_element_type=jnp.float32)
    gate_sig = jax.nn.sigmoid(gate_pre)
    gate_act = gate_pre * gate_sig
    hidden_units = (gate_act * up_pre).astype(jnp.bfloat16)
    block_out = middle + jnp.dot(
        hidden_units, contraction_matrix, preferred_element_type=jnp.float32
    )
    grad_low = out_grad.reshape(all_tokens, model_width)
    gain_back, gate_back, up_back, down_back = (
        lax.all_gather(ffn_gain, ("dp", "seq"), axis=0, tiled=True),
        lax.all_gather(w_gate, ("dp", "seq"), axis=0, tiled=True),
        lax.all_gather(w_up, ("dp", "seq"), axis=0, tiled=True),
        lax.all_gather(w_down, ("dp", "seq"), axis=0, tiled=True),
    )
    grad_units = contract_last(grad_low, down_back)
    grad_down = contract_first(hidden_units, grad_low)
    grad_gate_pre = (grad_units * up_pre * gate_sig * (1.0 + gate_pre * (1.0 - gate_sig))).astype(
        jnp.bfloat16
    )
    grad_up_pre = (grad_units * gate_act).astype(jnp.bfloat16)
    grad_gate = contract_first(rounded_ffn, grad_gate_pre)
    grad_up = contract_first(rounded_ffn, grad_up_pre)
    grad_rounded_ffn = contract_last(grad_gate_pre, gate_back) + contract_last(grad_up_pre, up_back)
    grad_gain_ffn = jnp.sum(grad_rounded_ffn * normed_ffn, axis=0)
    grad_middle = grad_low.astype(jnp.float32) + norm_back(
        grad_rounded_ffn * gain_back.astype(jnp.float32), normed_ffn, factor_ffn
    )
    ffn_shares = (
        lax.psum_scatter(grad_gain_ffn, ("dp", "seq"), scatter_dimension=0, tiled=True),
        lax.psum_scatter(grad_gate, ("dp", "seq"), scatter_dimension=0, tiled=True),
        lax.psum_scatter(grad_up, ("dp", "seq"), scatter_dimension=0, tiled=True),
        lax.psum_scatter(grad_down, ("dp", "seq"), scatter_dimension=0, tiled=True),
    )
    grad_mixer_low = grad_middle.astype(jnp.bfloat16)
    gain_mix_back, gain_out_back, query_back, forget_back, input_back, output_back = (
        lax.all_gather(attn_gain, ("dp", "seq"), axis=0, tiled=True),
        lax.all_gather(out_gain, ("dp", "seq"), axis=0, tiled=True),
        lax.all_gather(w_query, ("dp", "seq"), axis=0, tiled=True),
        lax.all_gather(w_forget, ("dp", "seq"), axis=0, tiled=True),
        lax.all_gather(w_input, ("dp", "seq"), axis=0, tiled=True),
        lax.all_gather(w_output, ("dp", "seq"), axis=0, tiled=True),
    )
    grad_mixed_low = contract_last(grad_mixer_low, output_back)
    grad_output = contract_first(mixed_low, grad_mixer_low)
    grad_gain_out = jnp.sum(grad_mixed_low * normed_out, axis=0)
    grad_mixed = norm_back(
        grad_mixed_low * gain_out_back.astype(jnp.float32), normed_out, factor_out
    )
    grad_mixed_heads = grad_mixed.reshape(row_count, row_tokens, HEADS, head_width)
    grad_reach = jnp.einsum(
        "rthv,rhkv->rthk",
        grad_mixed_heads * inherited_flag,
        state_before,
        precision=STRICT_ARITHMETIC,
    )
    local_grad = jnp.einsum(
        "rthk,rthv->rhkv",
        reach_query * inherited_flag,
        grad_mixed_heads,
        precision=STRICT_ARITHMETIC,
    )
    _, state_after = entering_2(
        (passing, local_grad),
        "seq",
        chain_backward,
        (jnp.ones_like(passing), jnp.zeros_like(local_grad)),
    )
    grad_keep = (
        jnp.sum(state_before * state_after, axis=-1)
        * (last_seg == prior_seg).astype(jnp.float32)[:, None, None]
    )
    grad_query_pre, grad_forget_pre, entry_logit_cotan, grad_gap = mixer_pullback(
        (grad_mixed.reshape(row_count, row_tokens, model_width), grad_reach, state_after, grad_keep)
    )
    query_low = grad_query_pre.astype(jnp.bfloat16)
    forget_low = grad_forget_pre.astype(jnp.bfloat16)
    input_low = entry_logit_cotan.astype(jnp.bfloat16)
    grad_query = contract_first(rounded_mix, query_low)
    grad_forget = contract_first(rounded_mix, forget_low)
    grad_input = contract_first(rounded_mix, input_low)
    grad_rounded_mix = (
        contract_last(query_low, query_back)
        + contract_last(forget_low, forget_back)
        + contract_last(input_low, input_back)
    )
    grad_gain_mix = jnp.sum(grad_rounded_mix * normed_mix, axis=0)
    grad_hidden = grad_middle + norm_back(
        grad_rounded_mix * gain_mix_back.astype(jnp.float32), normed_mix, factor_mix
    )
    mixer_shares = (
        lax.psum_scatter(grad_gain_mix, ("dp", "seq"), scatter_dimension=0, tiled=True),
        lax.psum_scatter(grad_gap, ("dp", "seq"), scatter_dimension=0, tiled=True),
        lax.psum_scatter(grad_gain_out, ("dp", "seq"), scatter_dimension=0, tiled=True),
        lax.psum_scatter(grad_query, ("dp", "seq"), scatter_dimension=0, tiled=True),
        lax.psum_scatter(grad_forget, ("dp", "seq"), scatter_dimension=0, tiled=True),
        lax.psum_scatter(grad_input, ("dp", "seq"), scatter_dimension=0, tiled=True),
        lax.psum_scatter(grad_output, ("dp", "seq"), scatter_dimension=0, tiled=True),
    )
    return (
        block_out.reshape(row_count, row_tokens, model_width).astype(jnp.bfloat16),
        grad_hidden.reshape(row_count, row_tokens, model_width).astype(jnp.bfloat16),
        mixer_shares[0],
        mixer_shares[1],
        mixer_shares[2],
        mixer_shares[3],
        mixer_shares[4],
        mixer_shares[5],
        mixer_shares[6],
        ffn_shares[0],
        ffn_shares[1],
        ffn_shares[2],
        ffn_shares[3],
    )


def solution(mesh):
    return jax.shard_map(
        on_device,
        mesh=mesh,
        in_specs=(
            P("dp", "seq", None),
            P("dp", "seq"),
            P("dp", "seq"),
            P(("dp", "seq")),
            P(("dp", "seq")),
            P(("dp", "seq")),
            P(("dp", "seq"), None),
            P(("dp", "seq"), None),
            P(("dp", "seq"), None),
            P(("dp", "seq"), None),
            P(("dp", "seq")),
            P(("dp", "seq"), None),
            P(("dp", "seq"), None),
            P(("dp", "seq"), None),
            P("dp", "seq", None),
        ),
        out_specs=(
            P("dp", "seq", None),
            P("dp", "seq", None),
            P(("dp", "seq")),
            P(("dp", "seq")),
            P(("dp", "seq")),
            P(("dp", "seq"), None),
            P(("dp", "seq"), None),
            P(("dp", "seq"), None),
            P(("dp", "seq"), None),
            P(("dp", "seq")),
            P(("dp", "seq"), None),
            P(("dp", "seq"), None),
            P(("dp", "seq"), None),
        ),
        check_vma=False,
    )
```

profile of v0, /device:TPU:0, one launch (start us, length us, event | category | flops | bytes accessed | tf_op | source)
XLA Modules:
  0.0 3284.5 jit_solution(9409346578336874424)
XLA Ops:
  12.9 42.6 %all-reduce.13 = (bf16[2048]{0:T(1024)(128)(2,1)S(1)}, bf16[2048]{0:T(1024)(128)(2,1)S(1)}, bf16[2048]{0:T(1024)(128)(2,1)S(1)}, bf16[2048]{0:T(1024)(128)(2,1)S(1)}) all-reduce(bf16[2048]{0:T(1024)(128)(2,1)S(1)} %dynamic-update-slice.1, bf16[2048]{0:T(1024)(128)(2,1)S(1)} %dynamic-update-slice, ...), channel_id=1, replica_groups=mesh['dp'=4,'seq'=8] {'dp','seq'}, use_global_device_ids=true, to_apply=%add.3 | all-reduce | flops 8192 | bytes 32768
  62.2 29.1 all-gather.16.cloned.1.call-done
  102.8 67.5 %all-gather.18.cloned.1.call-done = bf16[2048,2048]{1,0:T(8,128)(2,1)} async-done(((bf16[64,2048]{1,0:T(8,128)(2,1)}), bf16[2048,2048]{1,0:T(8,128)(2,1)}) %all-gather.18.cloned.1.call-update) | async-done | bytes 8388624 | tf_op jit(solution)/shard_map/all_gather | solution.py:199
  178.5 70.7 %all-gather.20.cloned.1.call-done = bf16[2048,2048]{1,0:T(8,128)(2,1)} async-done(((bf16[64,2048]{1,0:T(8,128)(2,1)}), bf16[2048,2048]{1,0:T(8,128)(2,1)}) %all-gather.20.cloned.1.call-update) | async-done | bytes 8388624 | tf_op jit(solution)/shard_map/all_gather | solution.py:197
  261.7 91.7 %while.79 = (s32[]{:T(128)}, f32[1,16,128,128]{3,2,1,0:T(8,128)S(1)}, f32[1,16,128]{2,1,0:T(8,128)S(1)}, f32[5,1,64,16,128]{4,2,3,1,0:T(8,128)}, f32[5,1,64,16,1...) while((s32[]{:T(128)}, ...), condition=%wide.region_3.4_spmd.clone, body=%wide.region_1.3_spmd.clone.sunk | while | flops 615207168 | bytes 16919284 | solution.py:134
  391.4 39.9 %while.80 = (s32[]{:T(128)}, f32[1,16,128,128]{3,2,1,0:T(8,128)S(1)}, f32[1]{0:T(128)}, s32[]{:T(128)}, bf16[8,1,16,128,128]{4,3,2,1,0:T(8,128)(2,1)}, /*index=5...) while((s32[]{:T(128)}, ...), condition=%wide.region_5.6_spmd.clone, body=%wide.region_4.5_spmd.clone.sunk | while | flops 1314829 | bytes 2642146 | solution.py:34
  447.2 22.7 all-gather.22.cloned.1.call-done
  478.0 137.8 %all-gather.24.cloned.1.call-done = bf16[2048,5632]{1,0:T(8,128)(2,1)} async-done(((bf16[64,5632]{1,0:T(8,128)(2,1)}), bf16[2048,5632]{1,0:T(8,128)(2,1)}) %all-gather.24.cloned.1.call-update) | async-done | bytes 23068688 | tf_op jit(solution)/shard_map/all_gather | solution.py:252
  615.8 15.4 fusion.182
  631.2 130.3 %all-gather.26.cloned.1.call-done = bf16[2048,5632]{1,0:T(8,128)(2,1)} async-done(((bf16[64,5632]{1,0:T(8,128)(2,1)}), bf16[2048,5632]{1,0:T(8,128)(2,1)}) %all-gather.26.cloned.1.call-update) | async-done | bytes 23068688 | tf_op jit(solution)/shard_map/all_gather | solution.py:253
  761.5 14.9 fusion.183
  776.4 130.7 %all-gather.28.cloned.1.call-done = bf16[5632,2048]{1,0:T(8,128)(2,1)} async-done(((bf16[176,2048]{1,0:T(8,128)(2,1)}), bf16[5632,2048]{1,0:T(8,128)(2,1)}) %all-gather.28.cloned.1.call-update) | async-done | bytes 23068688 | tf_op jit(solution)/shard_map/all_gather | solution.py:254
  907.1 21.2 multiply_convert_fusion
  942.5 16.5 multiply_reduce_fusion.1
  1037.0 186.7 %while.78 = (s32[]{:T(128)}, f32[1,16,128,128]{2,3,1,0:T(8,128)S(1)}, f32[1,16,128]{2,1,0:T(8,128)S(1)}, f32[5,1,64,16,128]{4,3,2,0,1:T(8,128)}, f32[5,1,64,16,1...) while((s32[]{:T(128)}, ...), condition=%wide.region_21.22_spmd, body=%wide.region_13.21_spmd.sunk | while | flops 1334462720 | bytes 46177060 | solution.py:134
  1267.8 20.4 fusion.186
  1288.3 20.4 fusion.187
  1310.1 20.7 fusion.143
  1363.7 42.9 %all-reduce.12 = (f32[2048]{0:T(1024)S(1)}, f32[2048]{0:T(1024)S(1)}, f32[2048]{0:T(1024)S(1)}, f32[2048]{0:T(1024)S(1)}) all-reduce(f32[2048]{0:T(1024)S(1)} %get-tuple-element.1039, f32[2048]{0:T(1024)S(1)} %get-tuple-element.1168, f32[2048]{0:T(1024)S(1)} %copy-done.33, ...), channel_id=8, replica_groups=mesh['dp'=4,'seq'=8] {'dp','seq'}, use_global_device_ids=true, to_apply=%region_24.25.clone | all-reduce | flops 8192 | bytes 65536
  1421.9 187.2 %reduce-scatter.10.cloned.1.call-done = f32[64,2048]{1,0:T(8,128)} async-done(((f32[2048,2048]{1,0:T(8,128)}), f32[64,2048]{1,0:T(8,128)}) %reduce-scatter.10.cloned.1.call-update) | async-done | bytes 524304 | tf_op jit(solution)/shard_map/reduce_scatter | solution.py:353
  1609.1 187.2 %reduce-scatter.12.cloned.1.call-done = f32[64,2048]{1,0:T(8,128)} async-done(((f32[2048,2048]{1,0:T(8,128)}), f32[64,2048]{1,0:T(8,128)}) %reduce-scatter.12.cloned.1.call-update) | async-done | bytes 524304 | tf_op jit(solution)/shard_map/reduce_scatter | solution.py:354
  1796.4 489.5 %reduce-scatter.16.cloned.1.call-done = f32[64,5632]{1,0:T(8,128)} async-done(((f32[2048,5632]{1,0:T(8,128)}), f32[64,5632]{1,0:T(8,128)}) %reduce-scatter.16.cloned.1.call-update) | async-done | bytes 1441808 | tf_op jit(solution)/shard_map/reduce_scatter | solution.py:288
  2285.9 495.8 %reduce-scatter.18.cloned.1.call-done = f32[64,5632]{1,0:T(8,128)} async-done(((f32[2048,5632]{1,0:T(8,128)}), f32[64,5632]{1,0:T(8,128)}) %reduce-scatter.18.cloned.1.call-update) | async-done | bytes 1441808 | tf_op jit(solution)/shard_map/reduce_scatter | solution.py:289
  2781.7 495.8 %reduce-scatter.20.cloned.1.call-done = f32[176,2048]{1,0:T(8,128)} async-done(((f32[5632,2048]{1,0:T(8,128)}), f32[176,2048]{1,0:T(8,128)}) %reduce-scatter.20.cloned.1.call-update) | async-done | bytes 1441808 | tf_op jit(solution)/shard_map/reduce_scatter | solution.py:290
  (513 shorter events, 588.0 us)
Async XLA Ops:
  7.2 84.1 %all-gather.16.cloned.1.call-start = ((), (), s32[]{:S(2)}) async-start(), calls=%async_computation.7 | async-start | bytes 8650752 | tf_op jit(solution)/shard_map/all_gather | solution.py:198
  7.9 162.4 %all-gather.18.cloned.1.call-start = ((), (), s32[]{:S(2)}) async-start(), calls=%async_computation.8 | async-start | bytes 8650752 | tf_op jit(solution)/shard_map/all_gather | solution.py:199
  8.7 240.6 %all-gather.20.cloned.1.call-start = ((), (), s32[]{:S(2)}) async-start(), calls=%async_computation.9 | async-start | bytes 8650752 | tf_op jit(solution)/shard_map/all_gather | solution.py:197
  9.4 382.0 %all-gather.30.cloned.1.call-start = ((), (), s32[]{:S(2)}) async-start(), calls=%async_computation.21 | async-start | bytes 4718592 | tf_op jit(solution)/shard_map/all_gather | solution.py:17
  55.5 193.7 %copy-start.22 = (f32[2048]{0:T(1024)}, f32[2048]{0:T(1024)S(1)}, u32[]{:S(2)}) copy-start(f32[2048]{0:T(1024)S(1)} %convert_element_type.263) | copy-start | bytes 24580
  55.5 41.7 %copy-start.26 = (f32[2048]{0:T(1024)}, f32[2048]{0:T(1024)S(1)}, u32[]{:S(2)}) copy-start(f32[2048]{0:T(1024)S(1)} %convert_element_type.262) | copy-start | bytes 24580
  60.4 109.9 %copy-start.30 = (f32[320]{0:T(512)}, f32[320]{0:T(512)S(1)}, u32[]{:S(2)}) copy-start(f32[320]{0:T(512)S(1)} %convert_reduce_fusion) | copy-start | bytes 3844
  62.2 187.0 %copy-start.24 = (f32[320]{0:T(512)}, f32[320]{0:T(512)S(1)}, u32[]{:S(2)}) copy-start(f32[320]{0:T(512)S(1)} %add_rsqrt_fusion.2) | copy-start | bytes 3844
  100.8 69.5 %copy-start = (bf16[1,320,2048]{2,1,0:T(8,128)(2,1)S(1)}, bf16[1,320,2048]{2,1,0:T(8,128)(2,1)}, u32[]{:S(2)}) copy-start(bf16[1,320,2048]{2,1,0:T(8,128)(2,1)} %param.23) | copy-start | bytes 3932164
  353.3 28.9 copy-start.29
  354.2 115.6 %all-gather.22.cloned.1.call-start = ((), (), s32[]{:S(2)}) async-start(), calls=%async_computation.10 | async-start | bytes 8650752 | tf_op jit(solution)/shard_map/all_gather | solution.py:200
  354.8 261.0 %all-gather.24.cloned.1.call-start = ((), (), s32[]{:S(2)}) async-start(), calls=%async_computation.11 | async-start | bytes 23789568 | tf_op jit(solution)/shard_map/all_gather | solution.py:252
  355.4 406.0 %all-gather.26.cloned.1.call-start = ((), (), s32[]{:S(2)}) async-start(), calls=%async_computation.12 | async-start | bytes 23789568 | tf_op jit(solution)/shard_map/all_gather | solution.py:253
  356.1 550.9 %all-gather.28.cloned.1.call-start = ((), (), s32[]{:S(2)}) async-start(), calls=%async_computation.13 | async-start | bytes 23789568 | tf_op jit(solution)/shard_map/all_gather | solution.py:254
  356.9 658.5 %all-gather.32.cloned.1.call-start = ((), (), s32[]{:S(2)}) async-start(), calls=%async_computation.22 | async-start | bytes 4718592 | tf_op jit(solution)/shard_map/all_gather | solution.py:40
  391.4 40.5 %copy-start.28 = (s32[1,320]{1,0:T(1,128)S(1)}, s32[1,320]{1,0:T(1,128)}, u32[]{:S(2)}) copy-start(s32[1,320]{1,0:T(1,128)} %param.24) | copy-start | bytes 3844
  478.0 283.4 %copy-start.11 = (bf16[320,2048]{1,0:T(8,128)(2,1)}, bf16[320,2048]{1,0:T(8,128)(2,1)S(1)}, u32[]{:S(2)}) copy-start(bf16[320,2048]{1,0:T(8,128)(2,1)S(1)} %multiply_convert_fusion.4) | copy-start | bytes 3932164
  980.3 433.0 %reduce-scatter.14.cloned.1.call-start = ((), (), s32[]{:S(2)}) async-start(), calls=%async_computation.17 | async-start | bytes 17301504 | tf_op jit(solution)/shard_map/reduce_scatter | solution.py:355
  1006.5 415.5 %reduce-scatter.8.cloned.1.call-start = ((), (), s32[]{:S(2)}) async-start(), calls=%async_computation.14 | async-start | bytes 17301504 | tf_op jit(solution)/shard_map/reduce_scatter | solution.py:352
  1237.4 371.8 %reduce-scatter.10.cloned.1.call-start = ((), (), s32[]{:S(2)}) async-start(), calls=%async_computation.15 | async-start | bytes 17301504 | tf_op jit(solution)/shard_map/reduce_scatter | solution.py:353
  1253.9 542.4 %reduce-scatter.12.cloned.1.call-start = ((), (), s32[]{:S(2)}) async-start(), calls=%async_computation.16 | async-start | bytes 17301504 | tf_op jit(solution)/shard_map/reduce_scatter | solution.py:354
  1266.5 1019.4 %reduce-scatter.16.cloned.1.call-start = ((), (), s32[]{:S(2)}) async-start(), calls=%async_computation.18 | async-start | bytes 47579136 | tf_op jit(solution)/shard_map/reduce_scatter | solution.py:288
  1288.3 1493.4 %reduce-scatter.18.cloned.1.call-start = ((), (), s32[]{:S(2)}) async-start(), calls=%async_computation.19 | async-start | bytes 47579136 | tf_op jit(solution)/shard_map/reduce_scatter | solution.py:289
  1308.7 1968.8 %reduce-scatter.20.cloned.1.call-start = ((), (), s32[]{:S(2)}) async-start(), calls=%async_computation.20 | async-start | bytes 47579136 | tf_op jit(solution)/shard_map/reduce_scatter | solution.py:290
  (30 other events, 130.9 us)
Sparse Core Ops, SparseCore 0:
  10.9 80.3 all-gather.15
  94.2 76.0 all-gather.17
  173.1 76.0 all-gather.19
  354.4 35.4 all-gather.29
  392.5 77.2 all-gather.21
  472.6 143.1 all-gather.23
  618.6 142.7 all-gather.25
  764.3 142.7 all-gather.27
  980.5 34.8 all-gather.31
  1018.1 182.8 reduce-scatter.13
  1237.5 184.3 reduce-scatter.7
  1424.6 184.4 reduce-scatter.9
  1612.0 184.3 reduce-scatter.11
  1799.1 486.7 reduce-scatter.15
  2288.6 493.0 reduce-scatter.17
  2784.4 493.0 reduce-scatter.19
where the time goes:
time: 3310 us; the launch traced here: 3280 us
  waiting for transfers between devices  2470 us (75%)
  matrix products  364 us (11%)
  other arithmetic  157 us (5%)
  local copies, waits for them, and re-layouts  128 us (4%)
  blocking collectives  117 us (4%)
  loops' own time  33.4 us (1%)
    reduce_scatter x1, waiting for transfers between devices, on_device(): lax.psum_scatter(grad_down, ('dp', 'seq'), scatter_dimension=0, tiled=True)  496 us
    reduce_scatter x1, waiting for transfers between devices, on_device(): lax.psum_scatter(grad_up, ('dp', 'seq'), scatter_dimension=0, tiled=True)  496 us
    reduce_scatter x1, waiting for transfers between devices, on_device(): lax.psum_scatter(grad_gate, ('dp', 'seq'), scatter_dimension=0, tiled=True)  490 us
    reduce_scatter x1, waiting for transfers between devices, on_device(): lax.psum_scatter(grad_forget, ('dp', 'seq'), scatter_dimension=0, tiled=T...  187 us
    reduce_scatter x1, waiting for transfers between devices, on_device(): lax.psum_scatter(grad_input, ('dp', 'seq'), scatter_dimension=0, tiled=True)  187 us
    all_gather x1, waiting for transfers between devices, on_device(): lax.all_gather(w_gate, ('dp', 'seq'), axis=0, tiled=True)  138 us
    all_gather x1, waiting for transfers between devices, on_device(): lax.all_gather(w_down, ('dp', 'seq'), axis=0, tiled=True)  131 us
    all_gather x1, waiting for transfers between devices, on_device(): lax.all_gather(w_up, ('dp', 'seq'), axis=0, tiled=True)  130 us
  transfers between devices with their start and end apart: 16, of which 14 were waited for; matrix products, arithmetic and copies ran while one was open for 14% of the time, Pallas kernels for 0%

commit v1 on v0

v1 whole, which is shorter than its diff:
```python
import functools

import jax
import jax.numpy as jnp
from jax import lax
from jax.experimental import pallas as pl
from jax.experimental.pallas import tpu as pltpu
from jax.sharding import PartitionSpec as P

HEADS = 16
BLOCK = 64
UNROLL = 2
EPSILON = 1e-06
BF = jnp.bfloat16
F32 = jnp.float32


def dot(a, b, dims):
    return lax.dot_general(a, b, (dims, ((), ())), preferred_element_type=F32)


def nn(a, b):
    return dot(a, b, ((1,), (0,)))


def nt(a, b):
    return dot(a, b, ((1,), (1,)))


def tn(a, b):
    return dot(a, b, ((0,), (0,)))


def split_sum(tri, v):
    high = v.astype(BF)
    low = (v - high.astype(F32)).astype(BF)
    return nn(tri, high) + nn(tri, low)


def chunk_prep(qfi, gap, live, width):
    query_pre, forget_pre, input_pre = (
        qfi[:, :width],
        qfi[:, width : 2 * width],
        qfi[:, 2 * width :],
    )
    sig_q = jax.nn.sigmoid(query_pre)
    sig_nf = jax.nn.sigmoid(-forget_pre)
    key = gap * sig_nf
    return query_pre, sig_q, sig_nf, key, input_pre * live


def triangle(lower):
    row = lax.broadcasted_iota(jnp.int32, (BLOCK, BLOCK), 0)
    col = lax.broadcasted_iota(jnp.int32, (BLOCK, BLOCK), 1)
    return (row >= col) if lower else (row <= col)


def chunk_masks(cut):
    row = lax.broadcasted_iota(jnp.int32, (BLOCK, BLOCK), 0)
    col = lax.broadcasted_iota(jnp.int32, (BLOCK, BLOCK), 1)
    allowed = (row >= col) & ((row >= cut) == (col >= cut))
    at = lax.broadcasted_iota(jnp.int32, (BLOCK, 1), 0)
    inherits = (at < cut).astype(F32)
    tail = ((at >= cut) | (cut >= BLOCK)).astype(F32)
    whole = (cut >= BLOCK).astype(F32)
    return allowed, inherits, tail, whole


def mixer_forward_kernel(heads, cut_ref, live_ref, qfi_ref, gap_ref, mixed_ref, square_ref, kept_ref, state):
    step = pl.program_id(0)
    width = heads * 128

    @pl.when(step == 0)
    def _():
        state[...] = jnp.zeros_like(state)

    lower = triangle(True).astype(BF)
    for u in range(UNROLL):
        chunk = step * UNROLL + u
        rows = slice(u * BLOCK, (u + 1) * BLOCK)
        at = lax.broadcasted_iota(jnp.int32, (BLOCK, 1), 0) + chunk * BLOCK
        live = (at < live_ref[0]).astype(F32)
        query_pre, sig_q, sig_nf, key, value = chunk_prep(qfi_ref[rows, :], gap_ref[...], live, width)
        query = query_pre * sig_q
        total = split_sum(lower, jnp.log1p(-key))
        centre = total[BLOCK // 2 : BLOCK // 2 + 1]
        ending = total[BLOCK - 1 :]
        scaled_q = (query * jnp.exp(total - centre)).astype(BF)
        scaled_k = (key * jnp.exp(centre - total)).astype(BF)
        value_low = value.astype(BF)
        allowed, inherits, tail, whole = chunk_masks(cut_ref[chunk])
        value_tail = (value * tail).astype(BF)
        e_centre = jnp.exp(centre)
        e_rest = jnp.exp(ending - centre)
        e_all = jnp.exp(ending) * whole
        square = jnp.zeros((BLOCK, 1), F32)
        for h in range(heads):
            cols = slice(h * 128, (h + 1) * 128)
            before = state[h]
            kept_ref[u, h] = before.astype(BF)
            scores = jnp.where(allowed, nt(scaled_q[:, cols], scaled_k[:, cols]), 0.0)
            inner = nn(scores.astype(BF), value_low[:, cols])
            outer = nt(scaled_q[:, cols], (before * e_centre[:, cols]).astype(BF))
            mixed = inner + outer * inherits
            square = square + jnp.sum(mixed * mixed, axis=1, keepdims=True)
            mixed_ref[rows, cols] = mixed.astype(BF)
            state[h] = before * e_all[:, cols] + tn(value_tail[:, cols], scaled_k[:, cols]) * e_rest[:, cols]
        square_ref[rows, :] = square


def mixer_backward_kernel(heads, cut_ref, live_ref, qfi_ref, gap_ref, kept_ref, grad_ref, out_ref, gap_out_ref, state):
    step = pl.program_id(0)
    last = pl.num_programs(0) - 1
    width = heads * 128

    @pl.when(step == 0)
    def _():
        state[...] = jnp.zeros_like(state)
        gap_out_ref[...] = jnp.zeros_like(gap_out_ref)

    lower = triangle(True).astype(BF)
    upper = triangle(False).astype(BF)
    for u in reversed(range(UNROLL)):
        chunk = (last - step) * UNROLL + u
        rows = slice(u * BLOCK, (u + 1) * BLOCK)
        at = lax.broadcasted_iota(jnp.int32, (BLOCK, 1), 0) + chunk * BLOCK
        live = (at < live_ref[0]).astype(F32)
        gap = gap_ref[...]
        query_pre, sig_q, sig_nf, key, value = chunk_prep(qfi_ref[rows, :], gap, live, width)
        query = query_pre * sig_q
        total = split_sum(lower, jnp.log1p(-key))
        centre = total[BLOCK // 2 : BLOCK // 2 + 1]
        ending = total[BLOCK - 1 :]
        e_q = jnp.exp(total - centre)
        e_k = jnp.exp(centre - total)
        scaled_q = (query * e_q).astype(BF)
        scaled_k = (key * e_k).astype(BF)
        value_low = value.astype(BF)
        allowed, inherits, tail, whole = chunk_masks(cut_ref[chunk])
        value_tail = (value * tail).astype(BF)
        grad = grad_ref[rows, :]
        grad_in = (grad.astype(F32) * inherits).astype(BF)
        e_centre = jnp.exp(centre)
        e_rest = jnp.exp(ending - centre)
        e_all = jnp.exp(ending) * whole
        d_query, d_key, d_value, d_total, d_end = [], [], [], [], []
        for h in range(heads):
            cols = slice(h * 128, (h + 1) * 128)
            before = kept_ref[u, h].astype(F32)
            after = state[h]
            q, k, v, g, gi = scaled_q[:, cols], scaled_k[:, cols], value_low[:, cols], grad[:, cols], grad_in[:, cols]
            vt = value_tail[:, cols]
            scores = jnp.where(allowed, nt(q, k), 0.0).astype(BF)
            d_scores = jnp.where(allowed, nt(g, v), 0.0).astype(BF)
            shifted = (before * e_centre[:, cols]).astype(BF)
            onward = (after * e_rest[:, cols]).astype(BF)
            dq = nn(d_scores, k) + nn(gi, shifted)
            dk_state = nn(vt, onward)
            dk = tn(d_scores, q) + dk_state
            dv = tn(scores, g) + nt(k, onward) * tail
            k32 = k.astype(F32)
            d_total.append(dq * q.astype(F32) - dk * k32)
            d_end.append(
                jnp.sum(after * before, axis=0, keepdims=True) * e_all[:, cols]
                + jnp.sum(dk_state * k32, axis=0, keepdims=True)
            )
            state[h] = after * e_all[:, cols] + tn(gi, q) * e_centre[:, cols]
            d_query.append(dq)
            d_key.append(dk)
            d_value.append(dv)
        d_query = jnp.concatenate(d_query, axis=1) * e_q
        d_key = jnp.concatenate(d_key, axis=1) * e_k
        d_value = jnp.concatenate(d_value, axis=1) * live
        d_log = split_sum(upper, jnp.concatenate(d_total, axis=1)) + jnp.concatenate(d_end, axis=1)
        d_key = d_key - d_log / (1.0 - key)
        gap_out_ref[...] += jnp.sum(d_key * sig_nf, axis=0, keepdims=True)
        out_ref[rows, :width] = (d_query * sig_q * (1.0 + query_pre * (1.0 - sig_q))).astype(BF)
        out_ref[rows, width : 2 * width] = (-d_key * key * (1.0 - sig_nf)).astype(BF)
        out_ref[rows, 2 * width :] = d_value.astype(BF)


def mixer_forward(cut, live, qfi, gap):
    tokens, heads = qfi.shape[0], gap.shape[1] // 128
    width, span = heads * 128, UNROLL * BLOCK
    steps = tokens // span
    return pl.pallas_call(
        functools.partial(mixer_forward_kernel, heads),
        grid_spec=pltpu.PrefetchScalarGridSpec(
            num_scalar_prefetch=2,
            grid=(steps,),
            in_specs=[
                pl.BlockSpec((span, 3 * width), lambda i, *_: (i, 0)),
                pl.BlockSpec((1, width), lambda i, *_: (0, 0)),
            ],
            out_specs=[
                pl.BlockSpec((span, width), lambda i, *_: (i, 0)),
                pl.BlockSpec((span, 1), lambda i, *_: (i, 0)),
                pl.BlockSpec((UNROLL, heads, 128, 128), lambda i, *_: (i, 0, 0, 0)),
            ],
            scratch_shapes=[pltpu.VMEM((heads, 128, 128), F32)],
        ),
        out_shape=[
            jax.ShapeDtypeStruct((tokens, width), BF),
            jax.ShapeDtypeStruct((tokens, 1), F32),
            jax.ShapeDtypeStruct((tokens // BLOCK, heads, 128, 128), BF),
        ],
        cost_estimate=pl.CostEstimate(
            flops=tokens * width * 128 * 10, bytes_accessed=tokens * width * 20, transcendentals=tokens * width * 6
        ),
        name="mixer_forward",
    )(cut, live, qfi, gap)


def mixer_backward(cut, live, qfi, gap, kept, grad):
    tokens, heads = qfi.shape[0], gap.shape[1] // 128
    width, span = heads * 128, UNROLL * BLOCK
    steps = tokens // span
    return pl.pallas_call(
        functools.partial(mixer_backward_kernel, heads),
        grid_spec=pltpu.PrefetchScalarGridSpec(
            num_scalar_prefetch=2,
            grid=(steps,),
            in_specs=[
                pl.BlockSpec((span, 3 * width), lambda i, *_: (steps - 1 - i, 0)),
                pl.BlockSpec((1, width), lambda i, *_: (0, 0)),
                pl.BlockSpec((UNROLL, heads, 128, 128), lambda i, *_: (steps - 1 - i, 0, 0, 0)),
                pl.BlockSpec((span, width), lambda i, *_: (steps - 1 - i, 0)),
            ],
            out_specs=[
                pl.BlockSpec((span, 3 * width), lambda i, *_: (steps - 1 - i, 0)),
                pl.BlockSpec((1, width), lambda i, *_: (0, 0)),
            ],
            scratch_shapes=[pltpu.VMEM((heads, 128, 128), F32)],
        ),
        out_shape=[
            jax.ShapeDtypeStruct((tokens, 3 * width), BF),
            jax.ShapeDtypeStruct((1, width), F32),
        ],
        cost_estimate=pl.CostEstimate(
            flops=tokens * width * 128 * 24, bytes_accessed=tokens * width * 28, transcendentals=tokens * width * 6
        ),
        name="mixer_backward",
    )(cut, live, qfi, gap, kept, grad)


def gather_seq(v):
    return lax.all_gather(v, "seq", axis=0, tiled=True)


def scatter_seq(v):
    return lax.psum_scatter(v, "seq", scatter_dimension=0, tiled=True).astype(F32)


def gather_dp(v):
    return lax.all_gather(v, "dp", axis=0, tiled=True)


def scatter_dp(v):
    return lax.psum_scatter(v, "dp", scatter_dimension=0, tiled=True)


def swap_seq(v):
    return lax.all_to_all(v, "seq", split_axis=0, concat_axis=0, tiled=True)


def inverse_rms(square_mean):
    return lax.rsqrt(square_mean + EPSILON)


def on_device(
    hidden,
    seg_ids,
    pad_mask,
    attn_gain,
    gate_gap,
    out_gain,
    w_query,
    w_forget,
    w_input,
    w_output,
    ffn_gain,
    w_gate,
    w_up,
    w_down,
    out_grad,
):
    planes, ranks = lax.axis_size("dp"), lax.axis_size("seq")
    row_tokens, model = hidden.shape[1:]
    rows = w_query.shape[0]
    units_in = w_down.shape[0]
    head = model // HEADS
    span = head // rows
    per_rank, groups = planes // span, ranks // span
    channels = per_rank * head
    units = planes * units_in
    tokens = ranks * row_tokens
    members = [[a * span + m for m in range(span)] for a in range(groups)]

    def to_heads(w):
        parts = w.reshape(rows, span, per_rank, groups, head)
        return parts.transpose(3, 1, 0, 2, 4).reshape(ranks, rows, channels)

    def from_heads(parts):
        parts = parts.reshape(groups, span, rows, per_rank, head)
        return parts.transpose(2, 1, 3, 0, 4).reshape(rows, model)

    def to_units(w):
        parts = w.reshape(rows, planes, ranks, units_in)
        return parts.transpose(2, 0, 1, 3).reshape(ranks, rows, units)

    def from_units(parts):
        parts = parts.reshape(ranks, rows, planes, units_in)
        return parts.transpose(1, 2, 0, 3).reshape(rows, planes * ranks * units_in)

    def own_rows(v):
        return v.reshape((span, per_rank) + v.shape[1:])

    def swap_group(v):
        return lax.all_to_all(v, "seq", split_axis=0, concat_axis=0, axis_index_groups=members)

    gain_a, gain_o, gain_f = (g.astype(F32)[:, None] for g in (attn_gain, out_gain, ffn_gain))

    def fold(gain, w):
        return (gain * w.astype(F32)).astype(BF)

    qfi_part = jnp.concatenate([to_heads(fold(gain_a, w)) for w in (w_query, w_forget, w_input)], axis=2)
    qfi_full = gather_dp(swap_seq(qfi_part).reshape(ranks * rows, 3 * channels))
    gap_pieces = lax.all_gather(gate_gap, "dp", axis=0)
    gap_own = swap_group(own_rows(gap_pieces)).transpose(1, 0, 2).reshape(1, channels).astype(F32)
    out_pieces = lax.all_gather(fold(gain_o, w_output), "dp", axis=0)
    out_own = swap_group(own_rows(out_pieces)).transpose(1, 0, 2, 3).reshape(channels, model)
    gu_part = jnp.concatenate([to_units(fold(gain_f, w)) for w in (w_gate, w_up)], axis=2)
    gu_full = gather_dp(swap_seq(gu_part).reshape(ranks * rows, 2 * units))
    down_own = gather_dp(w_down)

    ids = lax.all_gather(jnp.concatenate([seg_ids, pad_mask], axis=0), "seq", axis=0)
    segment = ids[:, 0].reshape(tokens // BLOCK, BLOCK)
    live = jnp.sum(ids[:, 1]).reshape(1)
    ends = segment[:, -1]
    before = jnp.concatenate([segment[:1, 0], ends[:-1]])
    cut = jnp.sum((segment == before[:, None]).astype(jnp.int32), axis=1)

    x = hidden[0].astype(F32)
    factor_x = inverse_rms(jnp.mean(x * x, axis=1, keepdims=True))
    normed_x = x * factor_x
    n1 = gather_seq(normed_x.astype(BF))
    qfi = nn(n1, qfi_full)
    mixed, square, kept = mixer_forward(cut, live, qfi, gap_own)
    square_all = lax.psum_scatter(square, "seq", scatter_dimension=0, tiled=True)
    factor_o = inverse_rms(square_all / model)
    attn_out = factor_o * scatter_seq(nn(mixed, out_own).astype(BF))
    middle = x + attn_out
    factor_m = inverse_rms(jnp.mean(middle * middle, axis=1, keepdims=True))
    normed_m = middle * factor_m
    n2 = gather_seq(normed_m.astype(BF))
    gate_up = nn(n2, gu_full)
    gate, up = gate_up[:, :units], gate_up[:, units:]
    sig_g = jax.nn.sigmoid(gate)
    act = gate * sig_g
    hidden_units = (act * up).astype(BF)
    block_out = middle + scatter_seq(nn(hidden_units, down_own).astype(BF))

    grad_all = gather_seq(out_grad[0])
    d_units = nt(grad_all, down_own)
    grad_down = tn(hidden_units, grad_all).astype(BF)
    d_gate = (d_units * up * sig_g * (1.0 + gate * (1.0 - sig_g))).astype(BF)
    d_up = (d_units * act).astype(BF)
    d_gu = jnp.concatenate([d_gate, d_up], axis=1)
    grad_gu = tn(n2, d_gu).astype(BF)
    d_n2 = scatter_seq(nt(d_gu, gu_full).astype(BF))
    d_middle = out_grad[0].astype(F32) + factor_m * (
        d_n2 - normed_m * jnp.mean(d_n2 * normed_m, axis=1, keepdims=True)
    )
    mean_o = jnp.mean(d_middle * attn_out, axis=1, keepdims=True)
    d_attn = gather_seq((factor_o * d_middle).astype(BF))
    beta = gather_seq(factor_o * factor_o * mean_o)
    grad_out = tn(mixed, d_attn).astype(BF)
    d_mixed = (nt(d_attn, out_own) - beta * mixed.astype(F32)).astype(BF)
    d_qfi, gap_grad = mixer_backward(cut, live, qfi, gap_own, kept, d_mixed)
    grad_qfi = tn(n1, d_qfi).astype(BF)
    d_n1 = scatter_seq(nt(d_qfi, qfi_full).astype(BF))
    hidden_grad = d_middle + factor_x * (d_n1 - normed_x * jnp.mean(d_n1 * normed_x, axis=1, keepdims=True))

    g_down = scatter_dp(grad_down).astype(F32)
    gu_rows = swap_seq(scatter_dp(grad_gu)).reshape(ranks, rows, 2 * units).astype(F32)
    gate_rows, up_rows = from_units(gu_rows[:, :, :units]), from_units(gu_rows[:, :, units:])
    out_back = grad_out.reshape(per_rank, span, rows, model).transpose(1, 0, 2, 3)
    out_back = swap_group(out_back).reshape(planes * rows, model)
    out_rows = scatter_dp(out_back).astype(F32)
    gap_back = swap_group(gap_grad.reshape(per_rank, span, rows).transpose(1, 0, 2)).reshape(planes * rows)
    g_gap = scatter_dp(gap_back)
    qfi_rows = swap_seq(scatter_dp(grad_qfi)).reshape(ranks, rows, 3 * channels).astype(F32)
    q_rows, f_rows, i_rows = (from_heads(qfi_rows[:, :, j * channels : (j + 1) * channels]) for j in range(3))

    def rowdot(w, g):
        return jnp.sum(w.astype(F32) * g, axis=1)

    g_attn_gain = rowdot(w_query, q_rows) + rowdot(w_forget, f_rows) + rowdot(w_input, i_rows)
    g_ffn_gain = rowdot(w_gate, gate_rows) + rowdot(w_up, up_rows)
    g_out_gain = rowdot(w_output, out_rows)
    return (
        block_out[None].astype(BF),
        hidden_grad[None].astype(BF),
        g_attn_gain,
        g_gap,
        g_out_gain,
        gain_a * q_rows,
        gain_a * f_rows,
        gain_a * i_rows,
        gain_o * out_rows,
        g_ffn_gain,
        gain_f * gate_rows,
        gain_f * up_rows,
        g_down,
    )


def solution(mesh):
    tok, row, both = P("dp", "seq", None), P("dp", "seq"), P(("dp", "seq"))
    mat = P(("dp", "seq"), None)
    return jax.shard_map(
        on_device,
        mesh=mesh,
        in_specs=(tok, row, row, both, both, both, mat, mat, mat, mat, both, mat, mat, mat, tok),
        out_specs=(tok, tok, both, both, both, mat, mat, mat, mat, both, mat, mat, mat),
        check_vma=False,
    )
```

time: 3310 us -> 1270 us (0.38)
  waiting for transfers between devices: 2470 us -> 803 us
  matrix products: 364 us -> 177 us
  other arithmetic: 157 us -> 43.9 us
  local copies, waits for them, and re-layouts: 128 us -> 43.8 us
  Pallas kernels: 0 us -> 51.8 us
  loops' own time: 33.4 us -> 0 us
    reduce_scatter x7 -> x9, waiting for transfers between devices: 1860 us -> 429 us  [the longest x4 293 us: scatter_seq(): lax.psum_scatter(v, 'seq', scatter_dimension=0, tiled=True).astype(F32)]
    all_gather x9 -> x8, waiting for transfers between devices: 598 us -> 372 us  [the longest x4 194 us: gather_seq(): return lax.all_gather(v, 'seq', axis=0, tiled=True)]
    dot_general x89 -> x12, matrix products: 364 us -> 177 us  [dot(): return lax.dot_general(a, b, (dims, ((), ())), preferred_element_type=F32)]
    all_to_all x0 -> x5, blocking collectives: none -> 56.8 us  [the longest x2 42.1 us: swap_seq(): return lax.all_to_all(v, 'seq', split_axis=0, concat_axis=0, tiled=True)]
    unnamed x3, blocking collectives: 98.7 us -> 47 us
    pallas_call x0 -> x2, Pallas kernels: none -> 51.8 us  [the longest x1 29 us: mixer_backward(): pl.pallas_call(functools.partial(mixer_backward_kernel, heads), grid_spec...]
    another operation x15 -> x0, other arithmetic: 44.9 us -> none  [block_step(): prefix_accumulations = jnp.cumsum(log_keep, axis=0)]
    dynamic_slice x53 -> x0, local copies, waits for them, and re-layouts: 34.6 us -> none  [the longest x45 29.9 us: mixer_local(): lax.scan(jax.checkpoint(block_step), initial, (to_blocks(probe_vectors),...]
  transfers between devices with their start and end apart: 16 -> 20, of which waited for: 14 -> 14; matrix products, arithmetic and copies ran while one was open for 14% -> 15% of each run, Pallas kernels for 0% -> 2%
where the time goes in v1:
time: 1270 us; the launch traced here: 1260 us
  waiting for transfers between devices  803 us (63%)
  matrix products  177 us (14%)
  blocking collectives  112 us (9%)
  Pallas kernels  51.8 us (4%)
  other arithmetic  43.9 us (3%)
  local copies, waits for them, and re-layouts  43.8 us (3%)
  between operations  16.7 us (1%)
  starting transfers between devices  13 us (1%)
    reduce_scatter x4, waiting for transfers between devices, scatter_seq(): lax.psum_scatter(v, 'seq', scatter_dimension=0, tiled=True).astype(F32)  293 us
    all_gather x4, waiting for transfers between devices, gather_seq(): return lax.all_gather(v, 'seq', axis=0, tiled=True)  194 us
    all_gather x3, waiting for transfers between devices, gather_dp(): return lax.all_gather(v, 'dp', axis=0, tiled=True)  178 us
    dot_general x12, matrix products, dot(): return lax.dot_general(a, b, (dims, ((), ())), preferred_element_type=F32)  177 us
    reduce_scatter x4, waiting for transfers between devices, scatter_dp(): return lax.psum_scatter(v, 'dp', scatter_dimension=0, tiled=True)  137 us
    unnamed x3, blocking collectives  47 us
    all_to_all x2, blocking collectives, swap_seq(): return lax.all_to_all(v, 'seq', split_axis=0, concat_axis=0, tiled=True)  42.1 us
    pallas_call x1, Pallas kernels, mixer_backward(): pl.pallas_call(functools.partial(mixer_backward_kernel, heads), grid_spec...  29 us
  transfers between devices with their start and end apart: 20, of which 14 were waited for; matrix products, arithmetic and copies ran while one was open for 15% of the time, Pallas kernels for 2%

profile of v1, /device:TPU:0, one launch (start us, length us, event | category | flops | bytes accessed | tf_op | source)
XLA Modules:
  0.0 1261.0 jit_solution(7895320015876947845)
XLA Ops:
  13.5 17.6 %all_to_all.48 = bf16[8,64,768]{2,1,0:T(8,128)(2,1)} all-to-all(bf16[8,64,768]{2,1,0:T(8,128)(2,1)S(1)} %pad_maximum_fusion.4), channel_id=1, replica_groups=mesh['dp'=4,'seq'=8] {'seq'}, dimensions={0} | all-to-all | bytes 1572864 | tf_op jit(solution)/shard_map/all_to_all | solution.py:263
  68.3 37.2 %all-gather.16.cloned.1.call-done = bf16[2048,768]{1,0:T(8,128)(2,1)} async-done(((bf16[512,768]{1,0:T(8,128)(2,1)}), bf16[2048,768]{1,0:T(8,128)(2,1)}) %all-gather.16.cloned.1.call-update) | async-done | bytes 3145744 | tf_op jit(solution)/shard_map/all_gather | solution.py:255
  105.6 64.4 %all-gather.14.cloned.1.call-done = bf16[2560,2048]{1,0:T(8,128)(2,1)} async-done(((bf16[320,2048]{1,0:T(8,128)(2,1)}), bf16[2560,2048]{1,0:T(8,128)(2,1)}) %all-gather.14.cloned.1.call-update) | async-done | bytes 10485776 | tf_op jit(solution)/shard_map/all_gather | solution.py:247
  170.0 14.0 %fusion.42.qfi_ref = f32[2560,768]{1,0:T(8,128)} fusion(bf16[2560,2048]{1,0:T(8,128)(2,1)} %all-gather.14.cloned.1.call-done, bf16[2048,768]{1,0:T(8,128)(2,1)} %all-gather.16.cloned.1.call-done), kind=kOutput, calls=%fused_computation.110 | convolution fusion | flops 8053063680 | bytes 21495808 | tf_op jit(solution)/shard_map/dot_general | solution.py:19
  184.0 22.8 %mixer_forward.1 = (bf16[2560,256]{1,0:T(8,128)(2,1)}, f32[2560,1]{1,0:T(8,128)}, bf16[40,2,128,128]{3,2,1,0:T(8,128)(2,1)}) custom-call(s32[40]{0:T(128)} %convert_reduce_fusion.cut_ref, s32[1]{0:T(128)} %bitcast.4.live_ref, f32[2560,768]{1,0:T(8,128)} %fusion.42.qfi_ref, f32[1,256]{1,0:T(1,128)} %reshape.213.gap_ref), custom_call_target="tpu_custom_call" | custom-call | flops 838860800 | bytes 13107200 | tf_op jit(solution)/shard_map/mixer_forward/pallas_call | solution.py:186
  227.5 24.5 %all_to_all.50 = bf16[8,64,1408]{2,1,0:T(8,128)(2,1)} all-to-all(bf16[8,64,1408]{2,1,0:T(8,128)(2,1)S(1)} %pad_maximum_fusion.3), channel_id=1, replica_groups=mesh['dp'=4,'seq'=8] {'seq'}, dimensions={0} | all-to-all | bytes 2883584 | tf_op jit(solution)/shard_map/all_to_all | solution.py:263
  253.1 79.8 %reduce-scatter.12.cloned.1.call-done = bf16[320,2048]{1,0:T(8,128)(2,1)} async-done(((bf16[2560,2048]{1,0:T(8,128)(2,1)}), bf16[320,2048]{1,0:T(8,128)(2,1)}) %reduce-scatter.12.cloned.1.call-update) | async-done | bytes 1310736 | tf_op jit(solution)/shard_map/reduce_scatter | solution.py:251
  338.7 102.4 %all-gather.20.cloned.1.call-done = bf16[2048,1408]{1,0:T(8,128)(2,1)} async-done(((bf16[512,1408]{1,0:T(8,128)(2,1)}), bf16[2048,1408]{1,0:T(8,128)(2,1)}) %all-gather.20.cloned.1.call-update) | async-done | bytes 5767184 | tf_op jit(solution)/shard_map/all_gather | solution.py:255
  441.1 64.0 %all-gather.18.cloned.1.call-done = bf16[2560,2048]{1,0:T(8,128)(2,1)} async-done(((bf16[320,2048]{1,0:T(8,128)(2,1)}), bf16[2560,2048]{1,0:T(8,128)(2,1)}) %all-gather.18.cloned.1.call-update) | async-done | bytes 10485776 | tf_op jit(solution)/shard_map/all_gather | solution.py:247
  505.1 22.6 %fusion.43 = f32[2560,1408]{0,1:T(8,128)} fusion(bf16[2560,2048]{1,0:T(8,128)(2,1)} %all-gather.18.cloned.1.call-done, bf16[2048,1408]{1,0:T(8,128)(2,1)} %all-gather.20.cloned.1.call-done), kind=kOutput, calls=%fused_computation.111 | convolution fusion | flops 14763950080 | bytes 30670848 | tf_op jit(solution)/shard_map/dot_general | solution.py:19
  527.7 38.2 %all-gather.22.cloned.1.call-done = bf16[704,2048]{1,0:T(8,128)(2,1)} async-done(((bf16[176,2048]{1,0:T(8,128)(2,1)}), bf16[704,2048]{1,0:T(8,128)(2,1)}) %all-gather.22.cloned.1.call-update) | async-done | bytes 2883600 | tf_op jit(solution)/shard_map/all_gather | solution.py:255
  565.9 63.9 %all-gather.28.cloned.1.call-done = bf16[1,2560,2048]{2,1,0:T(8,128)(2,1)} async-done(((bf16[1,320,2048]{2,1,0:T(8,128)(2,1)}), bf16[1,2560,2048]{2,1,0:T(8,128)(2,1)}) %all-gather.28.cloned.1.call-update) | async-done | bytes 10485776 | tf_op jit(solution)/shard_map/all_gather | solution.py:247
  629.8 19.1 %multiply_convert_fusion.1 = (bf16[2560,704]{0,1:T(8,128)(2,1)}, bf16[2560,704]{0,1:T(8,128)(2,1)}, bf16[2560,704]{0,1:T(8,128)(2,1)}) fusion(f32[2560,1408]{0,1:T(8,128)} %fusion.43, bf16[704,2048]{1,0:T(8,128)(2,1)} %all-gather.22.cloned.1.call-done, bf16[1,2560,2048]{2,1,0:T(8,128)(2,1)} %all-gather.28.cloned.1.call-done), kind=kOutput, calls=%fused_computation.11 | convolution fusion | flops 7409008640 | bytes 38600704 | tf_op jit(solution)/shard_map/dot_general | solution.py:19
  648.9 23.0 %convolution_convert_fusion.1 = bf16[2560,2048]{1,0:T(8,128)(2,1)} fusion(bf16[2048,1408]{1,0:T(8,128)(2,1)} %all-gather.20.cloned.1.call-done, bf16[2560,704]{0,1:T(8,128)(2,1)} %get-tuple-element.28, bf16[2560,704]{0,1:T(8,128)(2,1)} %get-tuple-element.27), kind=kOutput, calls=%fused_computation.1 | convolution fusion | flops 14783610880 | bytes 23461888 | tf_op jit(solution)/shard_map/dot_general | solution.py:19
  672.0 14.1 %convolution_convert_fusion.2 = bf16[2560,2048]{1,0:T(8,128)(2,1)} fusion(bf16[2560,704]{0,1:T(8,128)(2,1)} %get-tuple-element.29, bf16[704,2048]{1,0:T(8,128)(2,1)} %all-gather.22.cloned.1.call-done), kind=kOutput, calls=%fused_computation.2 | convolution fusion | flops 7387217920 | bytes 16973824 | tf_op jit(solution)/shard_map/dot_general | solution.py:19
  686.3 67.3 %reduce-scatter.16.cloned.1.call-done = bf16[320,2048]{1,0:T(8,128)(2,1)} async-done(((bf16[2560,2048]{1,0:T(8,128)(2,1)}), bf16[320,2048]{1,0:T(8,128)(2,1)}) %reduce-scatter.16.cloned.1.call-update) | async-done | bytes 1310736 | tf_op jit(solution)/shard_map/reduce_scatter | solution.py:251
  755.8 82.9 %reduce-scatter.14.cloned.1.call-done = bf16[320,2048]{1,0:T(8,128)(2,1)} async-done(((bf16[2560,2048]{1,0:T(8,128)(2,1)}), bf16[320,2048]{1,0:T(8,128)(2,1)}) %reduce-scatter.14.cloned.1.call-update) | async-done | bytes 1310736 | tf_op jit(solution)/shard_map/reduce_scatter | solution.py:251
  846.3 22.1 %convolution_convert_fusion.4 = bf16[2048,1408]{1,0:T(8,128)(2,1)} fusion(bf16[2560,2048]{1,0:T(8,128)(2,1)} %all-gather.18.cloned.1.call-done, bf16[2560,704]{0,1:T(8,128)(2,1)} %get-tuple-element.28, bf16[2560,704]{0,1:T(8,128)(2,1)} %get-tuple-element.27), kind=kOutput, calls=%fused_computation.8 | convolution fusion | flops 14781251584 | bytes 23461888 | tf_op jit(solution)/shard_map/dot_general | solution.py:19
  883.5 24.4 %all-reduce.1 = f32[2560]{0:T(1024)S(1)} all-reduce(f32[2560]{0:T(1024)S(1)} %dynamic-update-slice.1), channel_id=1, replica_groups=mesh['dp'=4,'seq'=8] {'seq'}, use_global_device_ids=true, to_apply=%add.1 | all-reduce | flops 2560 | bytes 20480
  918.4 29.0 %mixer_backward.1 = (bf16[2560,768]{1,0:T(8,128)(2,1)}, f32[1,256]{1,0:T(1,128)}) custom-call(s32[40]{0:T(128)} %convert_reduce_fusion.cut_ref, s32[1]{0:T(128)} %bitcast.4.live_ref, f32[2560,768]{1,0:T(8,128)} %fusion.42.qfi_ref, f32[1,256]{1,0:T(1,128)} %reshape.213.gap_ref, bf16[40,2,128,128]{3,2,1,0:T(8,128)(2,1)} %get-tuple-element.20.kept_ref, ...), custom_call_target="tpu_custom_call" | custom-call | flops 2013265920 | bytes 18350080 | tf_op jit(solution)/shard_map/mixer_backward/pallas_call | solution.py:218
  987.3 27.3 %reduce-scatter.24.cloned.1.call-done = bf16[512,1408]{1,0:T(8,128)(2,1)} async-done(((bf16[2048,1408]{1,0:T(8,128)(2,1)}), bf16[512,1408]{1,0:T(8,128)(2,1)}) %reduce-scatter.24.cloned.1.call-update) | async-done | bytes 1441808 | tf_op jit(solution)/shard_map/reduce_scatter | solution.py:259
  1018.8 54.6 %reduce-scatter.26.cloned.1.call-done = bf16[176,2048]{1,0:T(8,128)(2,1)} async-done(((bf16[704,2048]{1,0:T(8,128)(2,1)}), bf16[176,2048]{1,0:T(8,128)(2,1)}) %reduce-scatter.26.cloned.1.call-update) | async-done | bytes 720912 | tf_op jit(solution)/shard_map/reduce_scatter | solution.py:259
  1080.8 54.9 %reduce-scatter.20.cloned.1.call-done = bf16[512,768]{1,0:T(8,128)(2,1)} async-done(((bf16[2048,768]{1,0:T(8,128)(2,1)}), bf16[512,768]{1,0:T(8,128)(2,1)}) %reduce-scatter.20.cloned.1.call-update) | async-done | bytes 786448 | tf_op jit(solution)/shard_map/reduce_scatter | solution.py:259
  1186.6 62.5 %reduce-scatter.18.cloned.1.call-done = bf16[320,2048]{1,0:T(8,128)(2,1)} async-done(((bf16[2560,2048]{1,0:T(8,128)(2,1)}), bf16[320,2048]{1,0:T(8,128)(2,1)}) %reduce-scatter.18.cloned.1.call-update) | async-done | bytes 1310736 | tf_op jit(solution)/shard_map/reduce_scatter | solution.py:251
  (198 shorter events, 211.8 us)
Async XLA Ops:
  7.2 55.4 %all-gather.26.cloned.1.call-start = ((), (), s32[]{:S(2)}) async-start(), calls=%async_computation.32 | async-start | bytes 1310720 | tf_op jit(solution)/shard_map/all_gather | solution.py:330
  9.7 95.9 %all-gather.16.cloned.1.call-start = ((), (), s32[]{:S(2)}) async-start(), calls=%async_computation.18 | async-start | bytes 3932160 | tf_op jit(solution)/shard_map/all_gather | solution.py:255
  31.2 138.8 %all-gather.14.cloned.1.call-start = ((), (), s32[]{:S(2)}) async-start(), calls=%async_computation.17 | async-start | bytes 11796480 | tf_op jit(solution)/shard_map/all_gather | solution.py:247
  47.7 12.8 %all-to-all-start.1 = ((bf16[2,2,64]{2,1,0:T(2,128)(2,1)}), bf16[2,2,64]{2,1,0:T(2,128)(2,1)S(1)}, u32[]{:S(2)}, u32[]{:S(2)}) async-start(bf16[2,2,64]{2,1,0:T(2,128)(2,1)} %reshape.190), calls=%async_computation.1 | async-start | bytes 2048 | tf_op jit(solution)/shard_map/all_to_all | solution.py:319
  50.9 201.1 %reduce-scatter.10.cloned.1.call-start = ((), (), s32[]{:S(2)}) async-start(), calls=%async_computation.19 | async-start | bytes 1474560 | tf_op jit(solution)/shard_map/reduce_scatter | solution.py:349
  68.3 138.5 %copy-start.6 = (bf16[2,2,64,2048]{3,2,1,0:T(8,128)(2,1)}, bf16[2,2,64,2048]{3,2,1,0:T(8,128)(2,1)S(1)}, u32[]{:S(2)}) copy-start(bf16[2,2,64,2048]{3,2,1,0:T(8,128)(2,1)S(1)} %copy.88) | copy-start | bytes 3145732
  206.7 126.2 %reduce-scatter.12.cloned.1.call-start = ((), (), s32[]{:S(2)}) async-start(), calls=%async_computation.20 | async-start | bytes 11796480 | tf_op jit(solution)/shard_map/reduce_scatter | solution.py:251
  213.8 227.3 %all-gather.20.cloned.1.call-start = ((), (), s32[]{:S(2)}) async-start(), calls=%async_computation.22 | async-start | bytes 7208960 | tf_op jit(solution)/shard_map/all_gather | solution.py:255
  252.0 253.2 %all-gather.18.cloned.1.call-start = ((), (), s32[]{:S(2)}) async-start(), calls=%async_computation.21 | async-start | bytes 11796480 | tf_op jit(solution)/shard_map/all_gather | solution.py:247
  336.7 229.3 %all-gather.22.cloned.1.call-start = ((), (), s32[]{:S(2)}) async-start(), calls=%async_computation.23 | async-start | bytes 3604480 | tf_op jit(solution)/shard_map/all_gather | solution.py:255
  337.4 292.4 %all-gather.28.cloned.1.call-start = ((), (), s32[]{:S(2)}) async-start(), calls=%async_computation.33 | async-start | bytes 11796480 | tf_op jit(solution)/shard_map/all_gather | solution.py:247
  338.1 415.5 %reduce-scatter.16.cloned.1.call-start = ((), (), s32[]{:S(2)}) async-start(), calls=%async_computation.25 | async-start | bytes 11796480 | tf_op jit(solution)/shard_map/reduce_scatter | solution.py:251
  671.9 166.8 %reduce-scatter.14.cloned.1.call-start = ((), (), s32[]{:S(2)}) async-start(), calls=%async_computation.24 | async-start | bytes 11796480 | tf_op jit(solution)/shard_map/reduce_scatter | solution.py:251
  686.1 223.9 %all-gather.24.cloned.1.call-start = ((), (), s32[]{:S(2)}) async-start(), calls=%async_computation.26 | async-start | bytes 11796480 | tf_op jit(solution)/shard_map/all_gather | solution.py:247
  846.3 168.3 %reduce-scatter.24.cloned.1.call-start = ((), (), s32[]{:S(2)}) async-start(), calls=%async_computation.30 | async-start | bytes 7208960 | tf_op jit(solution)/shard_map/reduce_scatter | solution.py:259
  868.4 204.9 %reduce-scatter.26.cloned.1.call-start = ((), (), s32[]{:S(2)}) async-start(), calls=%async_computation.31 | async-start | bytes 3604480 | tf_op jit(solution)/shard_map/reduce_scatter | solution.py:259
  881.1 28.9 %copy-start.4 = (bf16[2560,256]{1,0:T(8,128)(2,1)S(1)}, bf16[2560,256]{1,0:T(8,128)(2,1)}, u32[]{:S(2)}) copy-start(bf16[2560,256]{1,0:T(8,128)(2,1)} %get-tuple-element.19) | copy-start | bytes 3932164
  881.1 254.6 %reduce-scatter.20.cloned.1.call-start = ((), (), s32[]{:S(2)}) async-start(), calls=%async_computation.28 | async-start | bytes 3932160 | tf_op jit(solution)/shard_map/reduce_scatter | solution.py:259
  961.0 215.8 %reduce-scatter.22.cloned.1.call-start = ((), (), s32[]{:S(2)}) async-start(), calls=%async_computation.29 | async-start | bytes 1310720 | tf_op jit(solution)/shard_map/reduce_scatter | solution.py:259
  973.4 275.7 %reduce-scatter.18.cloned.1.call-start = ((), (), s32[]{:S(2)}) async-start(), calls=%async_computation.27 | async-start | bytes 11796480 | tf_op jit(solution)/shard_map/reduce_scatter | solution.py:251
  987.3 89.0 %copy-start.21 = (f32[1,256]{1,0:T(1,128)S(1)}, f32[1,256]{1,0:T(1,128)}, u32[]{:S(2)}) copy-start(f32[1,256]{1,0:T(1,128)} %get-tuple-element.22) | copy-start | bytes 3076
  1014.5 62.6 %all-to-all-start.7 = ((bf16[8,64,1408]{2,1,0:T(8,128)(2,1)}), bf16[8,64,1408]{2,1,0:T(8,128)(2,1)S(1)}, u32[]{:S(2)}, u32[]{:S(2)}) async-start(bf16[8,64,1408]{2,1,0:T(8,128)(2,1)} %bitcast.123), calls=%async_computation.15 | async-start | bytes 2883584 | tf_op jit(solution)/shard_map/all_to_all | solution.py:263
  1135.7 43.8 %all-to-all-start.4 = ((bf16[8,64,768]{2,1,0:T(8,128)(2,1)}), bf16[8,64,768]{2,1,0:T(8,128)(2,1)}, u32[]{:S(2)}, u32[]{:S(2)}) async-start(bf16[8,64,768]{2,1,0:T(8,128)(2,1)} %bitcast.128), calls=%async_computation.10 | async-start | bytes 1572864 | tf_op jit(solution)/shard_map/all_to_all | solution.py:263
  1183.2 65.8 %copy-start.11 = (f32[320]{0:T(512)S(1)}, f32[320]{0:T(512)}, u32[]{:S(2)}) copy-start(f32[320]{0:T(512)} %copy-done.10) | copy-start | bytes 3844
  (21 other events, 110.8 us)
Sparse Core Ops, SparseCore 0:
  10.2 30.7 all-gather.25
  42.5 63.0 all-gather.15
  108.1 61.8 all-gather.13
  206.9 41.1 reduce-scatter.9
  251.4 81.5 reduce-scatter.11
  334.4 106.6 all-gather.19
  443.6 61.5 all-gather.17
  506.7 59.1 all-gather.21
  567.8 61.9 all-gather.27
  672.1 81.5 reduce-scatter.15
  757.2 81.5 reduce-scatter.13
  846.4 63.5 all-gather.23
  912.3 102.1 reduce-scatter.23
  1016.7 56.6 reduce-scatter.25
  1075.5 60.0 reduce-scatter.19
  1137.8 27.1 reduce-scatter.21
  1168.8 80.2 reduce-scatter.17

commit v2 on v1

--- a/solution.py
+++ b/solution.py
@@ -11,6 +11,7 @@
 BLOCK = 64
 UNROLL = 2
 EPSILON = 1e-06
+EXTRA = 128
 BF = jnp.bfloat16
 F32 = jnp.float32
 
@@ -66,7 +67,7 @@
     return allowed, inherits, tail, whole
 
 
-def mixer_forward_kernel(heads, cut_ref, live_ref, qfi_ref, gap_ref, mixed_ref, square_ref, kept_ref, state):
+def mixer_forward_kernel(heads, cut_ref, live_ref, qfi_ref, gap_ref, mixed_ref, kept_ref, state):
     step = pl.program_id(0)
     width = heads * 128
 
@@ -105,7 +106,9 @@
             square = square + jnp.sum(mixed * mixed, axis=1, keepdims=True)
             mixed_ref[rows, cols] = mixed.astype(BF)
             state[h] = before * e_all[:, cols] + tn(value_tail[:, cols], scaled_k[:, cols]) * e_rest[:, cols]
-        square_ref[rows, :] = square
+        lane = lax.broadcasted_iota(jnp.int32, (BLOCK, EXTRA), 1)
+        high = square.astype(BF).astype(F32)
+        mixed_ref[rows, width:] = jnp.where(lane == 0, high, jnp.where(lane == 1, square - high, 0.0)).astype(BF)
 
 
 def mixer_backward_kernel(heads, cut_ref, live_ref, qfi_ref, gap_ref, kept_ref, grad_ref, out_ref, gap_out_ref, state):
@@ -193,15 +196,13 @@
                 pl.BlockSpec((1, width), lambda i, *_: (0, 0)),
             ],
             out_specs=[
-                pl.BlockSpec((span, width), lambda i, *_: (i, 0)),
-                pl.BlockSpec((span, 1), lambda i, *_: (i, 0)),
+                pl.BlockSpec((span, width + EXTRA), lambda i, *_: (i, 0)),
                 pl.BlockSpec((UNROLL, heads, 128, 128), lambda i, *_: (i, 0, 0, 0)),
             ],
             scratch_shapes=[pltpu.VMEM((heads, 128, 128), F32)],
         ),
         out_shape=[
-            jax.ShapeDtypeStruct((tokens, width), BF),
-            jax.ShapeDtypeStruct((tokens, 1), F32),
+            jax.ShapeDtypeStruct((tokens, width + EXTRA), BF),
             jax.ShapeDtypeStruct((tokens // BLOCK, heads, 128, 128), BF),
         ],
         cost_estimate=pl.CostEstimate(
@@ -243,12 +244,411 @@
     )(cut, live, qfi, gap, kept, grad)
 
 
-def gather_seq(v):
-    return lax.all_gather(v, "seq", axis=0, tiled=True)
-
-
-def scatter_seq(v):
-    return lax.psum_scatter(v, "seq", scatter_dimension=0, tiled=True).astype(F32)
+MESH = pl.DeviceIdType.MESH
+PIECES = 5
+VMEM_LIMIT = 60 * 1024 * 1024
+(S_X, S_Y, S_CORE, S_DIAG_Y, S_DIAG_X, S_CORE_X, S_CORE_Y, S_CORE_D, R_CORE, R_X, R_Y, R_LAST_Y, R_LAST_X, KINDS) = range(14)
+
+
+class Place:
+    def __init__(self):
+        self.plane = lax.axis_index("dp")
+        me = lax.axis_index("seq")
+        self.me = me
+        self.core = me % 2
+        self.x = (me // 2) % 2
+        self.y = me // 4
+
+    def rank(self, fy=0, fx=0, fc=0):
+        y = 1 - self.y if fy else self.y
+        x = 1 - self.x if fx else self.x
+        core = 1 - self.core if fc else self.core
+        return 4 * y + 2 * x + core
+
+    def device(self, fy=0, fx=0, fc=0):
+        return (self.plane, self.rank(fy, fx, fc))
+
+
+def greet(place):
+    barrier = pltpu.get_barrier_semaphore()
+    for flip in ((0, 0, 1), (0, 1, 0), (1, 0, 0)):
+        pl.semaphore_signal(barrier, inc=1, device_id=place.device(*flip), device_id_type=MESH)
+    pl.semaphore_wait(barrier, 3)
+
+
+def remote(src, dst, sems, kind, b, device):
+    send, recv = sems
+    return pltpu.make_async_remote_copy(
+        src_ref=src,
+        dst_ref=dst,
+        send_sem=send.at[kind, b],
+        recv_sem=recv.at[kind, b],
+        device_id=device,
+        device_id_type=MESH,
+    )
+
+
+class Gather:
+    def __init__(self, place, own, full, sems, local_sem):
+        self.p, self.own, self.full, self.sems, self.local = place, own, full, sems, local_sem
+        self.half = full.shape[2] // 2
+
+    def keep(self, b):
+        return pltpu.make_async_copy(self.own.at[b], self.full.at[self.p.me, b], self.local.at[b])
+
+    def first(self, b):
+        p, dst = self.p, self.full.at[self.p.me, b]
+        return [
+            remote(self.own.at[b], dst, self.sems, S_X, b, p.device(0, 1, 0)),
+            remote(self.own.at[b], dst, self.sems, S_Y, b, p.device(1, 0, 0)),
+            remote(self.own.at[b], dst, self.sems, S_CORE, b, p.device(0, 0, 1)),
+        ]
+
+    def second(self, b):
+        p, h = self.p, self.half
+        from_x, from_y = self.full.at[p.rank(0, 1, 0), b], self.full.at[p.rank(1, 0, 0), b]
+        up, down = from_x.at[pl.ds(0, h)], from_y.at[pl.ds(h, h)]
+        return [
+            remote(up, up, self.sems, S_DIAG_Y, b, p.device(1, 0, 0)),
+            remote(down, down, self.sems, S_DIAG_X, b, p.device(0, 1, 0)),
+            remote(from_x, from_x, self.sems, S_CORE_X, b, p.device(0, 0, 1)),
+            remote(from_y, from_y, self.sems, S_CORE_Y, b, p.device(0, 0, 1)),
+        ]
+
+    def third(self, b):
+        p = self.p
+        block = self.full.at[p.rank(1, 1, 0), b]
+        return [remote(block, block, self.sems, S_CORE_D, b, p.device(0, 0, 1))]
+
+    def arrived(self, kind, b, flips, rows=None):
+        block = self.full.at[self.p.rank(*flips), b]
+        if rows is not None:
+            block = block.at[pl.ds(rows * self.half, self.half)]
+        remote(block, block, self.sems, kind, b, self.p.device(0, 0, 1)).wait_recv()
+
+    def start(self, b):
+        self.keep(b).start()
+        for copy in self.first(b):
+            copy.start()
+
+    def forward(self, b):
+        self.arrived(S_X, b, (0, 1, 0))
+        self.arrived(S_Y, b, (1, 0, 0))
+        for copy in self.second(b):
+            copy.start()
+
+    def forward_last(self, b):
+        self.arrived(S_DIAG_Y, b, (1, 1, 0), 0)
+        self.arrived(S_DIAG_X, b, (1, 1, 0), 1)
+        for copy in self.third(b):
+            copy.start()
+
+    def finish(self, b):
+        self.arrived(S_CORE, b, (0, 0, 1))
+        self.arrived(S_CORE_X, b, (0, 1, 1))
+        self.arrived(S_CORE_Y, b, (1, 0, 1))
+        self.arrived(S_CORE_D, b, (1, 1, 1))
+
+    def drain(self, b):
+        self.keep(b).wait()
+        for copy in self.first(b) + self.second(b) + self.third(b):
+            copy.wait_send()
+
+
+def swap_starts(place, parts, outs, send, recv, local):
+    copies = []
+    for i, (part, out) in enumerate(zip(parts, outs)):
+        own = pltpu.make_async_copy(part.at[place.me], out.at[place.me], local.at[i])
+        own.start()
+        for k, flips in enumerate(((0, 0, 1), (0, 1, 0), (1, 0, 0), (0, 1, 1), (1, 0, 1), (1, 1, 0), (1, 1, 1))):
+            copy = pltpu.make_async_remote_copy(
+                src_ref=part.at[place.rank(*flips)],
+                dst_ref=out.at[place.me],
+                send_sem=send.at[i, k],
+                recv_sem=recv.at[i, k],
+                device_id=place.device(*flips),
+                device_id_type=MESH,
+            )
+            copy.start()
+            there = out.at[place.rank(*flips)]
+            copies.append((copy, pltpu.make_async_remote_copy(
+                src_ref=there, dst_ref=there, send_sem=send.at[i, k], recv_sem=recv.at[i, k],
+                device_id=place.device(*flips), device_id_type=MESH)))
+        copies.append((own, None))
+    return copies
+
+
+def swap_waits(copies):
+    for copy, arrival in copies:
+        if arrival is None:
+            copy.wait()
+        else:
+            copy.wait_send()
+            arrival.wait_recv()
+
+
+def greet_all(place):
+    barrier = pltpu.get_barrier_semaphore()
+    for flips in ((0, 0, 1), (0, 1, 0), (1, 0, 0), (0, 1, 1), (1, 0, 1), (1, 1, 0), (1, 1, 1)):
+        pl.semaphore_signal(barrier, inc=1, device_id=place.device(*flips), device_id_type=MESH)
+    pl.semaphore_wait(barrier, 7)
+
+
+def swap_plane(parts, collective_id):
+    count = len(parts)
+
+    def kernel(*refs):
+        ins, outs, (send, recv, local) = refs[:count], refs[count : 2 * count], refs[2 * count :]
+        place = Place()
+        greet_all(place)
+        swap_waits(swap_starts(place, ins, outs, send, recv, local))
+
+    any_spec = pl.BlockSpec(memory_space=pl.ANY)
+    return pl.pallas_call(
+        kernel,
+        in_specs=[any_spec] * count,
+        out_specs=[any_spec] * count,
+        out_shape=[jax.ShapeDtypeStruct(p.shape, p.dtype) for p in parts],
+        scratch_shapes=[
+            pltpu.SemaphoreType.DMA((count, 7)),
+            pltpu.SemaphoreType.DMA((count, 7)),
+            pltpu.SemaphoreType.DMA((count,)),
+        ],
+        compiler_params=pltpu.CompilerParams(collective_id=collective_id, has_side_effects=True),
+        name="swap_plane",
+    )(*parts)
+
+
+def gather_plane(own, parts, collective_id):
+    tokens, width = own.shape
+    rows = tokens // PIECES
+    own = own.reshape(PIECES, rows, width)
+    count = len(parts)
+
+    def kernel(own_ref, *refs):
+        ins, full, outs = refs[:count], refs[count], refs[count + 1 : 2 * count + 1]
+        send, recv, local, swap_send, swap_recv, swap_local = refs[2 * count + 1 :]
+        place = Place()
+        greet_all(place)
+        gather = Gather(place, own_ref, full, (send, recv), local)
+        for b in range(PIECES):
+            gather.start(b)
+        for b in range(PIECES):
+            gather.forward(b)
+        copies = swap_starts(place, ins, outs, swap_send, swap_recv, swap_local)
+        for b in range(PIECES):
+            gather.forward_last(b)
+        for b in range(PIECES):
+            gather.finish(b)
+        swap_waits(copies)
+        for b in range(PIECES):
+            gather.drain(b)
+
+    any_spec = pl.BlockSpec(memory_space=pl.ANY)
+    results = pl.pallas_call(
+        kernel,
+        in_specs=[any_spec] * (1 + count),
+        out_specs=[any_spec] * (1 + count),
+        out_shape=[jax.ShapeDtypeStruct((8, PIECES, rows, width), own.dtype)]
+        + [jax.ShapeDtypeStruct(p.shape, p.dtype) for p in parts],
+        scratch_shapes=[
+            pltpu.SemaphoreType.DMA((KINDS, PIECES)),
+            pltpu.SemaphoreType.DMA((KINDS, PIECES)),
+            pltpu.SemaphoreType.DMA((PIECES,)),
+            pltpu.SemaphoreType.DMA((max(count, 1), 7)),
+            pltpu.SemaphoreType.DMA((max(count, 1), 7)),
+            pltpu.SemaphoreType.DMA((max(count, 1),)),
+        ],
+        compiler_params=pltpu.CompilerParams(collective_id=collective_id, has_side_effects=True),
+        name="gather_plane",
+    )(own, *parts)
+    return results[0].reshape(8 * tokens, width), results[1:]
+
+
+def product_scatter(left, weight, transposed, stats, epilogue, owned, outs, gathered, collective_id):
+    tokens = left.shape[0] // 8
+    rows = tokens // PIECES
+    depth = weight.shape[1] if transposed else weight.shape[0]
+    width = weight.shape[0] if transposed else weight.shape[1]
+    half = width // 2
+    extra = EXTRA if stats else 0
+    right = half + extra
+    columns = left.shape[1]
+    left = left.reshape(8, PIECES, rows, columns)
+    tile = 256
+
+    def kernel(*refs):
+        refs = list(refs)
+        left_ref, weight_ref = refs.pop(0), refs.pop(0)
+        own_refs = [refs.pop(0) for _ in owned]
+        out_refs = [refs.pop(0) for _ in outs]
+        full_ref = refs.pop(0) if gathered else None
+        (x_buf, w_buf, core_out, core_in, total, x_out, x_in, y_out, y_in, keep_a, keep_b, done_a, done_b, last_y_out, last_y_in,
+         last_x_out, last_x_in, send, recv, load_sem, w_sem) = refs[:21]
+        refs = refs[21:]
+        place = Place()
+        sems = (send, recv)
+
+        def loads(b):
+            copies = []
+            for j in range(4):
+                copies.append(pltpu.make_async_copy(left_ref.at[2 * j + 1 - place.core, b], x_buf.at[b, j], load_sem.at[b]))
+                copies.append(pltpu.make_async_copy(left_ref.at[2 * j + place.core, b], x_buf.at[b, 4 + j], load_sem.at[b]))
+            return copies
+
+        w_copy = pltpu.make_async_copy(weight_ref, w_buf, w_sem.at[0])
+        w_copy.start()
+        for b in range(PIECES):
+            for copy in loads(b):
+                copy.start()
+        greet(place)
+        if gathered:
+            n_buf, keep_sem = refs
+            gather = Gather(place, n_buf, full_ref, sems, keep_sem)
+
+        def send_core(b):
+            return remote(core_out.at[b], core_in.at[b], sems, R_CORE, b, place.device(0, 0, 1))
+
+        def send_x(b):
+            return remote(x_out.at[b], x_in.at[b], sems, R_X, b, place.device(0, 1, 0))
+
+        def send_y(b):
+            return remote(y_out.at[b], y_in.at[b], sems, R_Y, b, place.device(1, 0, 0))
+
+        def send_last_y(b):
+            return remote(last_y_out.at[b], last_y_in.at[b], sems, R_LAST_Y, b, place.device(1, 0, 0))
+
+        def send_last_x(b):
+            return remote(last_x_out.at[b], last_x_in.at[b], sems, R_LAST_X, b, place.device(0, 1, 0))
+
+        def produce(b):
+            pltpu.make_async_copy(x_buf.at[b], x_buf.at[b], load_sem.at[b]).wait()
+
+            @pl.loop(0, width // tile)
+            def _(t):
+                at = pl.multiple_of(t * tile, tile)
+                lhs = x_buf[b, :, :, :depth].reshape(8 * rows, depth)
+                if transposed:
+                    out = nt(lhs, w_buf[pl.ds(at, tile), :])
+                else:
+                    out = nn(lhs, w_buf[:, pl.ds(at, tile)])
+                core_out[b, :, :, pl.ds(at, tile)] = out[: 4 * rows].astype(BF).reshape(4, rows, tile)
+                total[:, :, pl.ds(at, tile)] = out[4 * rows :].reshape(4, rows, tile)
+
+            if stats:
+                core_out[b, :, :, width:] = x_buf[b, :4, :, depth:]
+                total[:, :, width:] = x_buf[b, 4:, :, depth:].astype(F32)
+            send_core(b).start()
+
+        def stage_one(b):
+            send_core(b).wait_recv()
+            for i in range(2):
+                go, stay = 2 * i + 1 - place.x, 2 * i + place.x
+                x_out[b, i] = (total[go, :, :half] + core_in[b, go, :, :half].astype(F32)).astype(BF)
+                keep_a[i] = total[stay, :, :half] + core_in[b, stay, :, :half].astype(F32)
+            send_x(b).start()
+            for i in range(2):
+                go, stay = 2 * (1 - place.y) + i, 2 * place.y + i
+                y_out[b, i] = (total[go, :, half:] + core_in[b, go, :, half:].astype(F32)).astype(BF)
+                keep_b[i] = total[stay, :, half:] + core_in[b, stay, :, half:].astype(F32)
+            send_y(b).start()
+
+        def stage_two(b):
+            send_x(b).wait_recv()
+            go, stay = 1 - place.y, place.y
+            last_y_out[b] = (keep_a[go] + x_in[b, go].astype(F32)).astype(BF)
+            send_last_y(b).start()
+            done_a[...] = keep_a[stay] + x_in[b, stay].astype(F32)
+            send_y(b).wait_recv()
+            go, stay = 1 - place.x, place.x
+            last_x_out[b] = (keep_b[go] + y_in[b, go].astype(F32)).astype(BF)
+            send_last_x(b).start()
+            done_b[...] = keep_b[stay] + y_in[b, stay].astype(F32)
+
+        def stage_three(b):
+            send_last_y(b).wait_recv()
+            send_last_x(b).wait_recv()
+            low = done_a[...] + last_y_in[b].astype(F32)
+            high = done_b[...] + last_x_in[b].astype(F32)
+            result = jnp.concatenate([low, high[:, :half]], axis=1)
+            stat = high[:, half:] if stats else None
+            written, sent = epilogue(result, stat, *[r[b] for r in own_refs])
+            for ref, value in zip(out_refs, written):
+                ref[b] = value
+            if gathered:
+                n_buf[b] = sent
+                gather.start(b)
+
+        w_copy.wait()
+
+        def guarded(body, b):
+            @pl.when((b >= 0) & (b < PIECES))
+            def _():
+                body(b)
+
+        @pl.loop(0, PIECES + (6 if gathered else 3))
+        def _(step):
+            guarded(stage_three, step - 3)
+            guarded(stage_two, step - 2)
+            guarded(stage_one, step - 1)
+            guarded(produce, step)
+            if gathered:
+                guarded(gather.forward, step - 4)
+                guarded(gather.forward_last, step - 5)
+
+        @pl.loop(0, PIECES)
+        def _(b):
+            if gathered:
+                gather.finish(b)
+                gather.drain(b)
+            for copy in (send_core, send_x, send_y, send_last_y, send_last_x):
+                copy(b).wait_send()
+
+    any_spec, vmem = pl.BlockSpec(memory_space=pl.ANY), pl.BlockSpec(memory_space=pltpu.VMEM)
+    out_shape = [jax.ShapeDtypeStruct((PIECES, rows, c), d) for c, d in outs]
+    out_specs = [vmem] * len(outs)
+    scratch = [
+        pltpu.VMEM((PIECES, 8, rows, columns), BF),
+        pltpu.VMEM(weight.shape, BF),
+        pltpu.VMEM((PIECES, 4, rows, width + extra), BF),
+        pltpu.VMEM((PIECES, 4, rows, width + extra), BF),
+        pltpu.VMEM((4, rows, width + extra), F32),
+        pltpu.VMEM((PIECES, 2, rows, half), BF),
+        pltpu.VMEM((PIECES, 2, rows, half), BF),
+        pltpu.VMEM((PIECES, 2, rows, right), BF),
+        pltpu.VMEM((PIECES, 2, rows, right), BF),
+        pltpu.VMEM((2, rows, half), F32),
+        pltpu.VMEM((2, rows, right), F32),
+        pltpu.VMEM((rows, half), F32),
+        pltpu.VMEM((rows, right), F32),
+        pltpu.VMEM((PIECES, rows, half), BF),
+        pltpu.VMEM((PIECES, rows, half), BF),
+        pltpu.VMEM((PIECES, rows, right), BF),
+        pltpu.VMEM((PIECES, rows, right), BF),
+        pltpu.SemaphoreType.DMA((KINDS, PIECES)),
+        pltpu.SemaphoreType.DMA((KINDS, PIECES)),
+        pltpu.SemaphoreType.DMA((PIECES,)),
+        pltpu.SemaphoreType.DMA((1,)),
+    ]
+    if gathered:
+        out_shape.append(jax.ShapeDtypeStruct((8, PIECES, rows, gathered), BF))
+        out_specs.append(any_spec)
+        scratch += [pltpu.VMEM((PIECES, rows, gathered), BF), pltpu.SemaphoreType.DMA((PIECES,))]
+    results = pl.pallas_call(
+        kernel,
+        in_specs=[any_spec, any_spec] + [vmem] * len(owned),
+        out_specs=out_specs,
+        out_shape=out_shape,
+        scratch_shapes=scratch,
+        compiler_params=pltpu.CompilerParams(
+            collective_id=collective_id, has_side_effects=True, vmem_limit_bytes=VMEM_LIMIT
+        ),
+        name="product_scatter",
+    )(left, weight, *[o.reshape(PIECES, rows, o.shape[1]) for o in owned])
+    flat = [r.reshape(tokens, r.shape[2]) for r in results[: len(outs)]]
+    if gathered:
+        flat.append(results[-1].reshape(8 * tokens, gathered))
+    return flat
 
 
 def gather_dp(v):
@@ -263,8 +663,44 @@
     return lax.all_to_all(v, "seq", split_axis=0, concat_axis=0, tiled=True)
 
 
+def swap_all(parts, collective_id):
+    if lax.axis_size("seq") == 8:
+        return swap_plane(parts, collective_id)
+    return [swap_seq(p) for p in parts]
+
+
+def gather_all(own, parts, collective_id):
+    if lax.axis_size("seq") == 8:
+        return gather_plane(own, parts, collective_id)
+    return lax.all_gather(own, "seq", axis=0, tiled=True), [swap_seq(p) for p in parts]
+
+
+def product_all(left, weight, transposed, stats, epilogue, owned, outs, gathered, collective_id):
+    if lax.axis_size("seq") == 8:
+        return product_scatter(left, weight, transposed, stats, epilogue, owned, outs, gathered, collective_id)
+    depth = left.shape[1] - (EXTRA if stats else 0)
+    product = (nt if transposed else nn)(left[:, :depth], weight).astype(BF)
+    result = lax.psum_scatter(product, "seq", scatter_dimension=0, tiled=True).astype(F32)
+    stat = None
+    if stats:
+        stat = lax.psum_scatter(left[:, depth:].astype(F32), "seq", scatter_dimension=0, tiled=True)
+    written, sent = epilogue(result, stat, *owned)
+    written = [w.astype(d) for w, (_, d) in zip(written, outs)]
+    return written + ([lax.all_gather(sent, "seq", axis=0, tiled=True)] if gathered else [])
+
+
+def split_lanes(v):
+    lane = lax.broadcasted_iota(jnp.int32, (v.shape[0], EXTRA), 1)
+    high = v.astype(BF).astype(F32)
+    return jnp.where(lane == 0, high, jnp.where(lane == 1, v - high, 0.0)).astype(BF)
+
+
 def inverse_rms(square_mean):
     return lax.rsqrt(square_mean + EPSILON)
+
+
+def row_mean(v):
+    return jnp.mean(v, axis=1, keepdims=True)
 
 
 def on_device(
@@ -323,63 +759,91 @@
     def fold(gain, w):
         return (gain * w.astype(F32)).astype(BF)
 
+    def order(first, *rest):
+        return lax.optimization_barrier((first,) + rest)
+
     qfi_part = jnp.concatenate([to_heads(fold(gain_a, w)) for w in (w_query, w_forget, w_input)], axis=2)
-    qfi_full = gather_dp(swap_seq(qfi_part).reshape(ranks * rows, 3 * channels))
+    (qfi_swapped,) = swap_all([qfi_part], 1)
+    qfi_full = gather_dp(qfi_swapped.reshape(ranks * rows, 3 * channels))
+    out_pieces = lax.all_gather(fold(gain_o, w_output), "dp", axis=0)
+    gu_part = jnp.concatenate([to_units(fold(gain_f, w)) for w in (w_gate, w_up)], axis=2)
+    x16 = hidden[0]
+    x = x16.astype(F32)
+    normed = (x * inverse_rms(row_mean(x * x))).astype(BF)
+    _, normed, gu_part = order(qfi_swapped, normed, gu_part)
+    n1, (gu_swapped,) = gather_all(normed, [gu_part], 2)
     gap_pieces = lax.all_gather(gate_gap, "dp", axis=0)
     gap_own = swap_group(own_rows(gap_pieces)).transpose(1, 0, 2).reshape(1, channels).astype(F32)
-    out_pieces = lax.all_gather(fold(gain_o, w_output), "dp", axis=0)
-    out_own = swap_group(own_rows(out_pieces)).transpose(1, 0, 2, 3).reshape(channels, model)
-    gu_part = jnp.concatenate([to_units(fold(gain_f, w)) for w in (w_gate, w_up)], axis=2)
-    gu_full = gather_dp(swap_seq(gu_part).reshape(ranks * rows, 2 * units))
-    down_own = gather_dp(w_down)
-
     ids = lax.all_gather(jnp.concatenate([seg_ids, pad_mask], axis=0), "seq", axis=0)
     segment = ids[:, 0].reshape(tokens // BLOCK, BLOCK)
     live = jnp.sum(ids[:, 1]).reshape(1)
     ends = segment[:, -1]
     before = jnp.concatenate([segment[:1, 0], ends[:-1]])
     cut = jnp.sum((segment == before[:, None]).astype(jnp.int32), axis=1)
-
-    x = hidden[0].astype(F32)
-    factor_x = inverse_rms(jnp.mean(x * x, axis=1, keepdims=True))
-    normed_x = x * factor_x
-    n1 = gather_seq(normed_x.astype(BF))
+    out_own = swap_group(own_rows(out_pieces)).transpose(1, 0, 2, 3).reshape(channels, model)
+    gu_full = gather_dp(gu_swapped.reshape(ranks * rows, 2 * units))
+    down_own = gather_dp(w_down)
+
     qfi = nn(n1, qfi_full)
-    mixed, square, kept = mixer_forward(cut, live, qfi, gap_own)
-    square_all = lax.psum_scatter(square, "seq", scatter_dimension=0, tiled=True)
-    factor_o = inverse_rms(square_all / model)
-    attn_out = factor_o * scatter_seq(nn(mixed, out_own).astype(BF))
-    middle = x + attn_out
-    factor_m = inverse_rms(jnp.mean(middle * middle, axis=1, keepdims=True))
-    normed_m = middle * factor_m
-    n2 = gather_seq(normed_m.astype(BF))
+    mixed, kept = mixer_forward(cut, live, qfi, gap_own)
+    og16 = out_grad[0]
+    grad_all, _ = gather_all(og16, [], 3)
+
+    def after_output(result, stat, x16):
+        x = x16.astype(F32)
+        factor_o = inverse_rms(jnp.sum(stat, axis=1, keepdims=True) / model)
+        middle = x + factor_o * result
+        normed = middle * inverse_rms(row_mean(middle * middle))
+        return [middle, jnp.broadcast_to(factor_o, (x.shape[0], EXTRA))], normed.astype(BF)
+
+    middle, factor_o, n2 = product_all(
+        mixed, out_own, False, True, after_output, [x16], [(model, F32), (EXTRA, F32)], model, 4
+    )
     gate_up = nn(n2, gu_full)
     gate, up = gate_up[:, :units], gate_up[:, units:]
     sig_g = jax.nn.sigmoid(gate)
     act = gate * sig_g
     hidden_units = (act * up).astype(BF)
-    block_out = middle + scatter_seq(nn(hidden_units, down_own).astype(BF))
-
-    grad_all = gather_seq(out_grad[0])
+
     d_units = nt(grad_all, down_own)
-    grad_down = tn(hidden_units, grad_all).astype(BF)
     d_gate = (d_units * up * sig_g * (1.0 + gate * (1.0 - sig_g))).astype(BF)
     d_up = (d_units * act).astype(BF)
     d_gu = jnp.concatenate([d_gate, d_up], axis=1)
+    grad_down = tn(hidden_units, grad_all).astype(BF)
     grad_gu = tn(n2, d_gu).astype(BF)
-    d_n2 = scatter_seq(nt(d_gu, gu_full).astype(BF))
-    d_middle = out_grad[0].astype(F32) + factor_m * (
-        d_n2 - normed_m * jnp.mean(d_n2 * normed_m, axis=1, keepdims=True)
+
+    def after_ffn(result, stat, middle, og16, x16, factor_o):
+        factor_o = factor_o[:, :1]
+        factor_m = inverse_rms(row_mean(middle * middle))
+        normed = middle * factor_m
+        d_middle = og16.astype(F32) + factor_m * (result - normed * row_mean(result * normed))
+        mean_o = row_mean(d_middle * (middle - x16.astype(F32)))
+        beta = split_lanes(factor_o * factor_o * mean_o)
+        return [d_middle], jnp.concatenate([(factor_o * d_middle).astype(BF), beta], axis=1)
+
+    d_middle, d_attn = product_all(
+        d_gu, gu_full, True, False, after_ffn, [middle, og16, x16, factor_o], [(model, F32)], model + EXTRA, 5
     )
-    mean_o = jnp.mean(d_middle * attn_out, axis=1, keepdims=True)
-    d_attn = gather_seq((factor_o * d_middle).astype(BF))
-    beta = gather_seq(factor_o * factor_o * mean_o)
+    beta = jnp.sum(d_attn[:, model:].astype(F32), axis=1, keepdims=True)
+    d_attn = d_attn[:, :model]
+
+    def after_down(result, stat, middle):
+        return [(middle + result).astype(BF)], None
+
+    (block_out,) = product_all(hidden_units, down_own, False, False, after_down, [middle], [(model, BF)], 0, 6)
+    mixed = mixed[:, :channels]
     grad_out = tn(mixed, d_attn).astype(BF)
     d_mixed = (nt(d_attn, out_own) - beta * mixed.astype(F32)).astype(BF)
     d_qfi, gap_grad = mixer_backward(cut, live, qfi, gap_own, kept, d_mixed)
     grad_qfi = tn(n1, d_qfi).astype(BF)
-    d_n1 = scatter_seq(nt(d_qfi, qfi_full).astype(BF))
-    hidden_grad = d_middle + factor_x * (d_n1 - normed_x * jnp.mean(d_n1 * normed_x, axis=1, keepdims=True))
+
+    def after_mixer(result, stat, x16, d_middle):
+        x = x16.astype(F32)
+        factor_x = inverse_rms(row_mean(x * x))
+        normed = x * factor_x
+        return [(d_middle + factor_x * (result - normed * row_mean(result * normed))).astype(BF)], None
+
+    (hidden_grad,) = product_all(d_qfi, qfi_full, True, False, after_mixer, [x16, d_middle], [(model, BF)], 0, 7)
 
     g_down = scatter_dp(grad_down).astype(F32)
     gu_rows = swap_seq(scatter_dp(grad_gu)).reshape(ranks, rows, 2 * units).astype(F32)
@@ -399,8 +863,8 @@
     g_ffn_gain = rowdot(w_gate, gate_rows) + rowdot(w_up, up_rows)
     g_out_gain = rowdot(w_output, out_rows)
     return (
-        block_out[None].astype(BF),
-        hidden_grad[None].astype(BF),
+        block_out[None],
+        hidden_grad[None],
         g_attn_gain,
         g_gap,
         g_out_gain,

time: 1270 us -> 920 us (0.72)
  waiting for transfers between devices: 803 us -> 93.8 us
  Pallas kernels: 51.8 us -> 517 us
  matrix products: 177 us -> 120 us
  blocking collectives: 112 us -> 63.4 us
  local copies, waits for them, and re-layouts: 43.8 us -> 59.4 us
    pallas_call x0 -> x7, Pallas kernels: none -> 466 us  [the longest x4 340 us: product_scatter(): pl.pallas_call(kernel, in_specs=[any_spec, any_spec] + [vmem] * len(owned...]
    reduce_scatter x5 -> x0, waiting for transfers between devices: 293 us -> none  [the longest x4 293 us: scatter_seq(): lax.psum_scatter(v, 'seq', scatter_dimension=0, tiled=True).astype(F32)]
    all_gather x4 -> x0, waiting for transfers between devices: 194 us -> none  [gather_seq(): return lax.all_gather(v, 'seq', axis=0, tiled=True)]
    all_gather x3, waiting for transfers between devices: 178 us -> 0.02 us  [gather_dp(): return lax.all_gather(v, 'dp', axis=0, tiled=True)]
    dot_general x12 -> x8, matrix products: 177 us -> 120 us  [dot(): return lax.dot_general(a, b, (dims, ((), ())), preferred_element_type=F32)]
    reduce_scatter x4, waiting for transfers between devices: 137 us -> 93.1 us  [scatter_dp(): return lax.psum_scatter(v, 'dp', scatter_dimension=0, tiled=True)]
    all_to_all x2 -> x1, blocking collectives: 42.1 us -> 16.2 us  [swap_seq(): return lax.all_to_all(v, 'seq', split_axis=0, concat_axis=0, tiled=True)]
    unnamed x3 -> x2, blocking collectives: 47 us -> 23 us
  transfers between devices with their start and end apart: 20 -> 10, of which waited for: 14 -> 2; matrix products, arithmetic and copies ran while one was open for 15% -> 14% of each run, Pallas kernels for 2% -> 42%
where the time goes in v2:
time: 920 us; the launch traced here: 910 us
  Pallas kernels  517 us (56%)
  matrix products  120 us (13%)
  waiting for transfers between devices  93.8 us (10%)
  blocking collectives  63.4 us (7%)
  local copies, waits for them, and re-layouts  59.4 us (6%)
  other arithmetic  33.4 us (4%)
  between operations  16.2 us (2%)
    pallas_call x4, Pallas kernels, product_scatter(): pl.pallas_call(kernel, in_specs=[any_spec, any_spec] + [vmem] * len(owned...  340 us
    dot_general x8, matrix products, dot(): return lax.dot_general(a, b, (dims, ((), ())), preferred_element_type=F32)  120 us
    pallas_call x2, Pallas kernels, gather_plane(): pl.pallas_call(kernel, in_specs=[any_spec] * (1 + count), out_specs=[any_...  112 us
    reduce_scatter x4, waiting for transfers between devices, scatter_dp(): return lax.psum_scatter(v, 'dp', scatter_dimension=0, tiled=True)  93.1 us
    pallas_call x1, Pallas kernels, mixer_backward(): pl.pallas_call(functools.partial(mixer_backward_kernel, heads), grid_spec...  29 us
    unnamed x2, blocking collectives  23 us
    pallas_call x1, Pallas kernels, mixer_forward(): pl.pallas_call(functools.partial(mixer_forward_kernel, heads), grid_spec=...  22.5 us
  transfers between devices with their start and end apart: 10, of which 2 were waited for; matrix products, arithmetic and copies ran while one was open for 14% of the time, Pallas kernels for 42%

profile of v2, /device:TPU:0, one launch (start us, length us, event | category | flops | bytes accessed | tf_op | source)
XLA Modules:
  0.0 910.4 jit_solution(3159890439122095271)
XLA Ops:
  14.9 13.9 %swap_plane.1 = bf16[8,64,768]{2,1,0:T(8,128)(2,1)} custom-call(bf16[8,64,768]{2,1,0:T(8,128)(2,1)} %pad_maximum_fusion.2.refs_0_), custom_call_target="tpu_custom_call" | custom-call | tf_op jit(solution)/shard_map/swap_plane/pallas_call | solution.py:407
  43.2 62.9 %gather_plane.2 = (bf16[8,5,64,2048]{3,2,1,0:T(8,128)(2,1)}, bf16[8,64,1408]{2,1,0:T(8,128)(2,1)}) custom-call(bf16[5,64,2048]{2,1,0:T(8,128)(2,1)} %bitcast.99, bf16[8,64,1408]{2,1,0:T(8,128)(2,1)} %pad_maximum_fusion.1.refs_0_), custom_call_target="tpu_custom_call" | custom-call | tf_op jit(solution)/shard_map/gather_plane/pallas_call | solution.py:448
  107.6 12.0 %all-reduce = bf16[256]{0:T(256)(128)(2,1)S(1)} all-reduce(bf16[256]{0:T(256)(128)(2,1)S(1)} %dynamic-update-slice), channel_id=3, replica_groups=mesh['dp'=4,'seq'=8] {'dp'}, use_global_device_ids=true, to_apply=%add | all-reduce | flops 256 | bytes 1024
  124.2 9.5 %all-gather.3 = s32[8,2,320]{2,1,0:T(2,128)S(1)} all-gather(s32[1,2,320]{2,1,0:T(2,128)S(1)} %add_bitcast_fusion), channel_id=2, replica_groups=mesh['dp'=4,'seq'=8] {'seq'}, dimensions={0}, use_global_device_ids=true | all-gather | bytes 23040 | tf_op jit(solution)/shard_map/all_gather | solution.py:777
  137.1 49.2 %gather_plane.3 = bf16[8,5,64,2048]{3,2,1,0:T(8,128)(2,1)} custom-call(bf16[5,64,2048]{2,1,0:T(8,128)(2,1)} %bitcast.96), custom_call_target="tpu_custom_call" | custom-call | tf_op jit(solution)/shard_map/gather_plane/pallas_call | solution.py:448
  193.1 13.8 %fusion.32.qfi_ref = f32[2560,768]{1,0:T(8,128)} fusion(bf16[2560,2048]{1,0:T(8,128)(2,1)} %bitcast.127, bf16[2048,768]{1,0:T(8,128)(2,1)} %all-gather.9.cloned.1.call-done.refs_1_), kind=kOutput, calls=%fused_computation.77 | convolution fusion | flops 8053063680 | bytes 21495808 | tf_op jit(solution)/shard_map/dot_general | solution.py:20
  206.9 22.5 %mixer_forward.1 = (bf16[2560,384]{1,0:T(8,128)(2,1)}, bf16[40,2,128,128]{3,2,1,0:T(8,128)(2,1)}) custom-call(s32[40]{0:T(128)} %convert_reduce_fusion.1.cut_ref, s32[1]{0:T(128)} %bitcast.3.live_ref, f32[2560,768]{1,0:T(8,128)} %fusion.32.qfi_ref, f32[1,256]{1,0:T(1,128)} %reshape.222.gap_ref), custom_call_target="tpu_custom_call" | custom-call | flops 838860800 | bytes 13107200 | tf_op jit(solution)/shard_map/mixer_forward/pallas_call | solution.py:189
  229.4 103.2 %product_scatter.4 = (f32[5,64,2048]{2,1,0:T(8,128)}, f32[5,64,128]{2,1,0:T(8,128)}, bf16[8,5,64,2048]{3,2,1,0:T(8,128)(2,1)}) custom-call(bf16[8,5,64,384]{3,2,1,0:T(8,128)(2,1)} %bitcast.113, bf16[256,2048]{1,0:T(8,128)(2,1)} %bitcast.106, bf16[5,64,2048]{2,1,0:T(8,128)(2,1)} %bitcast.87), custom_call_target="tpu_custom_call" | custom-call | tf_op jit(solution)/shard_map/product_scatter/pallas_call | solution.py:637
  332.7 22.7 %fusion.33 = f32[2560,1408]{0,1:T(8,128)} fusion(bf16[2560,2048]{1,0:T(8,128)(2,1)} %bitcast.129, bf16[2048,1408]{1,0:T(8,128)(2,1)} %all-gather.11.cloned.1.call-done.refs_1_), kind=kOutput, calls=%fused_computation.78 | convolution fusion | flops 14763950080 | bytes 30670848 | tf_op jit(solution)/shard_map/dot_general | solution.py:20
  355.4 18.8 %multiply_convert_fusion.1 = (bf16[2560,704]{0,1:T(8,128)(2,1)S(1)}, bf16[2560,704]{0,1:T(8,128)(2,1)}, bf16[2560,704]{0,1:T(8,128)(2,1)}) fusion(f32[2560,1408]{0,1:T(8,128)} %fusion.33, bf16[2560,2048]{1,0:T(8,128)(2,1)} %bitcast.92, bf16[704,2048]{1,0:T(8,128)(2,1)} %all-gather.13.cloned.1.call-done.refs_1_), kind=kOutput, calls=%fused_computation.7 | convolution fusion | flops 7409008640 | bytes 38600704 | tf_op jit(solution)/shard_map/dot_general | solution.py:20
  381.6 10.0 %copy.69 = bf16[2560,1408]{1,0:T(8,128)(2,1)} copy(bf16[2560,1408]{0,1:T(8,128)(2,1)} %pad_maximum_fusion) | data formatting | bytes 14417920 | tf_op jit(solution)/shard_map/concatenate | solution.py:811
  391.6 109.8 %product_scatter.6 = (f32[5,64,2048]{2,1,0:T(8,128)}, bf16[8,5,64,2176]{3,2,1,0:T(8,128)(2,1)}) custom-call(bf16[8,5,64,1408]{3,2,1,0:T(8,128)(2,1)} %bitcast.90, bf16[2048,1408]{1,0:T(8,128)(2,1)} %all-gather.11.cloned.1.call-done.refs_1_, f32[5,64,2048]{2,1,0:T(8,128)} %get-tuple-element.32.refs_2_, bf16[5,64,2048]{2,1,0:T(8,128)(2,1)} %bitcast.97, ...), custom_call_target="tpu_custom_call" | custom-call | tf_op jit(solution)/shard_map/product_scatter/pallas_call | solution.py:637
  502.8 8.1 fusion.8.grad_ref
  510.9 29.0 %mixer_backward.1 = (bf16[2560,768]{1,0:T(8,128)(2,1)}, f32[1,256]{1,0:T(1,128)}) custom-call(s32[40]{0:T(128)} %convert_reduce_fusion.1.cut_ref, s32[1]{0:T(128)} %bitcast.3.live_ref, f32[2560,768]{1,0:T(8,128)} %fusion.32.qfi_ref, f32[1,256]{1,0:T(1,128)} %reshape.222.gap_ref, bf16[40,2,128,128]{3,2,1,0:T(8,128)(2,1)} %get-tuple-element.33.kept_ref, ...), custom_call_target="tpu_custom_call" | custom-call | flops 2013265920 | bytes 18350080 | tf_op jit(solution)/shard_map/mixer_backward/pallas_call | solution.py:219
  539.9 14.0 %convolution_convert_fusion.1 = bf16[2048,768]{1,0:T(8,128)(2,1)} fusion(bf16[2560,2048]{1,0:T(8,128)(2,1)} %bitcast.128, bf16[2560,768]{1,0:T(8,128)(2,1)} %get-tuple-element.36), kind=kOutput, calls=%fused_computation.13 | convolution fusion | flops 8054636544 | bytes 17563648 | tf_op jit(solution)/shard_map/dot_general | solution.py:20
  553.9 22.6 %convolution_convert_fusion = bf16[2048,1408]{1,0:T(8,128)(2,1)} fusion(bf16[2560,2048]{1,0:T(8,128)(2,1)} %bitcast.130, bf16[2560,704]{0,1:T(8,128)(2,1)} %get-tuple-element.42, bf16[2560,704]{0,1:T(8,128)(2,1)} %copy-done.4), kind=kOutput, calls=%fused_computation.4 | convolution fusion | flops 14781251584 | bytes 23461888 | tf_op jit(solution)/shard_map/dot_general | solution.py:20
  576.7 6.9 fusion.13
  589.1 12.6 %convolution_convert_fusion.2 = bf16[704,2048]{1,0:T(8,128)(2,1)} fusion(bf16[2560,704]{0,1:T(8,128)(2,1)} %get-tuple-element.43, bf16[2560,2048]{1,0:T(8,128)(2,1)} %bitcast.93), kind=kOutput, calls=%fused_computation.14 | convolution fusion | flops 7383416832 | bytes 16973824 | tf_op jit(solution)/shard_map/dot_general | solution.py:20
  611.6 16.2 %all_to_all.41 = bf16[8,64,768]{2,1,0:T(8,128)(2,1)S(1)} all-to-all(bf16[8,64,768]{2,1,0:T(8,128)(2,1)} %bitcast.121), channel_id=1, replica_groups=mesh['dp'=4,'seq'=8] {'seq'}, dimensions={0} | all-to-all | bytes 1572864 | tf_op jit(solution)/shard_map/all_to_all | solution.py:663
  627.8 88.3 %reduce-scatter.9.cloned.1.call-done = bf16[512,1408]{1,0:T(8,128)(2,1)} async-done(((bf16[2048,1408]{1,0:T(8,128)(2,1)}), bf16[512,1408]{1,0:T(8,128)(2,1)}) %reduce-scatter.9.cloned.1.call-update) | async-done | bytes 1441808 | tf_op jit(solution)/shard_map/reduce_scatter | solution.py:659
  720.4 6.1 copy.68
  726.5 65.1 %product_scatter.7 = bf16[5,64,2048]{2,1,0:T(8,128)(2,1)} custom-call(bf16[8,5,64,768]{3,2,1,0:T(8,128)(2,1)} %bitcast.108, bf16[2048,768]{1,0:T(8,128)(2,1)} %all-gather.9.cloned.1.call-done.refs_1_, bf16[5,64,2048]{2,1,0:T(8,128)(2,1)} %bitcast.89, f32[5,64,2048]{2,1,0:T(8,128)} %get-tuple-element.37.refs_3_), custom_call_target="tpu_custom_call" | custom-call | tf_op jit(solution)/shard_map/product_scatter/pallas_call | solution.py:637
  793.0 61.8 %product_scatter.5 = bf16[5,64,2048]{2,1,0:T(8,128)(2,1)} custom-call(bf16[8,5,64,704]{3,2,1,0:T(8,128)(2,1)} %bitcast.91, bf16[704,2048]{1,0:T(8,128)(2,1)} %all-gather.13.cloned.1.call-done.refs_1_, f32[5,64,2048]{2,1,0:T(8,128)} %get-tuple-element.32.refs_2_), custom_call_target="tpu_custom_call" | custom-call | tf_op jit(solution)/shard_map/product_scatter/pallas_call | solution.py:637
  854.8 11.0 %all-reduce.1 = f32[256]{0:T(256)S(1)} all-reduce(f32[256]{0:T(256)S(1)} %reshape.214), channel_id=6, replica_groups=mesh['dp'=4,'seq'=8] {'dp'}, use_global_device_ids=true, to_apply=%region_8.0.clone | all-reduce | flops 256 | bytes 2048
  (152 shorter events, 104.1 us)
Async XLA Ops:
  7.2 179.2 %all-gather.15.cloned.1.call-start = ((), (), s32[]{:S(2)}) async-start(), calls=%async_computation.17 | async-start | bytes 1310720 | tf_op jit(solution)/shard_map/all_gather | solution.py:768
  10.2 182.9 %all-gather.9.cloned.1.call-start = ((), (), s32[]{:S(2)}) async-start(), calls=%async_computation.10 | async-start | bytes 3932160 | tf_op jit(solution)/shard_map/all_gather | solution.py:655
  12.8 16.0 %copy-start.19 = (bf16[64]{0:T(256)(128)(2,1)S(1)}, bf16[64]{0:T(256)(128)(2,1)}, u32[]{:S(2)}) copy-start(bf16[64]{0:T(256)(128)(2,1)} %param.25) | copy-start | bytes 388
  12.8 16.0 %copy-start.6 = (bf16[64,5632]{1,0:T(8,128)(2,1)S(1)}, bf16[64,5632]{1,0:T(8,128)(2,1)}, u32[]{:S(2)}) copy-start(bf16[64,5632]{1,0:T(8,128)(2,1)} %param.26) | copy-start | bytes 2162692
  28.8 303.9 %all-gather.11.cloned.1.call-start = ((), (), s32[]{:S(2)}) async-start(), calls=%async_computation.11 | async-start | bytes 7208960 | tf_op jit(solution)/shard_map/all_gather | solution.py:655
  32.7 6.0 copy-start
  41.8 64.3 %copy-start.15 = (u32[32]{0:T(128)S(1)}, u32[32]{0:T(128)}, u32[]{:S(2)}) copy-start(u32[32]{0:T(128)} %constant.18) | copy-start | bytes 388
  41.8 65.5 %copy-start.20 = (bf16[64]{0:T(256)(128)(2,1)S(1)}, bf16[64]{0:T(256)(128)(2,1)}, u32[]{:S(2)}) copy-start(bf16[64]{0:T(256)(128)(2,1)} %param.19) | copy-start | bytes 388
  41.8 82.3 %copy-start.16 = (s32[1,320]{1,0:T(1,128)S(1)}, s32[1,320]{1,0:T(1,128)}, u32[]{:S(2)}) copy-start(s32[1,320]{1,0:T(1,128)} %param.17) | copy-start | bytes 3844
  41.8 82.3 %copy-start.17 = (s32[1,320]{1,0:T(1,128)S(1)}, s32[1,320]{1,0:T(1,128)}, u32[]{:S(2)}) copy-start(s32[1,320]{1,0:T(1,128)} %param.16) | copy-start | bytes 3844
  120.3 16.1 %all-to-all-start = ((bf16[2,2,64]{2,1,0:T(2,128)(2,1)}), bf16[2,2,64]{2,1,0:T(2,128)(2,1)S(1)}, u32[]{:S(2)}, u32[]{:S(2)}) async-start(bf16[2,2,64]{2,1,0:T(2,128)(2,1)} %reshape.196), calls=%async_computation | async-start | bytes 2048 | tf_op jit(solution)/shard_map/all_to_all | solution.py:755
  123.5 231.9 %all-gather.13.cloned.1.call-start = ((), (), s32[]{:S(2)}) async-start(), calls=%async_computation.12 | async-start | bytes 3604480 | tf_op jit(solution)/shard_map/all_gather | solution.py:655
  124.1 487.5 %reduce-scatter.5.cloned.1.call-start = ((), (), s32[]{:S(2)}) async-start(), calls=%async_computation.13 | async-start | bytes 3932160 | tf_op jit(solution)/shard_map/reduce_scatter | solution.py:659
  391.6 111.1 %copy-start.3 = (bf16[2,2,64,2048]{3,2,1,0:T(8,128)(2,1)S(1)}, bf16[2,2,64,2048]{3,2,1,0:T(8,128)(2,1)}, u32[]{:S(2)}) copy-start(bf16[2,2,64,2048]{3,2,1,0:T(8,128)(2,1)} %copy.67) | copy-start | bytes 3145732
  391.6 111.2 %copy-start.7 = (bf16[2560,384]{1,0:T(8,128)(2,1)S(1)}, bf16[2560,384]{1,0:T(8,128)(2,1)}, u32[]{:S(2)}) copy-start(bf16[2560,384]{1,0:T(8,128)(2,1)} %get-tuple-element.29) | copy-start | bytes 5898244
  553.9 162.2 %reduce-scatter.9.cloned.1.call-start = ((), (), s32[]{:S(2)}) async-start(), calls=%async_computation.15 | async-start | bytes 7208960 | tf_op jit(solution)/shard_map/reduce_scatter | solution.py:659
  576.6 289.8 %reduce-scatter.7.cloned.1.call-start = ((), (), s32[]{:S(2)}) async-start(), calls=%async_computation.14 | async-start | bytes 1310720 | tf_op jit(solution)/shard_map/reduce_scatter | solution.py:659
  589.1 279.8 %reduce-scatter.11.cloned.1.call-start = ((), (), s32[]{:S(2)}) async-start(), calls=%async_computation.16 | async-start | bytes 3604480 | tf_op jit(solution)/shard_map/reduce_scatter | solution.py:659
  589.1 13.1 %copy-start.18 = (f32[1,256]{1,0:T(1,128)S(1)}, f32[1,256]{1,0:T(1,128)}, u32[]{:S(2)}) copy-start(f32[1,256]{1,0:T(1,128)} %get-tuple-element.38) | copy-start | bytes 3076
  716.1 162.8 %all-to-all-start.5 = ((bf16[8,64,1408]{2,1,0:T(8,128)(2,1)}), bf16[8,64,1408]{2,1,0:T(8,128)(2,1)S(1)}, u32[]{:S(2)}, u32[]{:S(2)}) async-start(bf16[8,64,1408]{2,1,0:T(8,128)(2,1)} %bitcast.114), calls=%async_computation.8 | async-start | bytes 2883584 | tf_op jit(solution)/shard_map/all_to_all | solution.py:663
  793.0 73.4 %copy-start.8 = (bf16[64,2048]{1,0:T(8,128)(2,1)S(1)}, bf16[64,2048]{1,0:T(8,128)(2,1)}, u32[]{:S(2)}) copy-start(bf16[64,2048]{1,0:T(8,128)(2,1)} %param.24) | copy-start | bytes 786436
  793.0 73.4 %copy-start.10 = (f32[64]{0:T(128)S(1)}, f32[64]{0:T(128)}, u32[]{:S(2)}) copy-start(f32[64]{0:T(128)} %copy-done.9) | copy-start | bytes 772
  892.1 5.0 copy-start.14
  897.2 5.2 copy-start.1
  (7 other events, 13.3 us)
Sparse Core Ops, SparseCore 0:
  10.3 30.6 all-gather.14
  42.5 63.0 all-gather.8
  107.2 106.9 all-gather.10
  215.5 57.4 all-gather.12
  554.0 57.5 reduce-scatter.4
  613.7 102.2 reduce-scatter.8
  718.4 27.6 reduce-scatter.6
  748.5 54.8 reduce-scatter.10

commit v3 on v2

v3 whole, which is shorter than its diff:
```python
import functools

import jax
import jax.numpy as jnp
from jax import lax
from jax.experimental import pallas as pl
from jax.experimental.pallas import tpu as pltpu
from jax.sharding import PartitionSpec as P

HEADS = 16
BLOCK = 64
UNROLL = 2
UNROLL_FORWARD = 4
EPSILON = 1e-06
EXTRA = 128
BF = jnp.bfloat16
F32 = jnp.float32


def dot(a, b, dims):
    return lax.dot_general(a, b, (dims, ((), ())), preferred_element_type=F32)


def nn(a, b):
    return dot(a, b, ((1,), (0,)))


def nt(a, b):
    return dot(a, b, ((1,), (1,)))


def tn(a, b):
    return dot(a, b, ((0,), (0,)))


def inverse_rms(square_mean):
    return lax.rsqrt(square_mean + EPSILON)


def row_mean(v):
    return jnp.mean(v, axis=1, keepdims=True)


def split_sum(tri, v):
    high = v.astype(BF)
    low = (v - high.astype(F32)).astype(BF)
    return nn(tri, high) + nn(tri, low)


def chunk_prep(qfi, gap, live, width):
    query_pre, forget_pre, input_pre = (
        qfi[:, :width],
        qfi[:, width : 2 * width],
        qfi[:, 2 * width :],
    )
    sig_q = jax.nn.sigmoid(query_pre)
    sig_nf = jax.nn.sigmoid(-forget_pre)
    key = gap * sig_nf
    return query_pre, sig_q, sig_nf, key, input_pre * live


def triangle(lower):
    row = lax.broadcasted_iota(jnp.int32, (BLOCK, BLOCK), 0)
    col = lax.broadcasted_iota(jnp.int32, (BLOCK, BLOCK), 1)
    return (row >= col) if lower else (row <= col)


def chunk_masks(cut):
    row = lax.broadcasted_iota(jnp.int32, (BLOCK, BLOCK), 0)
    col = lax.broadcasted_iota(jnp.int32, (BLOCK, BLOCK), 1)
    allowed = (row >= col) & ((row >= cut) == (col >= cut))
    at = lax.broadcasted_iota(jnp.int32, (BLOCK, 1), 0)
    inherits = (at < cut).astype(F32)
    tail = ((at >= cut) | (cut >= BLOCK)).astype(F32)
    whole = (cut >= BLOCK).astype(F32)
    return allowed, inherits, tail, whole


def mixer_forward_kernel(heads, cut_ref, live_ref, n_ref, w_ref, gap_ref, mixed_ref, kept_ref, qfi_ref, state):
    step = pl.program_id(0)
    width = heads * 128

    @pl.when(step == 0)
    def _():
        state[...] = jnp.zeros_like(state)

    qfi_ref[...] = nn(n_ref[...], w_ref[...])
    lower = triangle(True).astype(BF)
    for u in range(UNROLL_FORWARD):
        chunk = step * UNROLL_FORWARD + u
        rows = slice(u * BLOCK, (u + 1) * BLOCK)
        at = lax.broadcasted_iota(jnp.int32, (BLOCK, 1), 0) + chunk * BLOCK
        live = (at < live_ref[0]).astype(F32)
        query_pre, sig_q, sig_nf, key, value = chunk_prep(qfi_ref[rows, :], gap_ref[...], live, width)
        query = query_pre * sig_q
        total = split_sum(lower, jnp.log1p(-key))
        centre = total[BLOCK // 2 : BLOCK // 2 + 1]
        ending = total[BLOCK - 1 :]
        scaled_q = (query * jnp.exp(total - centre)).astype(BF)
        scaled_k = (key * jnp.exp(centre - total)).astype(BF)
        value_low = value.astype(BF)
        allowed, inherits, tail, whole = chunk_masks(cut_ref[chunk])
        value_tail = (value * tail).astype(BF)
        e_centre = jnp.exp(centre)
        e_rest = jnp.exp(ending - centre)
        e_all = jnp.exp(ending) * whole
        square = jnp.zeros((BLOCK, 1), F32)
        for h in range(heads):
            cols = slice(h * 128, (h + 1) * 128)
            before = state[h]
            kept_ref[u, h] = before.astype(BF)
            scores = jnp.where(allowed, nt(scaled_q[:, cols], scaled_k[:, cols]), 0.0)
            inner = nn(scores.astype(BF), value_low[:, cols])
            outer = nt(scaled_q[:, cols], (before * e_centre[:, cols]).astype(BF))
            mixed = inner + outer * inherits
            square = square + jnp.sum(mixed * mixed, axis=1, keepdims=True)
            mixed_ref[rows, cols] = mixed.astype(BF)
            state[h] = before * e_all[:, cols] + tn(value_tail[:, cols], scaled_k[:, cols]) * e_rest[:, cols]
        lane = lax.broadcasted_iota(jnp.int32, (BLOCK, EXTRA), 1)
        high = square.astype(BF).astype(F32)
        mixed_ref[rows, width:] = jnp.where(lane == 0, high, jnp.where(lane == 1, square - high, 0.0)).astype(BF)


def mixer_backward_kernel(heads, cut_ref, live_ref, qfi_ref, gap_ref, kept_ref, grad_ref, out_ref, gap_out_ref, state):
    step = pl.program_id(0)
    last = pl.num_programs(0) - 1
    width = heads * 128

    @pl.when(step == 0)
    def _():
        state[...] = jnp.zeros_like(state)
        gap_out_ref[...] = jnp.zeros_like(gap_out_ref)

    lower = triangle(True).astype(BF)
    upper = triangle(False).astype(BF)
    for u in reversed(range(UNROLL)):
        chunk = (last - step) * UNROLL + u
        rows = slice(u * BLOCK, (u + 1) * BLOCK)
        at = lax.broadcasted_iota(jnp.int32, (BLOCK, 1), 0) + chunk * BLOCK
        live = (at < live_ref[0]).astype(F32)
        gap = gap_ref[...]
        query_pre, sig_q, sig_nf, key, value = chunk_prep(qfi_ref[rows, :], gap, live, width)
        query = query_pre * sig_q
        total = split_sum(lower, jnp.log1p(-key))
        centre = total[BLOCK // 2 : BLOCK // 2 + 1]
        ending = total[BLOCK - 1 :]
        e_q = jnp.exp(total - centre)
        e_k = jnp.exp(centre - total)
        scaled_q = (query * e_q).astype(BF)
        scaled_k = (key * e_k).astype(BF)
        value_low = value.astype(BF)
        allowed, inherits, tail, whole = chunk_masks(cut_ref[chunk])
        value_tail = (value * tail).astype(BF)
        grad = grad_ref[rows, :]
        grad_in = (grad.astype(F32) * inherits).astype(BF)
        e_centre = jnp.exp(centre)
        e_rest = jnp.exp(ending - centre)
        e_all = jnp.exp(ending) * whole
        d_query, d_key, d_value, d_total, d_end = [], [], [], [], []
        for h in range(heads):
            cols = slice(h * 128, (h + 1) * 128)
            before = kept_ref[u, h].astype(F32)
            after = state[h]
            q, k, v, g, gi = scaled_q[:, cols], scaled_k[:, cols], value_low[:, cols], grad[:, cols], grad_in[:, cols]
            vt = value_tail[:, cols]
            scores = jnp.where(allowed, nt(q, k), 0.0).astype(BF)
            d_scores = jnp.where(allowed, nt(g, v), 0.0).astype(BF)
            shifted = (before * e_centre[:, cols]).astype(BF)
            onward = (after * e_rest[:, cols]).astype(BF)
            dq = nn(d_scores, k) + nn(gi, shifted)
            dk_state = nn(vt, onward)
            dk = tn(d_scores, q) + dk_state
            dv = tn(scores, g) + nt(k, onward) * tail
            k32 = k.astype(F32)
            d_total.append(dq * q.astype(F32) - dk * k32)
            d_end.append(
                jnp.sum(after * before, axis=0, keepdims=True) * e_all[:, cols]
                + jnp.sum(dk_state * k32, axis=0, keepdims=True)
            )
            state[h] = after * e_all[:, cols] + tn(gi, q) * e_centre[:, cols]
            d_query.append(dq)
            d_key.append(dk)
            d_value.append(dv)
        d_query = jnp.concatenate(d_query, axis=1) * e_q
        d_key = jnp.concatenate(d_key, axis=1) * e_k
        d_value = jnp.concatenate(d_value, axis=1) * live
        d_log = split_sum(upper, jnp.concatenate(d_total, axis=1)) + jnp.concatenate(d_end, axis=1)
        d_key = d_key - d_log / (1.0 - key)
        gap_out_ref[...] += jnp.sum(d_key * sig_nf, axis=0, keepdims=True)
        out_ref[rows, :width] = (d_query * sig_q * (1.0 + query_pre * (1.0 - sig_q))).astype(BF)
        out_ref[rows, width : 2 * width] = (-d_key * key * (1.0 - sig_nf)).astype(BF)
        out_ref[rows, 2 * width :] = d_value.astype(BF)


MESH = pl.DeviceIdType.MESH
PIECES = 5
VMEM_LIMIT = 60 * 1024 * 1024
(S_X, S_Y, S_CORE, S_DIAG_Y, S_DIAG_X, S_CORE_X, S_CORE_Y, S_CORE_D, R_CORE, R_X, R_Y, R_LAST_Y, R_LAST_X, KINDS) = range(14)


class Place:
    def __init__(self):
        self.plane = lax.axis_index("dp")
        me = lax.axis_index("seq")
        self.me = me
        self.core = me % 2
        self.x = (me // 2) % 2
        self.y = me // 4

    def rank(self, fy=0, fx=0, fc=0):
        y = 1 - self.y if fy else self.y
        x = 1 - self.x if fx else self.x
        core = 1 - self.core if fc else self.core
        return 4 * y + 2 * x + core

    def device(self, fy=0, fx=0, fc=0):
        return (self.plane, self.rank(fy, fx, fc))


def greet(place):
    barrier = pltpu.get_barrier_semaphore()
    for flip in ((0, 0, 1), (0, 1, 0), (1, 0, 0)):
        pl.semaphore_signal(barrier, inc=1, device_id=place.device(*flip), device_id_type=MESH)
    pl.semaphore_wait(barrier, 3)


def remote(src, dst, sems, kind, b, device):
    send, recv = sems
    return pltpu.make_async_remote_copy(
        src_ref=src,
        dst_ref=dst,
        send_sem=send.at[kind, b],
        recv_sem=recv.at[kind, b],
        device_id=device,
        device_id_type=MESH,
    )


class Gather:
    def __init__(self, place, own, full, sems, local_sem):
        self.p, self.own, self.full, self.sems, self.local = place, own, full, sems, local_sem
        self.half = full.shape[2] // 2

    def keep(self, b):
        return pltpu.make_async_copy(self.own.at[b], self.full.at[self.p.me, b], self.local.at[b])

    def first(self, b):
        p, dst = self.p, self.full.at[self.p.me, b]
        return [
            remote(self.own.at[b], dst, self.sems, S_X, b, p.device(0, 1, 0)),
            remote(self.own.at[b], dst, self.sems, S_Y, b, p.device(1, 0, 0)),
            remote(self.own.at[b], dst, self.sems, S_CORE, b, p.device(0, 0, 1)),
        ]

    def second(self, b):
        p, h = self.p, self.half
        from_x, from_y = self.full.at[p.rank(0, 1, 0), b], self.full.at[p.rank(1, 0, 0), b]
        up, down = from_x.at[pl.ds(0, h)], from_y.at[pl.ds(h, h)]
        return [
            remote(up, up, self.sems, S_DIAG_Y, b, p.device(1, 0, 0)),
            remote(down, down, self.sems, S_DIAG_X, b, p.device(0, 1, 0)),
            remote(from_x, from_x, self.sems, S_CORE_X, b, p.device(0, 0, 1)),
            remote(from_y, from_y, self.sems, S_CORE_Y, b, p.device(0, 0, 1)),
        ]

    def third(self, b):
        p = self.p
        block = self.full.at[p.rank(1, 1, 0), b]
        return [remote(block, block, self.sems, S_CORE_D, b, p.device(0, 0, 1))]

    def arrived(self, kind, b, flips, rows=None):
        block = self.full.at[self.p.rank(*flips), b]
        if rows is not None:
            block = block.at[pl.ds(rows * self.half, self.half)]
        remote(block, block, self.sems, kind, b, self.p.device(0, 0, 1)).wait_recv()

    def start(self, b):
        self.keep(b).start()
        for copy in self.first(b):
            copy.start()

    def forward(self, b):
        self.arrived(S_X, b, (0, 1, 0))
        self.arrived(S_Y, b, (1, 0, 0))
        for copy in self.second(b):
            copy.start()

    def forward_last(self, b):
        self.arrived(S_DIAG_Y, b, (1, 1, 0), 0)
        self.arrived(S_DIAG_X, b, (1, 1, 0), 1)
        for copy in self.third(b):
            copy.start()

    def finish(self, b):
        self.arrived(S_CORE, b, (0, 0, 1))
        self.arrived(S_CORE_X, b, (0, 1, 1))
        self.arrived(S_CORE_Y, b, (1, 0, 1))
        self.arrived(S_CORE_D, b, (1, 1, 1))

    def drain(self, b):
        self.keep(b).wait()
        for copy in self.first(b) + self.second(b) + self.third(b):
            copy.wait_send()


def swap_starts(place, parts, outs, send, recv, local):
    copies = []
    for i, (part, out) in enumerate(zip(parts, outs)):
        own = pltpu.make_async_copy(part.at[place.me], out.at[place.me], local.at[i])
        own.start()
        for k, flips in enumerate(((0, 0, 1), (0, 1, 0), (1, 0, 0), (0, 1, 1), (1, 0, 1), (1, 1, 0), (1, 1, 1))):
            copy = pltpu.make_async_remote_copy(
                src_ref=part.at[place.rank(*flips)],
                dst_ref=out.at[place.me],
                send_sem=send.at[i, k],
                recv_sem=recv.at[i, k],
                device_id=place.device(*flips),
                device_id_type=MESH,
            )
            copy.start()
            there = out.at[place.rank(*flips)]
            copies.append((copy, pltpu.make_async_remote_copy(
                src_ref=there, dst_ref=there, send_sem=send.at[i, k], recv_sem=recv.at[i, k],
                device_id=place.device(*flips), device_id_type=MESH)))
        copies.append((own, None))
    return copies


def swap_waits(copies):
    for copy, arrival in copies:
        if arrival is None:
            copy.wait()
        else:
            copy.wait_send()
            arrival.wait_recv()


def greet_all(place):
    barrier = pltpu.get_barrier_semaphore()
    for flips in ((0, 0, 1), (0, 1, 0), (1, 0, 0), (0, 1, 1), (1, 0, 1), (1, 1, 0), (1, 1, 1)):
        pl.semaphore_signal(barrier, inc=1, device_id=place.device(*flips), device_id_type=MESH)
    pl.semaphore_wait(barrier, 7)


def fold(gain, w):
    return (gain * w.astype(F32)).astype(BF)


FLIPS = ((0, 0, 1), (0, 1, 0), (1, 0, 0), (0, 1, 1), (1, 0, 1), (1, 1, 0), (1, 1, 1))
ANY_SPEC = pl.BlockSpec(memory_space=pl.ANY)
VMEM_SPEC = pl.BlockSpec(memory_space=pltpu.VMEM)


def column_peers(place, planes):
    peers = []
    for hop in range(planes):
        for flip in (0, 1):
            if hop or flip:
                plane = lax.rem(place.plane + hop, planes)
                peers.append((plane, place.rank(0, 0, flip)))
    return peers


def column_spread(place, planes, src, dst, send, recv):
    waits = []
    for k, (plane, rank) in enumerate(column_peers(place, planes)):
        mine = dst.at[place.plane, place.core]
        copy = pltpu.make_async_remote_copy(
            src_ref=src, dst_ref=mine, send_sem=send.at[k], recv_sem=recv.at[k],
            device_id=(plane, rank), device_id_type=MESH,
        )
        copy.start()
        back = lax.rem(planes + 2 * place.plane - plane, planes)
        there = dst.at[back, lax.rem(rank, 2)]
        waits.append((copy, pltpu.make_async_remote_copy(
            src_ref=there, dst_ref=there, send_sem=send.at[k], recv_sem=recv.at[k],
            device_id=(plane, rank), device_id_type=MESH,
        )))
    return waits


def greet_column_and_plane(place, planes):
    barrier = pltpu.get_barrier_semaphore()
    devices = [place.device(*flips) for flips in FLIPS]
    devices += [p for p in column_peers(place, planes)[1:]]
    for device in devices:
        pl.semaphore_signal(barrier, inc=1, device_id=device, device_id_type=MESH)
    pl.semaphore_wait(barrier, len(devices))


def enter_plane(weights, gain, ids, gap, per_rank, groups, planes, collective_id):
    rows, model = weights[0].shape
    head = model // (8 * per_rank)
    channels = per_rank * head
    span = 8 // groups

    def kernel(q_ref, f_ref, i_ref, gain_ref, ids_ref, gap_ref, out_ref, ids_out, gap_out, part, *sems):
        send, recv, local, gap_send, gap_recv = sems
        place = Place()
        scale = gain_ref[...]
        for w, ref in enumerate((q_ref, f_ref, i_ref)):
            for a in range(groups):
                for m in range(span):
                    for j in range(per_rank):
                        h = (m * per_rank + j) * groups + a
                        at = w * channels + j * head
                        part[a * span + m, :, at : at + head] = fold(scale, ref[:, h * head : (h + 1) * head])
        greet_column_and_plane(place, planes)
        copies = swap_starts(place, [part], [out_ref], send, recv, local)
        gaps = column_spread(place, planes, gap_ref, gap_out, gap_send, gap_recv)
        own_gap = pltpu.make_async_copy(gap_ref, gap_out.at[place.plane, place.core], local.at[2])
        own_gap.start()
        own_ids = pltpu.make_async_copy(ids_ref, ids_out.at[place.me], local.at[1])
        own_ids.start()
        ids_copies = []
        for k, flips in enumerate(FLIPS):
            there = ids_out.at[place.rank(*flips)]
            made = [
                pltpu.make_async_remote_copy(
                    src_ref=src, dst_ref=dst, send_sem=send.at[1, k], recv_sem=recv.at[1, k],
                    device_id=place.device(*flips), device_id_type=MESH,
                )
                for src, dst in ((ids_ref, ids_out.at[place.me]), (there, there))
            ]
            made[0].start()
            ids_copies.append(made)
        swap_waits(copies)
        for copy, arrival in ids_copies + gaps:
            copy.wait_send()
            arrival.wait_recv()
        own_gap.wait()
        own_ids.wait()

    return pl.pallas_call(
        kernel,
        in_specs=[VMEM_SPEC] * 4 + [ANY_SPEC] * 2,
        out_specs=[ANY_SPEC] * 3,
        out_shape=[
            jax.ShapeDtypeStruct((8, rows, 3 * channels), BF),
            jax.ShapeDtypeStruct((8,) + ids.shape, ids.dtype),
            jax.ShapeDtypeStruct((planes, 2) + gap.shape, gap.dtype),
        ],
        scratch_shapes=[
            pltpu.VMEM((8, rows, 3 * channels), BF),
            pltpu.SemaphoreType.DMA((2, 7)),
            pltpu.SemaphoreType.DMA((2, 7)),
            pltpu.SemaphoreType.DMA((3,)),
            pltpu.SemaphoreType.DMA((2 * planes - 1,)),
            pltpu.SemaphoreType.DMA((2 * planes - 1,)),
        ],
        compiler_params=pltpu.CompilerParams(
            collective_id=collective_id, has_side_effects=True, vmem_limit_bytes=VMEM_LIMIT
        ),
        name="enter_plane",
    )(*weights, gain, ids, gap)


def gather_plane(x, w_gate, w_up, gain, planes, collective_id):
    tokens, width = x.shape
    rows = tokens // PIECES
    w_rows, every_unit = w_gate.shape
    units_in = every_unit // (8 * planes)
    units = units_in * planes
    x = x.reshape(PIECES, rows, width)

    def kernel(x_ref, gate_ref, up_ref, gain_ref, full, out_ref, normed, part, *sems):
        send, recv, local, swap_send, swap_recv, swap_local = sems
        place = Place()
        gather = Gather(place, normed, full, (send, recv), local)
        value = x_ref[0].astype(F32)
        normed[0] = (value * inverse_rms(row_mean(value * value))).astype(BF)
        greet_all(place)
        gather.start(0)
        for b in range(1, PIECES):
            value = x_ref[b].astype(F32)
            normed[b] = (value * inverse_rms(row_mean(value * value))).astype(BF)
            gather.start(b)
        scale = gain_ref[...]
        for side, ref in enumerate((gate_ref, up_ref)):
            for i in range(planes):
                for s in range(8):
                    at = (i * 8 + s) * units_in
                    to = side * units + i * units_in
                    part[s, :, to : to + units_in] = fold(scale, ref[:, at : at + units_in])
        copies = swap_starts(place, [part], [out_ref], swap_send, swap_recv, swap_local)
        for stage in (gather.forward, gather.forward_last, gather.finish):
            pl.loop(0, PIECES)(stage)
        swap_waits(copies)
        pl.loop(0, PIECES)(gather.drain)

    full, swapped = pl.pallas_call(
        kernel,
        in_specs=[VMEM_SPEC] * 4,
        out_specs=[ANY_SPEC] * 2,
        out_shape=[
            jax.ShapeDtypeStruct((8, PIECES, rows, width), BF),
            jax.ShapeDtypeStruct((8, w_rows, 2 * units), BF),
        ],
        scratch_shapes=[
            pltpu.VMEM((PIECES, rows, width), BF),
            pltpu.VMEM((8, w_rows, 2 * units), BF),
            pltpu.SemaphoreType.DMA((KINDS, PIECES)),
            pltpu.SemaphoreType.DMA((KINDS, PIECES)),
            pltpu.SemaphoreType.DMA((PIECES,)),
            pltpu.SemaphoreType.DMA((1, 7)),
            pltpu.SemaphoreType.DMA((1, 7)),
            pltpu.SemaphoreType.DMA((1,)),
        ],
        compiler_params=pltpu.CompilerParams(
            collective_id=collective_id, has_side_effects=True, vmem_limit_bytes=VMEM_LIMIT
        ),
        name="gather_plane",
    )(x, w_gate, w_up, gain)
    return full.reshape(8 * tokens, width), swapped


def finish_units(in_ref, weights, outs, scale, planes):
    ranks, rows, both = in_ref.shape
    units = both // 2
    units_in = units // planes
    total = jnp.zeros((rows, 1), F32)
    for side, (ref, out) in enumerate(zip(weights, outs)):
        for i in range(planes):
            for s in range(ranks):
                at = side * units + i * units_in
                to = (i * ranks + s) * units_in
                grad = in_ref[s, :, at : at + units_in].astype(F32)
                total += jnp.sum(grad * ref[:, to : to + units_in].astype(F32), axis=1, keepdims=True)
                out[:, to : to + units_in] = grad * scale
    return total


def exit_plane(summed, weights, gain, gap_grad, unit_rows, unit_weights, unit_gain, per_rank, groups, planes, collective_id):
    rows, model = weights[0].shape
    head = model // (8 * per_rank)
    channels = per_rank * head
    span = 8 // groups

    def kernel(sum_ref, q_ref, f_ref, i_ref, gain_ref, gap_ref, unit_ref, gate_ref, up_ref, unit_gain_ref,
               q_out, f_out, i_out, gain_out, gap_out, gate_out, up_out, unit_gain_out, landed, *sems):
        send, recv, local, gap_send, gap_recv = sems
        place = Place()
        greet_column_and_plane(place, planes)
        copies = swap_starts(place, [sum_ref], [landed], send, recv, local)
        gaps = column_spread(place, planes, gap_ref, gap_out, gap_send, gap_recv)
        own_gap = pltpu.make_async_copy(gap_ref, gap_out.at[place.plane, place.core], local.at[1])
        own_gap.start()
        unit_gain_out[...] = finish_units(unit_ref, (gate_ref, up_ref), (gate_out, up_out), unit_gain_ref[...], planes)
        swap_waits(copies)
        scale = gain_ref[...]
        total = jnp.zeros((rows, 1), F32)
        for w, (ref, out) in enumerate(((q_ref, q_out), (f_ref, f_out), (i_ref, i_out))):
            for a in range(groups):
                for m in range(span):
                    for j in range(per_rank):
                        h = (m * per_rank + j) * groups + a
                        at = w * channels + j * head
                        grad = landed[a * span + m, :, at : at + head].astype(F32)
                        cols = slice(h * head, (h + 1) * head)
                        total += jnp.sum(grad * ref[:, cols].astype(F32), axis=1, keepdims=True)
                        out[:, cols] = grad * scale
        gain_out[...] = total
        for copy, arrival in gaps:
            copy.wait_send()
            arrival.wait_recv()
        own_gap.wait()

    return pl.pallas_call(
        kernel,
        in_specs=[ANY_SPEC] + [VMEM_SPEC] * 4 + [ANY_SPEC] + [VMEM_SPEC] * 4,
        out_specs=[VMEM_SPEC] * 4 + [ANY_SPEC] + [VMEM_SPEC] * 3,
        out_shape=[jax.ShapeDtypeStruct((rows, model), F32)] * 3
        + [
            jax.ShapeDtypeStruct((rows, 1), F32),
            jax.ShapeDtypeStruct((planes, 2) + gap_grad.shape, gap_grad.dtype),
        ]
        + [jax.ShapeDtypeStruct(unit_weights[0].shape, F32)] * 2
        + [jax.ShapeDtypeStruct((rows, 1), F32)],
        scratch_shapes=[
            pltpu.VMEM((8, rows, 3 * channels), BF),
            pltpu.SemaphoreType.DMA((1, 7)),
            pltpu.SemaphoreType.DMA((1, 7)),
            pltpu.SemaphoreType.DMA((2,)),
            pltpu.SemaphoreType.DMA((2 * planes - 1,)),
            pltpu.SemaphoreType.DMA((2 * planes - 1,)),
        ],
        compiler_params=pltpu.CompilerParams(
            collective_id=collective_id, has_side_effects=True, vmem_limit_bytes=VMEM_LIMIT
        ),
        name="exit_plane",
    )(summed, *weights, gain, gap_grad, unit_rows, *unit_weights, unit_gain)


class Scatter:
    def __init__(self, left, weight, transposed, stats):
        self.rows, self.columns = left[2], left[3]
        self.transposed, self.stats = transposed, stats
        self.weight = weight
        self.depth = weight[1] if transposed else weight[0]
        self.width = weight[0] if transposed else weight[1]
        self.half = self.width // 2
        self.extra = EXTRA if stats else 0

    def scratch(self):
        rows, half, full = self.rows, self.half, self.width + self.extra
        right = half + self.extra
        return [
            pltpu.VMEM((PIECES, 8, rows, self.columns), BF),
            pltpu.VMEM(self.weight, BF),
            pltpu.VMEM((PIECES, 4, rows, full), BF),
            pltpu.VMEM((PIECES, 4, rows, full), BF),
            pltpu.VMEM((4, rows, full), F32),
            pltpu.VMEM((PIECES, 2, rows, half), BF),
            pltpu.VMEM((PIECES, 2, rows, half), BF),
            pltpu.VMEM((PIECES, 2, rows, right), BF),
            pltpu.VMEM((PIECES, 2, rows, right), BF),
            pltpu.VMEM((PIECES, 2, rows, half), F32),
            pltpu.VMEM((PIECES, 2, rows, right), F32),
            pltpu.VMEM((PIECES, rows, half), BF),
            pltpu.VMEM((PIECES, rows, half), BF),
            pltpu.VMEM((PIECES, rows, right), BF),
            pltpu.VMEM((PIECES, rows, right), BF),
            pltpu.SemaphoreType.DMA((PIECES,)),
            pltpu.SemaphoreType.DMA((1,)),
        ]

    def bind(self, place, sems, left_ref, weight_ref, refs):
        self.place, self.sems, self.left_ref, self.weight_ref = place, sems, left_ref, weight_ref
        (self.x_buf, self.w_buf, self.core_out, self.core_in, self.total, self.x_out, self.x_in, self.y_out, self.y_in,
         self.keep_a, self.keep_b, self.last_y_out, self.last_y_in, self.last_x_out,
         self.last_x_in, self.load_sem, self.w_sem) = refs

    def weight_copy(self):
        return pltpu.make_async_copy(self.weight_ref, self.w_buf, self.w_sem.at[0])

    def start_loads(self):
        core = self.place.core
        self.weight_copy().start()
        for b in range(PIECES):
            for j in range(4):
                for side, at in ((0, 2 * j + 1 - core), (4, 2 * j + core)):
                    pltpu.make_async_copy(
                        self.left_ref.at[at, b], self.x_buf.at[b, side + j], self.load_sem.at[b]
                    ).start()

    def send_core(self, b):
        return remote(self.core_out.at[b], self.core_in.at[b], self.sems, R_CORE, b, self.place.device(0, 0, 1))

    def send_x(self, b):
        return remote(self.x_out.at[b], self.x_in.at[b], self.sems, R_X, b, self.place.device(0, 1, 0))

    def send_y(self, b):
        return remote(self.y_out.at[b], self.y_in.at[b], self.sems, R_Y, b, self.place.device(1, 0, 0))

    def send_last_y(self, b):
        return remote(self.last_y_out.at[b], self.last_y_in.at[b], self.sems, R_LAST_Y, b, self.place.device(1, 0, 0))

    def send_last_x(self, b):
        return remote(self.last_x_out.at[b], self.last_x_in.at[b], self.sems, R_LAST_X, b, self.place.device(0, 1, 0))

    def produce(self, b):
        rows, depth, width, tile = self.rows, self.depth, self.width, 256
        pltpu.make_async_copy(self.x_buf.at[b], self.x_buf.at[b], self.load_sem.at[b]).wait()

        @pl.loop(0, width // tile)
        def _(t):
            at = pl.multiple_of(t * tile, tile)
            lhs = self.x_buf[b, :, :, :depth].reshape(8 * rows, depth)
            if self.transposed:
                out = nt(lhs, self.w_buf[pl.ds(at, tile), :])
            else:
                out = nn(lhs, self.w_buf[:, pl.ds(at, tile)])
            self.core_out[b, :, :, pl.ds(at, tile)] = out[: 4 * rows].astype(BF).reshape(4, rows, tile)
            self.total[:, :, pl.ds(at, tile)] = out[4 * rows :].reshape(4, rows, tile)

        if self.stats:
            self.core_out[b, :, :, width:] = self.x_buf[b, :4, :, depth:]
            self.total[:, :, width:] = self.x_buf[b, 4:, :, depth:].astype(F32)
        self.send_core(b).start()

    def stage_one(self, b):
        place, half, total, core_in = self.place, self.half, self.total, self.core_in
        self.send_core(b).wait_recv()
        for i in range(2):
            go, stay = 2 * i + 1 - place.x, 2 * i + place.x
            self.x_out[b, i] = (total[go, :, :half] + core_in[b, go, :, :half].astype(F32)).astype(BF)
            self.keep_a[b, i] = total[stay, :, :half] + core_in[b, stay, :, :half].astype(F32)
        self.send_x(b).start()
        for i in range(2):
            go, stay = 2 * (1 - place.y) + i, 2 * place.y + i
            self.y_out[b, i] = (total[go, :, half:] + core_in[b, go, :, half:].astype(F32)).astype(BF)
            self.keep_b[b, i] = total[stay, :, half:] + core_in[b, stay, :, half:].astype(F32)
        self.send_y(b).start()

    def stage_two(self, b):
        self.send_x(b).wait_recv()
        go = 1 - self.place.y
        self.last_y_out[b] = (self.keep_a[b, go] + self.x_in[b, go].astype(F32)).astype(BF)
        self.send_last_y(b).start()
        self.send_y(b).wait_recv()
        go = 1 - self.place.x
        self.last_x_out[b] = (self.keep_b[b, go] + self.y_in[b, go].astype(F32)).astype(BF)
        self.send_last_x(b).start()

    def stage_three(self, b):
        self.send_last_y(b).wait_recv()
        self.send_last_x(b).wait_recv()
        y, x = self.place.y, self.place.x
        low = self.keep_a[b, y] + self.x_in[b, y].astype(F32) + self.last_y_in[b].astype(F32)
        high = self.keep_b[b, x] + self.y_in[b, x].astype(F32) + self.last_x_in[b].astype(F32)
        result = jnp.concatenate([low, high[:, : self.half]], axis=1)
        return result, (high[:, self.half :] if self.stats else None)

    def drain(self, b):
        for copy in (self.send_core, self.send_x, self.send_y, self.send_last_y, self.send_last_x):
            copy(b).wait_send()


def guarded(body, b):
    @pl.when((b >= 0) & (b < PIECES))
    def _():
        body(b)


def plane_sems():
    return [pltpu.SemaphoreType.DMA((KINDS, PIECES)), pltpu.SemaphoreType.DMA((KINDS, PIECES))]


def product_scatter(left, weight, transposed, stats, epilogue, owned, outs, gathered, collective_id):
    tokens = left.shape[0] // 8
    rows = tokens // PIECES
    left = left.reshape(8, PIECES, rows, left.shape[1])
    scatter = Scatter(left.shape, weight.shape, transposed, stats)
    count = len(scatter.scratch())

    def kernel(*refs):
        refs = list(refs)
        left_ref, weight_ref = refs.pop(0), refs.pop(0)
        own_refs = [refs.pop(0) for _ in owned]
        out_refs = [refs.pop(0) for _ in outs]
        full_ref = refs.pop(0) if gathered else None
        place = Place()
        sems = (refs.pop(0), refs.pop(0))
        scatter.bind(place, sems, left_ref, weight_ref, refs[:count])
        scatter.start_loads()
        greet(place)
        if gathered:
            n_buf, keep_sem = refs[count:]
            gather = Gather(place, n_buf, full_ref, sems, keep_sem)

        def end(b):
            result, stat = scatter.stage_three(b)
            written, sent = epilogue(result, stat, *[r[b] for r in own_refs])
            for ref, value in zip(out_refs, written):
                ref[b] = value
            if gathered:
                n_buf[b] = sent
                gather.start(b)

        scatter.weight_copy().wait()

        @pl.loop(0, PIECES + (9 if gathered else 5))
        def _(step):
            guarded(scatter.stage_one, step - 1)
            guarded(scatter.produce, step)
            guarded(scatter.stage_two, step - 3)
            guarded(end, step - 5)
            if gathered:
                guarded(gather.forward, step - 7)
                guarded(gather.forward_last, step - 9)

        @pl.loop(0, PIECES)
        def _(b):
            if gathered:
                gather.finish(b)
                gather.drain(b)
            scatter.drain(b)

    any_spec, vmem = pl.BlockSpec(memory_space=pl.ANY), pl.BlockSpec(memory_space=pltpu.VMEM)
    out_shape = [jax.ShapeDtypeStruct((PIECES, rows, c), d) for c, d in outs]
    out_specs = [vmem] * len(outs)
    scratch = plane_sems() + scatter.scratch()
    if gathered:
        out_shape.append(jax.ShapeDtypeStruct((8, PIECES, rows, gathered), BF))
        out_specs.append(any_spec)
        scratch += [pltpu.VMEM((PIECES, rows, gathered), BF), pltpu.SemaphoreType.DMA((PIECES,))]
    results = pl.pallas_call(
        kernel,
        in_specs=[any_spec, any_spec] + [vmem] * len(owned),
        out_specs=out_specs,
        out_shape=out_shape,
        scratch_shapes=scratch,
        compiler_params=pltpu.CompilerParams(
            collective_id=collective_id, has_side_effects=True, vmem_limit_bytes=VMEM_LIMIT
        ),
        cost_estimate=pl.CostEstimate(
            flops=16 * tokens * scatter.depth * scatter.width,
            bytes_accessed=(240 if gathered else 140) * tokens * scatter.width * 2,
            transcendentals=0,
        ),
        name="product_scatter",
    )(left, weight, *[o.reshape(PIECES, rows, o.shape[1]) for o in owned])
    flat = [r.reshape(tokens, r.shape[2]) for r in results[: len(outs)]]
    if gathered:
        flat.append(results[-1].reshape(8 * tokens, gathered))
    return flat


def mixer_specs(tokens, heads, reverse):
    width, unroll = heads * 128, UNROLL if reverse else UNROLL_FORWARD
    span = unroll * BLOCK
    steps = tokens // span

    def at(i):
        return steps - 1 - i if reverse else i

    return (
        steps,
        pl.BlockSpec((span, 3 * width), lambda i, *_: (at(i), 0)),
        pl.BlockSpec((1, width), lambda i, *_: (0, 0)),
        pl.BlockSpec((unroll, heads, 128, 128), lambda i, *_: (at(i), 0, 0, 0)),
        lambda columns: pl.BlockSpec((span, columns), lambda i, *_: (at(i), 0)),
    )


def mixer_forward(cut, live, n1, weight, gap, own, out_pieces, per_rank, collective_id):
    tokens, heads = n1.shape[0], gap.shape[1] // 128
    width = heads * 128
    steps, qfi_spec, gap_spec, kept_spec, block = mixer_specs(tokens, heads, False)
    together = lax.axis_size("seq") == 8

    def kernel(cut_ref, live_ref, n_ref, w_ref, gap_ref, *refs):
        if not together:
            return mixer_forward_kernel(heads, cut_ref, live_ref, n_ref, w_ref, gap_ref, *refs)
        own_ref, pieces_ref, mixed_ref, kept_ref, qfi_ref, full_ref, rows_ref, state, send, recv, local, w_send, w_recv, w_local = refs
        place = Place()
        gather = Gather(place, own_ref, full_ref, (send, recv), local)

        def exchange(j):
            core = place.core
            here = pltpu.make_async_copy(
                pieces_ref.at[core * per_rank + j], rows_ref.at[j, core], w_local.at[j]
            )
            there = pltpu.make_async_remote_copy(
                src_ref=pieces_ref.at[(1 - core) * per_rank + j], dst_ref=rows_ref.at[j, core],
                send_sem=w_send.at[j], recv_sem=w_recv.at[j], device_id=place.device(0, 0, 1), device_id_type=MESH,
            )
            back = rows_ref.at[j, 1 - core]
            arrival = pltpu.make_async_remote_copy(
                src_ref=back, dst_ref=back, send_sem=w_send.at[j], recv_sem=w_recv.at[j],
                device_id=place.device(0, 0, 1), device_id_type=MESH,
            )
            return here, there, arrival

        @pl.when(pl.program_id(0) == 0)
        def _():
            greet(place)
            pl.loop(0, PIECES)(gather.start)
            for j in range(per_rank):
                here, there, _ = exchange(j)
                here.start()
                there.start()

        mixer_forward_kernel(
            heads, cut_ref, live_ref, n_ref, w_ref, gap_ref, mixed_ref, kept_ref, qfi_ref, state
        )

        @pl.when(pl.program_id(0) == steps - 1)
        def _():
            for stage in (gather.forward, gather.forward_last, gather.finish, gather.drain):
                pl.loop(0, PIECES)(stage)
            for j in range(per_rank):
                here, there, arrival = exchange(j)
                here.wait()
                there.wait_send()
                arrival.wait_recv()

    fixed = pl.BlockSpec(weight.shape, lambda i, *_: (0, 0), pipeline_mode=pl.Buffered(1))
    in_specs, args = [block(n1.shape[1]), fixed, gap_spec], [n1, weight, gap]
    out_specs = [block(width + EXTRA), kept_spec, qfi_spec]
    out_shape = [
        jax.ShapeDtypeStruct((tokens, width + EXTRA), BF),
        jax.ShapeDtypeStruct((tokens // BLOCK, heads, 128, 128), BF),
        jax.ShapeDtypeStruct((tokens, 3 * width), F32),
    ]
    scratch = [pltpu.VMEM((heads, 128, 128), F32)]
    params = pltpu.CompilerParams(vmem_limit_bytes=VMEM_LIMIT)
    if together:
        rows = own.shape[0] // PIECES
        own = own.reshape(PIECES, rows, own.shape[1])
        w_rows, model = out_pieces.shape[1:]
        in_specs, args = in_specs + [ANY_SPEC] * 2, args + [own, out_pieces]
        out_specs = out_specs + [ANY_SPEC] * 2
        out_shape = out_shape + [
            jax.ShapeDtypeStruct((8,) + own.shape, own.dtype),
            jax.ShapeDtypeStruct((per_rank, 2, w_rows, model), BF),
        ]
        scratch = scratch + plane_sems() + [pltpu.SemaphoreType.DMA((PIECES,))]
        scratch = scratch + [pltpu.SemaphoreType.DMA((per_rank,))] * 3
        params = pltpu.CompilerParams(
            vmem_limit_bytes=VMEM_LIMIT, collective_id=collective_id, has_side_effects=True
        )
    results = pl.pallas_call(
        kernel,
        grid_spec=pltpu.PrefetchScalarGridSpec(
            num_scalar_prefetch=2, grid=(steps,), in_specs=in_specs, out_specs=out_specs, scratch_shapes=scratch
        ),
        out_shape=out_shape,
        compiler_params=params,
        cost_estimate=pl.CostEstimate(
            flops=tokens * width * (128 * 10 + 6 * n1.shape[1]),
            bytes_accessed=60 * tokens * n1.shape[1],
            transcendentals=tokens * width * 6,
        ),
        name="mixer_forward",
    )(cut, live, *args)
    mixed, kept, qfi = results[:3]
    if together:
        return mixed, kept, qfi, results[3].reshape(tokens, own.shape[2]), results[4].reshape(width, model)
    return mixed, kept, qfi, lax.all_gather(own, "seq", axis=0, tiled=True), None


def mixer_backward(cut, live, qfi, gap, kept, grad, left, weight, epilogue, owned, collective_id):
    tokens, heads = qfi.shape[0], gap.shape[1] // 128
    width = heads * 128
    steps, qfi_spec, gap_spec, kept_spec, block = mixer_specs(tokens, heads, True)
    together = lax.axis_size("seq") == 8
    in_specs = [qfi_spec, gap_spec, kept_spec, block(width)]
    out_specs = [block(3 * width), gap_spec]
    out_shape = [jax.ShapeDtypeStruct((tokens, 3 * width), BF), jax.ShapeDtypeStruct((1, width), F32)]
    scratch = [pltpu.VMEM((heads, 128, 128), F32)]
    args = [qfi, gap, kept, grad]
    params = pltpu.CompilerParams(vmem_limit_bytes=VMEM_LIMIT)
    if together:
        rows = tokens // 8 // PIECES
        left = left.reshape(8, PIECES, rows, left.shape[1])
        scatter = Scatter(left.shape, weight.shape, False, False)
        model = weight.shape[1]
        stride = max(1, (steps - 2) // PIECES)
        any_spec = pl.BlockSpec(memory_space=pl.ANY)
        whole = pl.BlockSpec((PIECES, rows, model), lambda i, *_: (0, 0, 0), pipeline_mode=pl.Buffered(1))
        in_specs = in_specs + [any_spec, any_spec, whole]
        args = args + [left, weight, owned.reshape(PIECES, rows, model)]
        out_specs = out_specs + [whole]
        out_shape = out_shape + [jax.ShapeDtypeStruct((PIECES, rows, model), BF)]
        scratch = scratch + plane_sems() + scatter.scratch()
        params = pltpu.CompilerParams(
            vmem_limit_bytes=VMEM_LIMIT, collective_id=collective_id, has_side_effects=True
        )

    def kernel(cut_ref, live_ref, qfi_ref, gap_ref, kept_ref, grad_ref, *refs):
        if not together:
            out_ref, gap_out_ref, state = refs
            mixer_backward_kernel(
                heads, cut_ref, live_ref, qfi_ref, gap_ref, kept_ref, grad_ref, out_ref, gap_out_ref, state
            )
            return
        left_ref, weight_ref, owned_ref, out_ref, gap_out_ref, sum_ref, state, send, recv = refs[:9]
        place, step = Place(), pl.program_id(0)
        scatter.bind(place, (send, recv), left_ref, weight_ref, refs[9:])

        @pl.when(step == 0)
        def _():
            scatter.start_loads()
            greet(place)
            scatter.weight_copy().wait()

        def end(b):
            result, _ = scatter.stage_three(b)
            sum_ref[b] = epilogue(result, None, owned_ref[b])[0][0]

        def phases(at):
            for body, first in ((scatter.stage_one, 2), (scatter.produce, 0), (scatter.stage_two, 8), (end, 12)):
                @pl.when((at >= first) & (lax.rem(at - first, stride) == 0) & (at < first + stride * PIECES))
                def _():
                    body((at - first) // stride)

        phases(step)
        mixer_backward_kernel(
            heads, cut_ref, live_ref, qfi_ref, gap_ref, kept_ref, grad_ref, out_ref, gap_out_ref, state
        )

        @pl.when(step == steps - 1)
        def _():
            @pl.loop(steps, stride * (PIECES - 1) + 13)
            def _(late):
                phases(late)

            pl.loop(0, PIECES)(scatter.drain)

    results = pl.pallas_call(
        kernel,
        grid_spec=pltpu.PrefetchScalarGridSpec(
            num_scalar_prefetch=2, grid=(steps,), in_specs=in_specs, out_specs=out_specs, scratch_shapes=scratch
        ),
        out_shape=out_shape,
        compiler_params=params,
        cost_estimate=pl.CostEstimate(
            flops=tokens * width * 128 * 24, bytes_accessed=tokens * width * 28, transcendentals=tokens * width * 6
        ),
        name="mixer_backward",
    )(cut, live, *args)
    if together:
        return results[0], results[1], results[2].reshape(tokens // 8, model)
    (summed,) = product_all(left, weight, False, False, epilogue, [owned], [(weight.shape[1], BF)], 0, collective_id)
    return results[0], results[1], summed


def feed_forward_kernel(units, n_ref, g_ref, gu_ref, down_ref, units_ref, grad_ref, gate_w, up_w):
    @pl.when(pl.program_id(0) == 0)
    def _():
        gate_w[...] = gu_ref[:, :units]
        up_w[...] = gu_ref[:, units:]

    n = n_ref[...]
    gate, up = nn(n, gate_w[...]), nn(n, up_w[...])
    d_units = nt(g_ref[...], down_ref[...])
    sig = jax.nn.sigmoid(gate)
    act = gate * sig
    units_ref[...] = (act * up).astype(BF)
    grad_ref[:, :units] = (d_units * up * sig * (1.0 + gate * (1.0 - sig))).astype(BF)
    grad_ref[:, units:] = (d_units * act).astype(BF)


def feed_forward(n2, grad, gu, down):
    tokens, model = n2.shape
    units = down.shape[0]
    span = 512
    fixed = lambda shape: pl.BlockSpec(shape, lambda i: (0, 0), pipeline_mode=pl.Buffered(1))
    block = lambda columns: pl.BlockSpec((span, columns), lambda i: (i, 0))
    return pl.pallas_call(
        functools.partial(feed_forward_kernel, units),
        grid=(tokens // span,),
        in_specs=[block(model), block(model), fixed(gu.shape), fixed(down.shape)],
        out_specs=[block(units), block(2 * units)],
        out_shape=[jax.ShapeDtypeStruct((tokens, units), BF), jax.ShapeDtypeStruct((tokens, 2 * units), BF)],
        scratch_shapes=[pltpu.VMEM((model, units), BF), pltpu.VMEM((model, units), BF)],
        compiler_params=pltpu.CompilerParams(vmem_limit_bytes=VMEM_LIMIT),
        cost_estimate=pl.CostEstimate(
            flops=6 * tokens * model * units, bytes_accessed=4 * tokens * model, transcendentals=tokens * units
        ),
        name="feed_forward",
    )(n2, grad, gu, down)


def gather_dp(v):
    return lax.all_gather(v, "dp", axis=0, tiled=True)


def scatter_dp(v):
    return lax.psum_scatter(v, "dp", scatter_dimension=0, tiled=True)


def swap_seq(v):
    return lax.all_to_all(v, "seq", split_axis=0, concat_axis=0, tiled=True)


def product_all(left, weight, transposed, stats, epilogue, owned, outs, gathered, collective_id):
    if lax.axis_size("seq") == 8:
        return product_scatter(left, weight, transposed, stats, epilogue, owned, outs, gathered, collective_id)
    depth = left.shape[1] - (EXTRA if stats else 0)
    product = (nt if transposed else nn)(left[:, :depth], weight).astype(BF)
    result = lax.psum_scatter(product, "seq", scatter_dimension=0, tiled=True).astype(F32)
    stat = None
    if stats:
        stat = lax.psum_scatter(left[:, depth:].astype(F32), "seq", scatter_dimension=0, tiled=True)
    written, sent = epilogue(result, stat, *owned)
    written = [w.astype(d) for w, (_, d) in zip(written, outs)]
    return written + ([lax.all_gather(sent, "seq", axis=0, tiled=True)] if gathered else [])


def split_lanes(v):
    lane = lax.broadcasted_iota(jnp.int32, (v.shape[0], EXTRA), 1)
    high = v.astype(BF).astype(F32)
    return jnp.where(lane == 0, high, jnp.where(lane == 1, v - high, 0.0)).astype(BF)


def on_device(
    hidden,
    seg_ids,
    pad_mask,
    attn_gain,
    gate_gap,
    out_gain,
    w_query,
    w_forget,
    w_input,
    w_output,
    ffn_gain,
    w_gate,
    w_up,
    w_down,
    out_grad,
):
    planes, ranks = lax.axis_size("dp"), lax.axis_size("seq")
    row_tokens, model = hidden.shape[1:]
    rows = w_query.shape[0]
    units_in = w_down.shape[0]
    head = model // HEADS
    span = head // rows
    per_rank, groups = planes // span, ranks // span
    channels = per_rank * head
    units = planes * units_in
    tokens = ranks * row_tokens
    members = [[a * span + m for m in range(span)] for a in range(groups)]

    def to_heads(w):
        parts = w.reshape(rows, span, per_rank, groups, head)
        return parts.transpose(3, 1, 0, 2, 4).reshape(ranks, rows, channels)

    def from_heads(parts):
        parts = parts.reshape(groups, span, rows, per_rank, head)
        return parts.transpose(2, 1, 3, 0, 4).reshape(rows, model)

    def to_units(w):
        parts = w.reshape(rows, planes, ranks, units_in)
        return parts.transpose(2, 0, 1, 3).reshape(ranks, rows, units)

    def from_units(parts):
        parts = parts.reshape(ranks, rows, planes, units_in)
        return parts.transpose(1, 2, 0, 3).reshape(rows, planes * ranks * units_in)

    def own_rows(v):
        return v.reshape((span, per_rank) + v.shape[1:])

    def swap_group(v):
        return lax.all_to_all(v, "seq", split_axis=0, concat_axis=0, axis_index_groups=members)

    gain_a, gain_o, gain_f = (g.astype(F32)[:, None] for g in (attn_gain, out_gain, ffn_gain))

    plain = ranks != 8

    def order(first, *rest):
        return lax.optimization_barrier((first,) + rest)

    x16 = hidden[0]
    ids = jnp.concatenate([seg_ids, pad_mask], axis=0)
    mixer_weights = (w_query, w_forget, w_input)
    out_pieces = lax.all_gather(fold(gain_o, w_output), "dp", axis=0)
    if plain:
        qfi_part = jnp.concatenate([to_heads(fold(gain_a, w)) for w in mixer_weights], axis=2)
        qfi_swapped = swap_seq(qfi_part)
        gu_part = jnp.concatenate([to_units(fold(gain_f, w)) for w in (w_gate, w_up)], axis=2)
        gu_swapped = swap_seq(gu_part)
        x = x16.astype(F32)
        normed = (x * inverse_rms(row_mean(x * x))).astype(BF)
        n1 = lax.all_gather(normed, "seq", axis=0, tiled=True)
        gap_pieces = lax.all_gather(gate_gap, "dp", axis=0)
        gap_own = swap_group(own_rows(gap_pieces)).transpose(1, 0, 2)
        ids = lax.all_gather(ids, "seq", axis=0)
    else:
        wide = -(-row_tokens // 128) * 128
        ids = jnp.pad(ids, ((0, 6), (0, wide - row_tokens)))
        gap_tile = jnp.pad(gate_gap[None], ((0, 15), (0, 128 - rows)))
        qfi_swapped, ids, gap_all = enter_plane(
            mixer_weights, gain_a, ids, gap_tile, per_rank, groups, planes, 1
        )
        ids = ids[:, :2, :row_tokens]
        mine = lax.rem(lax.axis_index("seq"), 2) * per_rank
        gap_own = lax.dynamic_slice_in_dim(gap_all[:, :, 0, :rows], mine, per_rank, axis=0)
        x16, qfi_swapped = order(x16, qfi_swapped)
        n1, gu_swapped = gather_plane(x16, w_gate, w_up, gain_f, planes, 2)
    qfi_full = gather_dp(qfi_swapped.reshape(ranks * rows, 3 * channels))
    gu_full = gather_dp(gu_swapped.reshape(ranks * rows, 2 * units))
    down_own = gather_dp(w_down)
    gap_own = gap_own.reshape(1, channels).astype(F32)
    segment = ids[:, 0].reshape(tokens // BLOCK, BLOCK)
    live = jnp.sum(ids[:, 1]).reshape(1)
    ends = segment[:, -1]
    before = jnp.concatenate([segment[:1, 0], ends[:-1]])
    cut = jnp.sum((segment == before[:, None]).astype(jnp.int32), axis=1)

    og16 = out_grad[0]
    mixed, kept, qfi, grad_all, out_own = mixer_forward(
        cut, live, n1, qfi_full, gap_own, og16, out_pieces, per_rank, 3
    )
    if plain:
        out_own = swap_group(own_rows(out_pieces)).transpose(1, 0, 2, 3).reshape(channels, model)

    def after_output(result, stat, x16):
        x = x16.astype(F32)
        factor_o = inverse_rms(jnp.sum(stat, axis=1, keepdims=True) / model)
        middle = x + factor_o * result
        normed = middle * inverse_rms(row_mean(middle * middle))
        return [middle, jnp.broadcast_to(factor_o, (x.shape[0], EXTRA))], normed.astype(BF)

    middle, factor_o, n2 = product_all(
        mixed, out_own, False, True, after_output, [x16], [(model, F32), (EXTRA, F32)], model, 4
    )
    hidden_units, d_gu = feed_forward(n2, grad_all, gu_full, down_own)
    grad_down = tn(hidden_units, grad_all).astype(BF)
    down_sum = scatter_dp(grad_down)
    n2, _ = order(n2, grad_down)
    grad_gu = tn(n2, d_gu).astype(BF)
    gu_sum = scatter_dp(grad_gu)
    d_gu, _ = order(d_gu, grad_gu)

    def after_ffn(result, stat, middle, og16, x16, factor_o):
        factor_o = factor_o[:, :1]
        factor_m = inverse_rms(row_mean(middle * middle))
        normed = middle * factor_m
        d_middle = og16.astype(F32) + factor_m * (result - normed * row_mean(result * normed))
        mean_o = row_mean(d_middle * (middle - x16.astype(F32)))
        beta = split_lanes(factor_o * factor_o * mean_o)
        return [d_middle], jnp.concatenate([(factor_o * d_middle).astype(BF), beta], axis=1)

    d_middle, d_attn = product_all(
        d_gu, gu_full, True, False, after_ffn, [middle, og16, x16, factor_o], [(model, F32)], model + EXTRA, 5
    )
    d_attn, down_sum = order(d_attn, down_sum)
    beta = jnp.sum(d_attn[:, model:].astype(F32), axis=1, keepdims=True)
    d_attn = d_attn[:, :model]

    def after_down(result, stat, middle):
        return [(middle + result).astype(BF)], None

    mixed = mixed[:, :channels]
    grad_out = tn(mixed, d_attn).astype(BF)
    d_mixed = (nt(d_attn, out_own) - beta * mixed.astype(F32)).astype(BF)
    grad_out, d_mixed = order(grad_out, d_mixed)
    out_back = grad_out.reshape(per_rank, span, rows, model).transpose(1, 0, 2, 3)
    out_sum = scatter_dp(swap_group(out_back).reshape(planes * rows, model))
    d_qfi, gap_grad, block_out = mixer_backward(
        cut, live, qfi, gap_own, kept, d_mixed, hidden_units, down_own, after_down, middle, 6
    )
    grad_qfi = tn(n1, d_qfi).astype(BF)
    grad_qfi, d_qfi, gu_sum = order(grad_qfi, d_qfi, gu_sum)
    qfi_sum = scatter_dp(grad_qfi)
    gu_rows = swap_seq(gu_sum).reshape(ranks, rows, 2 * units)

    def after_mixer(result, stat, x16, d_middle):
        x = x16.astype(F32)
        factor_x = inverse_rms(row_mean(x * x))
        normed = x * factor_x
        return [(d_middle + factor_x * (result - normed * row_mean(result * normed))).astype(BF)], None

    (hidden_grad,) = product_all(d_qfi, qfi_full, True, False, after_mixer, [x16, d_middle], [(model, BF)], 0, 7)

    hidden_grad, qfi_sum, gap_grad = order(hidden_grad, qfi_sum, gap_grad)

    def rowdot(w, g):
        return jnp.sum(w.astype(F32) * g, axis=1)

    out_rows = out_sum.astype(F32)
    g_out_gain = rowdot(w_output, out_rows)
    if plain:
        gu_rows = gu_rows.astype(F32)
        gate_rows, up_rows = from_units(gu_rows[:, :, :units]), from_units(gu_rows[:, :, units:])
        g_ffn_gain = rowdot(w_gate, gate_rows) + rowdot(w_up, up_rows)
        g_gate, g_up = gain_f * gate_rows, gain_f * up_rows
        gap_back = swap_group(gap_grad.reshape(per_rank, span, rows).transpose(1, 0, 2)).reshape(planes * rows)
        g_gap = scatter_dp(gap_back)
        qfi_rows = swap_seq(qfi_sum).reshape(ranks, rows, 3 * channels).astype(F32)
        parts = [from_heads(qfi_rows[:, :, j * channels : (j + 1) * channels]) for j in range(3)]
        g_attn_gain = sum(rowdot(w, g) for w, g in zip(mixer_weights, parts))
        g_query, g_forget, g_input = [gain_a * g for g in parts]
    else:
        gap_tile = jnp.broadcast_to(gap_grad, (8, channels))
        g_query, g_forget, g_input, g_attn_gain, gap_all, g_gate, g_up, g_ffn_gain = exit_plane(
            qfi_sum.reshape(ranks, rows, 3 * channels), mixer_weights, gain_a, gap_tile,
            gu_rows, (w_gate, w_up), gain_f, per_rank, groups, planes, 8,
        )
        g_attn_gain, g_ffn_gain = g_attn_gain[:, 0], g_ffn_gain[:, 0]
        plane, me = lax.axis_index("dp"), lax.axis_index("seq")
        at = lax.rem(plane, per_rank) * head + lax.rem(me, 2) * rows
        from_core = jnp.sum(gap_all[:, :, 0], axis=0)
        g_gap = lax.dynamic_slice(from_core, (plane // per_rank, at), (1, rows))[0]
    return (
        block_out[None],
        hidden_grad[None],
        g_attn_gain,
        g_gap,
        g_out_gain,
        g_query,
        g_forget,
        g_input,
        gain_o * out_rows,
        g_ffn_gain,
        g_gate,
        g_up,
        down_sum.astype(F32),
    )


def solution(mesh):
    tok, row, both = P("dp", "seq", None), P("dp", "seq"), P(("dp", "seq"))
    mat = P(("dp", "seq"), None)
    return jax.shard_map(
        on_device,
        mesh=mesh,
        in_specs=(tok, row, row, both, both, both, mat, mat, mat, mat, both, mat, mat, mat, tok),
        out_specs=(tok, tok, both, both, both, mat, mat, mat, mat, both, mat, mat, mat),
        check_vma=False,
    )
```

time: 920 us -> 662 us (0.72)
  waiting for transfers between devices: 93.8 us -> 0.89 us
  matrix products: 120 us -> 59.7 us
  blocking collectives: 63.4 us -> 5.36 us
  local copies, waits for them, and re-layouts: 59.4 us -> 15.5 us
  Pallas kernels: 517 us -> 540 us
  other arithmetic: 33.4 us -> 16.5 us
    reduce_scatter x4, waiting for transfers between devices: 93.1 us -> 0.05 us  [scatter_dp(): return lax.psum_scatter(v, 'dp', scatter_dimension=0, tiled=True)]
    pallas_call x5 -> x6, Pallas kernels: 177 us -> 265 us  [the longest x1 65.5 us: gather_plane(): pl.pallas_call(kernel, in_specs=[VMEM_SPEC] * 4, out_specs=[ANY_SPEC] * 2...]
    pallas_call x4 -> x3, Pallas kernels: 340 us -> 275 us  [product_scatter(): pl.pallas_call(kernel, in_specs=[any_spec, any_spec] + [vmem] * len(owned...]
    dot_general x8 -> x5, matrix products: 120 us -> 59.7 us  [dot(): return lax.dot_general(a, b, (dims, ((), ())), preferred_element_type=F32)]
    reshape x34 -> x0, local copies, waits for them, and re-layouts: 30.5 us -> none  [the longest x4 11.1 us: from_units(): parts = parts.reshape(ranks, rows, planes, units_in)]
    unnamed x2 -> x0, blocking collectives: 23 us -> none
    all_to_all x1 -> x0, blocking collectives: 16.2 us -> none  [swap_seq(): return lax.all_to_all(v, 'seq', split_axis=0, concat_axis=0, tiled=True)]
    concatenate x1 -> x0, local copies, waits for them, and re-layouts: 10 us -> none  [on_device(): d_gu = jnp.concatenate([d_gate, d_up], axis=1)]
  transfers between devices with their start and end apart: 10 -> 9, of which waited for: 2 -> 0; matrix products, arithmetic and copies ran while one was open for 14% -> 10% of each run, Pallas kernels for 42% -> 74%
where the time goes in v3:
time: 662 us; the launch traced here: 658 us
  Pallas kernels  540 us (82%)
  matrix products  59.7 us (9%)
  other arithmetic  16.5 us (2%)
  local copies, waits for them, and re-layouts  15.5 us (2%)
  between operations  14.7 us (2%)
    pallas_call x3, Pallas kernels, product_scatter(): pl.pallas_call(kernel, in_specs=[any_spec, any_spec] + [vmem] * len(owned...  275 us
    pallas_call x1, Pallas kernels, gather_plane(): pl.pallas_call(kernel, in_specs=[VMEM_SPEC] * 4, out_specs=[ANY_SPEC] * 2...  65.5 us
    pallas_call x1, Pallas kernels, mixer_backward(): pl.pallas_call(kernel, grid_spec=pltpu.PrefetchScalarGridSpec(num_scalar_...  64.5 us
    pallas_call x1, Pallas kernels, mixer_forward(): pl.pallas_call(kernel, grid_spec=pltpu.PrefetchScalarGridSpec(num_scalar_...  64 us
    dot_general x5, matrix products, dot(): return lax.dot_general(a, b, (dims, ((), ())), preferred_element_type=F32)  59.7 us
    pallas_call x1, Pallas kernels, feed_forward(): pl.pallas_call(functools.partial(feed_forward_kernel, units), grid=(token...  34.2 us
    pallas_call x1, Pallas kernels, enter_plane(): pl.pallas_call(kernel, in_specs=[VMEM_SPEC] * 4 + [ANY_SPEC] * 2, out_spe...  19.7 us
    pallas_call x1, Pallas kernels, exit_plane(): pl.pallas_call(kernel, in_specs=[ANY_SPEC] + [VMEM_SPEC] * 4 + [ANY_SPEC]...  17.1 us
  transfers between devices with their start and end apart: 9, of which 0 were waited for; matrix products, arithmetic and copies ran while one was open for 10% of the time, Pallas kernels for 74%

profile of v3, /device:TPU:0, one launch (start us, length us, event | category | flops | bytes accessed | tf_op | source)
XLA Modules:
  0.0 658.3 jit_solution(2453044975897137256)
XLA Ops:
  7.9 1.8 fusion.14
  13.7 19.7 %enter_plane.1 = (bf16[8,64,768]{2,1,0:T(8,128)(2,1)}, s32[8,8,384]{2,1,0:T(8,128)}, bf16[4,2,16,128]{3,2,1,0:T(8,128)(2,1)}) custom-call(bf16[64,2048]{1,0:T(8,128)(2,1)} %q_ref.3, bf16[64,2048]{1,0:T(8,128)(2,1)} %f_ref.3, bf16[64,2048]{1,0:T(8,128)(2,1)} %i_ref.3, f32[64,1]{1,0:T(8,128)} %copy.40.gain_ref, s32[8,384]{1,0:T(8,128)} %pad.8.ids_ref, ...), custom_call_target="tpu_custom_call" | custom-call | tf_op jit(solution)/shard_map/enter_plane/pallas_call | solution.py:434
  35.6 65.5 %gather_plane.1 = (bf16[8,5,64,2048]{3,2,1,0:T(8,128)(2,1)}, bf16[8,64,1408]{2,1,0:T(8,128)(2,1)}) custom-call(bf16[5,64,2048]{2,1,0:T(8,128)(2,1)} %bitcast.50, bf16[64,5632]{1,0:T(8,128)(2,1)} %gate_ref.3, bf16[64,5632]{1,0:T(8,128)(2,1)} %up_ref.3, f32[64,1]{1,0:T(8,128)} %copy.42.gain_ref.unit_gain_ref), custom_call_target="tpu_custom_call" | custom-call | tf_op jit(solution)/shard_map/gather_plane/pallas_call | solution.py:491
  101.7 1.6 slice_reduce_fusion
  106.9 64.0 %mixer_forward.1 = (bf16[2560,384]{1,0:T(8,128)(2,1)}, bf16[40,2,128,128]{3,2,1,0:T(8,128)(2,1)}, f32[2560,768]{1,0:T(8,128)}, bf16[8,5,64,2048]{3,2,1,0:T(8,128)(2,1)}, bf16[2,2,64,2048]{3,2,1,0:T(8,128)(2,1)}) custom-call(s32[40]{0:T(128)} %convert_reduce_fusion.1.cut_ref, s32[1]{0:T(128)} %bitcast.4.live_ref, bf16[2560,2048]{1,0:T(8,128)(2,1)} %bitcast.67, ...), custom_call_target="tpu_custom_call" | custom-call | flops 8891924480 | bytes 314572800 | tf_op jit(solution)/shard_map/mixer_forward/pallas_call | solution.py:903
  170.9 102.1 %product_scatter.3 = (f32[5,64,2048]{2,1,0:T(8,128)}, f32[5,64,128]{2,1,0:T(8,128)}, bf16[8,5,64,2048]{3,2,1,0:T(8,128)(2,1)}) custom-call(bf16[8,5,64,384]{3,2,1,0:T(8,128)(2,1)} %bitcast.78, bf16[256,2048]{1,0:T(8,128)(2,1)} %bitcast.79, bf16[5,64,2048]{2,1,0:T(8,128)(2,1)} %bitcast.51), custom_call_target="tpu_custom_call" | custom-call | flops 2684354560 | bytes 314572800 | tf_op jit(solution)/shard_map/product_scatter/pallas_call | solution.py:787
  273.1 34.2 %feed_forward.1 = (bf16[2560,704]{1,0:T(8,128)(2,1)}, bf16[2560,1408]{1,0:T(8,128)(2,1)}) custom-call(bf16[2560,2048]{1,0:T(8,128)(2,1)} %bitcast.73, bf16[2560,2048]{1,0:T(8,128)(2,1)} %bitcast.75, bf16[2048,1408]{1,0:T(8,128)(2,1)} %all-gather.8.cloned.1.call-done.gu_ref.refs_1_, bf16[704,2048]{1,0:T(8,128)(2,1)} %all-gather.10.cloned.1.call-done.down_ref.refs_1_), custom_call_target="tpu_custom_call" | custom-call | flops 22145925120 | bytes 20971520 | tf_op jit(solution)/shard_map/feed_forward/pallas_call | solution.py:1031
  307.3 12.7 %convolution_convert_fusion.2 = bf16[704,2048]{1,0:T(8,128)(2,1)} fusion(bf16[2560,704]{1,0:T(8,128)(2,1)} %get-tuple-element.69, bf16[2560,2048]{1,0:T(8,128)(2,1)} %bitcast.76), kind=kOutput, calls=%fused_computation.8 | convolution fusion | flops 7383416832 | bytes 16973824 | tf_op jit(solution)/shard_map/dot_general | solution.py:21
  320.2 22.2 %convolution_convert_fusion = bf16[2048,1408]{1,0:T(8,128)(2,1)} fusion(bf16[2560,2048]{1,0:T(8,128)(2,1)} %bitcast.74, bf16[2560,1408]{1,0:T(8,128)(2,1)} %get-tuple-element.71), kind=kOutput, calls=%fused_computation.4 | convolution fusion | flops 14766833664 | bytes 23461888 | tf_op jit(solution)/shard_map/dot_general | solution.py:21
  342.5 112.6 %product_scatter.4 = (f32[5,64,2048]{2,1,0:T(8,128)}, bf16[8,5,64,2176]{3,2,1,0:T(8,128)(2,1)}) custom-call(bf16[8,5,64,1408]{3,2,1,0:T(8,128)(2,1)} %bitcast.77, bf16[2048,1408]{1,0:T(8,128)(2,1)} %all-gather.8.cloned.1.call-done.gu_ref.refs_1_, f32[5,64,2048]{2,1,0:T(8,128)} %get-tuple-element.72.refs_2_, bf16[5,64,2048]{2,1,0:T(8,128)(2,1)} %bitcast.71, ...), custom_call_target="tpu_custom_call" | custom-call | flops 14763950080 | bytes 314572800 | tf_op jit(solution)/shard_map/product_scatter/pallas_call | solution.py:787
  455.2 1.5 convert_reduce_fusion
  456.8 7.0 %fusion.10 = bf16[256,2048]{1,0:T(8,128)(2,1)S(1)} fusion(bf16[2560,2176]{1,0:T(8,128)(2,1)} %bitcast.60, bf16[2560,384]{1,0:T(8,128)(2,1)S(1)} %copy-done.10), kind=kOutput, calls=%fused_computation.9 | convolution fusion | flops 2684878848 | bytes 12845056 | tf_op jit(solution)/shard_map/dot_general | solution.py:21
  463.8 4.3 fusion.7.grad_ref
  468.2 5.4 all_to_all.14
  473.8 64.5 %mixer_backward.1 = (bf16[2560,768]{1,0:T(8,128)(2,1)}, f32[1,256]{1,0:T(1,128)}, bf16[5,64,2048]{2,1,0:T(8,128)(2,1)}) custom-call(s32[40]{0:T(128)} %convert_reduce_fusion.1.cut_ref, s32[1]{0:T(128)} %bitcast.4.live_ref, f32[2560,768]{1,0:T(8,128)} %get-tuple-element.61.qfi_ref, f32[1,256]{1,0:T(1,128)} %reshape.124.gap_ref, ...), custom_call_target="tpu_custom_call" | custom-call | flops 2013265920 | bytes 18350080 | tf_op jit(solution)/shard_map/mixer_backward/pallas_call | solution.py:991
  538.3 13.5 %convolution_convert_fusion.1 = bf16[2048,768]{1,0:T(8,128)(2,1)} fusion(bf16[2560,2048]{1,0:T(8,128)(2,1)} %bitcast.68, bf16[2560,768]{1,0:T(8,128)(2,1)} %get-tuple-element.79), kind=kOutput, calls=%fused_computation.7 | convolution fusion | flops 8054636544 | bytes 17563648 | tf_op jit(solution)/shard_map/dot_general | solution.py:21
  551.9 4.0 all-to-all-start
  555.9 1.3 convert_element_type.63
  557.2 2.5 convert_multiply_fusion
  559.7 60.6 %product_scatter.5 = bf16[5,64,2048]{2,1,0:T(8,128)(2,1)} custom-call(bf16[8,5,64,768]{3,2,1,0:T(8,128)(2,1)} %bitcast.69, bf16[2048,768]{1,0:T(8,128)(2,1)} %all-gather.6.cloned.1.call-done.w_ref.refs_1_, bf16[5,64,2048]{2,1,0:T(8,128)(2,1)} %bitcast.53, f32[5,64,2048]{2,1,0:T(8,128)} %get-tuple-element.80.refs_3_), custom_call_target="tpu_custom_call" | custom-call | flops 8053063680 | bytes 183500800 | tf_op jit(solution)/shard_map/product_scatter/pallas_call | solution.py:787
  621.4 17.1 %exit_plane.1 = (f32[64,2048]{1,0:T(8,128)}, f32[64,2048]{1,0:T(8,128)}, f32[64,2048]{1,0:T(8,128)}, f32[64,1]{1,0:T(8,128)}, f32[4,2,8,256]{3,2,1,0:T(8,128)}, ...) custom-call(bf16[8,64,768]{2,1,0:T(8,128)(2,1)} %bitcast.58, bf16[64,2048]{1,0:T(8,128)(2,1)} %q_ref.3, ...), custom_call_target="tpu_custom_call" | custom-call | tf_op jit(solution)/shard_map/exit_plane/pallas_call | solution.py:568
  638.6 1.5 reduce.4
  640.1 1.4 reduce.5
  644.0 2.6 copy.57
  (83 shorter events, 20.0 us)
Async XLA Ops:
  7.2 99.7 %all-gather.12.cloned.1.call-start = ((), (), s32[]{:S(2)}) async-start(), calls=%async_computation.13 | async-start | bytes 1310720 | tf_op jit(solution)/shard_map/all_gather | solution.py:1139
  9.7 97.2 %all-gather.6.cloned.1.call-start = ((), (), s32[]{:S(2)}) async-start(), calls=%async_computation.6 | async-start | bytes 3932160 | tf_op jit(solution)/shard_map/all_gather | solution.py:1047
  33.4 239.6 %all-gather.10.cloned.1.call-start = ((), (), s32[]{:S(2)}) async-start(), calls=%async_computation.8 | async-start | bytes 3604480 | tf_op jit(solution)/shard_map/all_gather | solution.py:1047
  34.2 238.9 %all-gather.8.cloned.1.call-start = ((), (), s32[]{:S(2)}) async-start(), calls=%async_computation.7 | async-start | bytes 7208960 | tf_op jit(solution)/shard_map/all_gather | solution.py:1047
  101.1 354.1 %reduce-scatter.5.cloned.1.call-start = ((), (), s32[]{:S(2)}) async-start(), calls=%async_computation.9 | async-start | bytes 3604480 | tf_op jit(solution)/shard_map/reduce_scatter | solution.py:1051
  320.0 231.9 %reduce-scatter.7.cloned.1.call-start = ((), (), s32[]{:S(2)}) async-start(), calls=%async_computation.10 | async-start | bytes 7208960 | tf_op jit(solution)/shard_map/reduce_scatter | solution.py:1051
  342.5 214.7 %reduce-scatter.11.cloned.1.call-start = ((), (), s32[]{:S(2)}) async-start(), calls=%async_computation.12 | async-start | bytes 1310720 | tf_op jit(solution)/shard_map/reduce_scatter | solution.py:1051
  342.5 114.2 %copy-start.10 = (bf16[2560,384]{1,0:T(8,128)(2,1)S(1)}, bf16[2560,384]{1,0:T(8,128)(2,1)}, u32[]{:S(2)}) copy-start(bf16[2560,384]{1,0:T(8,128)(2,1)} %get-tuple-element.63) | copy-start | bytes 5898244
  455.2 8.6 %slice-start = ((s8[11141120]{0:T(1024)(128)(4,1)}), s8[4194304]{0:T(1024)(128)(4,1)S(1)}, s32[]{:S(2)}) async-start(s8[11141120]{0:T(1024)(128)(4,1)} %bitcast.61), calls=%async_computation.14 | async-start | bytes 8388608
  456.7 7.1 %slice-start.1 = ((s8[11141120]{0:T(1024)(128)(4,1)}), s8[4194304]{0:T(1024)(128)(4,1)S(1)}, s32[]{:S(2)}) async-start(s8[11141120]{0:T(1024)(128)(4,1)} %bitcast.61), calls=%async_computation.15 | async-start | bytes 8388608
  456.7 7.1 %slice-start.2 = ((s8[11141120]{0:T(1024)(128)(4,1)}), s8[2752512]{0:T(1024)(128)(4,1)S(1)}, s32[]{:S(2)}) async-start(s8[11141120]{0:T(1024)(128)(4,1)} %bitcast.61), calls=%async_computation.16 | async-start | bytes 5505024
  456.7 7.1 %copy-start.11 = (bf16[2,2,64,2048]{3,2,1,0:T(8,128)(2,1)S(1)}, bf16[2,2,64,2048]{3,2,1,0:T(8,128)(2,1)}, u32[]{:S(2)}) copy-start(bf16[2,2,64,2048]{3,2,1,0:T(8,128)(2,1)} %get-tuple-element.64) | copy-start | bytes 3145732
  473.6 146.7 %reduce-scatter.9.cloned.1.call-start = ((), (), s32[]{:S(2)}) async-start(), calls=%async_computation.11 | async-start | bytes 3932160 | tf_op jit(solution)/shard_map/reduce_scatter | solution.py:1051
  551.9 4.0 copy-start.5
  551.9 5.3 copy-start.4
  551.9 68.4 %all-to-all-start = ((bf16[8,64,1408]{2,1,0:T(8,128)(2,1)}), bf16[8,64,1408]{2,1,0:T(8,128)(2,1)S(1)}, u32[]{:S(2)}, u32[]{:S(2)}) async-start(bf16[8,64,1408]{2,1,0:T(8,128)(2,1)} %bitcast.48), calls=%async_computation.3 | async-start | bytes 2883584 | tf_op jit(solution)/shard_map/all_to_all | solution.py:1055
  559.7 60.7 %copy-start.9 = (f32[1,256]{1,0:T(1,128)S(1)}, f32[1,256]{1,0:T(1,128)}, u32[]{:S(2)}) copy-start(f32[1,256]{1,0:T(1,128)} %get-tuple-element.85) | copy-start | bytes 3076
  620.2 22.7 %copy-start.3 = (bf16[5,64,2048]{2,1,0:T(8,128)(2,1)S(1)}, bf16[5,64,2048]{2,1,0:T(8,128)(2,1)}, u32[]{:S(2)}) copy-start(bf16[5,64,2048]{2,1,0:T(8,128)(2,1)} %get-tuple-element.77) | copy-start | bytes 3932164
  620.3 1.1 copy-start
  638.5 8.1 %copy-start.8 = (f32[64,2048]{1,0:T(8,128)S(1)}, f32[64,2048]{1,0:T(8,128)}, u32[]{:S(2)}) copy-start(f32[64,2048]{1,0:T(8,128)} %get-tuple-element.119) | copy-start | bytes 1572868
  638.6 8.8 %copy-start.7 = (f32[64,2048]{1,0:T(8,128)S(1)}, f32[64,2048]{1,0:T(8,128)}, u32[]{:S(2)}) copy-start(f32[64,2048]{1,0:T(8,128)} %get-tuple-element.120) | copy-start | bytes 1572868
  638.6 9.6 %copy-start.6 = (f32[64,2048]{1,0:T(8,128)S(1)}, f32[64,2048]{1,0:T(8,128)}, u32[]{:S(2)}) copy-start(f32[64,2048]{1,0:T(8,128)} %get-tuple-element.121) | copy-start | bytes 1572868
  642.9 6.1 copy-start.2
  644.0 6.1 copy-start.1
Sparse Core Ops, SparseCore 0:
  10.2 31.2 all-gather.11
  43.0 62.4 all-gather.5
  107.1 57.8 all-gather.9
  166.4 105.4 all-gather.7
  320.1 54.1 reduce-scatter.4
  376.5 102.1 reduce-scatter.6
  480.9 27.6 reduce-scatter.10
  552.0 57.8 reduce-scatter.8

commit v4 on v3

--- a/solution.py
+++ b/solution.py
@@ -9,8 +9,7 @@
 
 HEADS = 16
 BLOCK = 64
-UNROLL = 2
-UNROLL_FORWARD = 4
+UNROLL = 4
 EPSILON = 1e-06
 EXTRA = 128
 BF = jnp.bfloat16
@@ -86,8 +85,8 @@
 
     qfi_ref[...] = nn(n_ref[...], w_ref[...])
     lower = triangle(True).astype(BF)
-    for u in range(UNROLL_FORWARD):
-        chunk = step * UNROLL_FORWARD + u
+    for u in range(UNROLL):
+        chunk = step * UNROLL + u
         rows = slice(u * BLOCK, (u + 1) * BLOCK)
         at = lax.broadcasted_iota(jnp.int32, (BLOCK, 1), 0) + chunk * BLOCK
         live = (at < live_ref[0]).astype(F32)
@@ -194,6 +193,8 @@
 
 MESH = pl.DeviceIdType.MESH
 PIECES = 5
+EARLY = 3
+TILE = 1024
 VMEM_LIMIT = 60 * 1024 * 1024
 (S_X, S_Y, S_CORE, S_DIAG_Y, S_DIAG_X, S_CORE_X, S_CORE_Y, S_CORE_D, R_CORE, R_X, R_Y, R_LAST_Y, R_LAST_X, KINDS) = range(14)
 
@@ -303,31 +304,31 @@
             copy.wait_send()
 
 
+def swap_pairs(place, parts, outs, send, recv, local):
+    pairs = []
+    for i, (part, out) in enumerate(zip(parts, outs)):
+        pairs.append((pltpu.make_async_copy(part.at[place.me], out.at[place.me], local.at[i]), None))
+        for k, flips in enumerate(FLIPS):
+            there = out.at[place.rank(*flips)]
+            pairs.append(tuple(
+                pltpu.make_async_remote_copy(
+                    src_ref=src, dst_ref=dst, send_sem=send.at[i, k], recv_sem=recv.at[i, k],
+                    device_id=place.device(*flips), device_id_type=MESH,
+                )
+                for src, dst in ((part.at[place.rank(*flips)], out.at[place.me]), (there, there))
+            ))
+    return pairs
+
+
 def swap_starts(place, parts, outs, send, recv, local):
-    copies = []
-    for i, (part, out) in enumerate(zip(parts, outs)):
-        own = pltpu.make_async_copy(part.at[place.me], out.at[place.me], local.at[i])
-        own.start()
-        for k, flips in enumerate(((0, 0, 1), (0, 1, 0), (1, 0, 0), (0, 1, 1), (1, 0, 1), (1, 1, 0), (1, 1, 1))):
-            copy = pltpu.make_async_remote_copy(
-                src_ref=part.at[place.rank(*flips)],
-                dst_ref=out.at[place.me],
-                send_sem=send.at[i, k],
-                recv_sem=recv.at[i, k],
-                device_id=place.device(*flips),
-                device_id_type=MESH,
-            )
-            copy.start()
-            there = out.at[place.rank(*flips)]
-            copies.append((copy, pltpu.make_async_remote_copy(
-                src_ref=there, dst_ref=there, send_sem=send.at[i, k], recv_sem=recv.at[i, k],
-                device_id=place.device(*flips), device_id_type=MESH)))
-        copies.append((own, None))
-    return copies
-
-
-def swap_waits(copies):
-    for copy, arrival in copies:
+    pairs = swap_pairs(place, parts, outs, send, recv, local)
+    for copy, _ in pairs:
+        copy.start()
+    return pairs
+
+
+def swap_waits(pairs):
+    for copy, arrival in pairs:
         if arrival is None:
             copy.wait()
         else:
@@ -514,30 +515,8 @@
     return full.reshape(8 * tokens, width), swapped
 
 
-def finish_units(in_ref, weights, outs, scale, planes):
-    ranks, rows, both = in_ref.shape
-    units = both // 2
-    units_in = units // planes
-    total = jnp.zeros((rows, 1), F32)
-    for side, (ref, out) in enumerate(zip(weights, outs)):
-        for i in range(planes):
-            for s in range(ranks):
-                at = side * units + i * units_in
-                to = (i * ranks + s) * units_in
-                grad = in_ref[s, :, at : at + units_in].astype(F32)
-                total += jnp.sum(grad * ref[:, to : to + units_in].astype(F32), axis=1, keepdims=True)
-                out[:, to : to + units_in] = grad * scale
-    return total
-
-
-def exit_plane(summed, weights, gain, gap_grad, unit_rows, unit_weights, unit_gain, per_rank, groups, planes, collective_id):
-    rows, model = weights[0].shape
-    head = model // (8 * per_rank)
-    channels = per_rank * head
-    span = 8 // groups
-
-    def kernel(sum_ref, q_ref, f_ref, i_ref, gain_ref, gap_ref, unit_ref, gate_ref, up_ref, unit_gain_ref,
-               q_out, f_out, i_out, gain_out, gap_out, gate_out, up_out, unit_gain_out, landed, *sems):
+def exit_plane(summed, gap_grad, planes, collective_id):
+    def kernel(sum_ref, gap_ref, landed, gap_out, *sems):
         send, recv, local, gap_send, gap_recv = sems
         place = Place()
         greet_column_and_plane(place, planes)
@@ -545,21 +524,7 @@
         gaps = column_spread(place, planes, gap_ref, gap_out, gap_send, gap_recv)
         own_gap = pltpu.make_async_copy(gap_ref, gap_out.at[place.plane, place.core], local.at[1])
         own_gap.start()
-        unit_gain_out[...] = finish_units(unit_ref, (gate_ref, up_ref), (gate_out, up_out), unit_gain_ref[...], planes)
         swap_waits(copies)
-        scale = gain_ref[...]
-        total = jnp.zeros((rows, 1), F32)
-        for w, (ref, out) in enumerate(((q_ref, q_out), (f_ref, f_out), (i_ref, i_out))):
-            for a in range(groups):
-                for m in range(span):
-                    for j in range(per_rank):
-                        h = (m * per_rank + j) * groups + a
-                        at = w * channels + j * head
-                        grad = landed[a * span + m, :, at : at + head].astype(F32)
-                        cols = slice(h * head, (h + 1) * head)
-                        total += jnp.sum(grad * ref[:, cols].astype(F32), axis=1, keepdims=True)
-                        out[:, cols] = grad * scale
-        gain_out[...] = total
         for copy, arrival in gaps:
             copy.wait_send()
             arrival.wait_recv()
@@ -567,28 +532,81 @@
 
     return pl.pallas_call(
         kernel,
-        in_specs=[ANY_SPEC] + [VMEM_SPEC] * 4 + [ANY_SPEC] + [VMEM_SPEC] * 4,
-        out_specs=[VMEM_SPEC] * 4 + [ANY_SPEC] + [VMEM_SPEC] * 3,
-        out_shape=[jax.ShapeDtypeStruct((rows, model), F32)] * 3
-        + [
-            jax.ShapeDtypeStruct((rows, 1), F32),
+        in_specs=[ANY_SPEC] * 2,
+        out_specs=[ANY_SPEC] * 2,
+        out_shape=[
+            jax.ShapeDtypeStruct(summed.shape, summed.dtype),
             jax.ShapeDtypeStruct((planes, 2) + gap_grad.shape, gap_grad.dtype),
-        ]
-        + [jax.ShapeDtypeStruct(unit_weights[0].shape, F32)] * 2
-        + [jax.ShapeDtypeStruct((rows, 1), F32)],
+        ],
         scratch_shapes=[
-            pltpu.VMEM((8, rows, 3 * channels), BF),
             pltpu.SemaphoreType.DMA((1, 7)),
             pltpu.SemaphoreType.DMA((1, 7)),
             pltpu.SemaphoreType.DMA((2,)),
             pltpu.SemaphoreType.DMA((2 * planes - 1,)),
             pltpu.SemaphoreType.DMA((2 * planes - 1,)),
         ],
-        compiler_params=pltpu.CompilerParams(
-            collective_id=collective_id, has_side_effects=True, vmem_limit_bytes=VMEM_LIMIT
-        ),
+        compiler_params=pltpu.CompilerParams(collective_id=collective_id, has_side_effects=True),
         name="exit_plane",
-    )(summed, *weights, gain, gap_grad, unit_rows, *unit_weights, unit_gain)
+    )(summed, gap_grad)
+
+
+def finish(weights, gain, swapped, moves):
+    rows, width = weights[0].shape
+    tile = 512
+
+    def kernel(*refs):
+        in_ref, gain_ref = refs[0], refs[1]
+        w_refs = refs[2 : 2 + len(weights)]
+        outs, gain_out = refs[2 + len(weights) : -1], refs[-1]
+        for w, rank, source, target in moves:
+            outs[w][:, target] = in_ref[rank, :, source].astype(F32)
+        scale = gain_ref[...]
+        total = jnp.zeros((rows, tile), F32)
+        for ref, out in zip(w_refs, outs):
+            for at in range(0, width, tile):
+                grad = out[:, at : at + tile]
+                total += grad * ref[:, at : at + tile].astype(F32)
+                out[:, at : at + tile] = grad * scale
+        column = jnp.sum(total, axis=1, keepdims=True)
+        diagonal = lax.broadcasted_iota(jnp.int32, (rows, rows), 0) == lax.broadcasted_iota(jnp.int32, (rows, rows), 1)
+        gain_out[...] = jnp.sum(jnp.where(diagonal, column, 0.0), axis=0, keepdims=True)
+
+    results = pl.pallas_call(
+        kernel,
+        in_specs=[VMEM_SPEC] * (2 + len(weights)),
+        out_specs=[VMEM_SPEC] * (len(weights) + 1),
+        out_shape=[jax.ShapeDtypeStruct((rows, width), F32)] * len(weights) + [jax.ShapeDtypeStruct((1, rows), F32)],
+        compiler_params=pltpu.CompilerParams(vmem_limit_bytes=VMEM_LIMIT),
+        name="finish",
+    )(swapped, gain, *weights)
+    return results[:-1], results[-1].reshape(rows)
+
+
+def unit_moves(units, planes, ranks):
+    units_in = units // planes
+    return [
+        (
+            side,
+            s,
+            slice(side * units + i * units_in, side * units + (i + 1) * units_in),
+            slice((i * ranks + s) * units_in, (i * ranks + s + 1) * units_in),
+        )
+        for side in range(2)
+        for i in range(planes)
+        for s in range(ranks)
+    ]
+
+
+def head_moves(head, per_rank, groups, span):
+    moves = []
+    for w in range(3):
+        for a in range(groups):
+            for m in range(span):
+                for j in range(per_rank):
+                    h = (m * per_rank + j) * groups + a
+                    at = (w * per_rank + j) * head
+                    moves.append((w, a * span + m, slice(at, at + head), slice(h * head, (h + 1) * head)))
+    return moves
 
 
 class Scatter:
@@ -635,13 +653,14 @@
 
     def start_loads(self):
         core = self.place.core
-        self.weight_copy().start()
         for b in range(PIECES):
             for j in range(4):
                 for side, at in ((0, 2 * j + 1 - core), (4, 2 * j + core)):
                     pltpu.make_async_copy(
                         self.left_ref.at[at, b], self.x_buf.at[b, side + j], self.load_sem.at[b]
                     ).start()
+            if b == 0:
+                self.weight_copy().start()
 
     def send_core(self, b):
         return remote(self.core_out.at[b], self.core_in.at[b], self.sems, R_CORE, b, self.place.device(0, 0, 1))
@@ -659,24 +678,26 @@
         return remote(self.last_x_out.at[b], self.last_x_in.at[b], self.sems, R_LAST_X, b, self.place.device(0, 1, 0))
 
     def produce(self, b):
-        rows, depth, width, tile = self.rows, self.depth, self.width, 256
+        rows, depth, width, tile = self.rows, self.depth, self.width, min(TILE, self.width)
         pltpu.make_async_copy(self.x_buf.at[b], self.x_buf.at[b], self.load_sem.at[b]).wait()
 
-        @pl.loop(0, width // tile)
-        def _(t):
-            at = pl.multiple_of(t * tile, tile)
-            lhs = self.x_buf[b, :, :, :depth].reshape(8 * rows, depth)
-            if self.transposed:
-                out = nt(lhs, self.w_buf[pl.ds(at, tile), :])
-            else:
-                out = nn(lhs, self.w_buf[:, pl.ds(at, tile)])
-            self.core_out[b, :, :, pl.ds(at, tile)] = out[: 4 * rows].astype(BF).reshape(4, rows, tile)
-            self.total[:, :, pl.ds(at, tile)] = out[4 * rows :].reshape(4, rows, tile)
-
+        def product(side, t):
+            lhs = self.x_buf[b, 4 * side : 4 * side + 4, :, :depth].reshape(4 * rows, depth)
+            at = slice(t * tile, (t + 1) * tile)
+            out = nt(lhs, self.w_buf[at, :]) if self.transposed else nn(lhs, self.w_buf[:, at])
+            return out.reshape(4, rows, tile), at
+
+        for t in range(width // tile):
+            out, at = product(0, t)
+            self.core_out[b, :, :, at] = out.astype(BF)
         if self.stats:
             self.core_out[b, :, :, width:] = self.x_buf[b, :4, :, depth:]
+        self.send_core(b).start()
+        for t in range(width // tile):
+            out, at = product(1, t)
+            self.total[:, :, at] = out
+        if self.stats:
             self.total[:, :, width:] = self.x_buf[b, 4:, :, depth:].astype(F32)
-        self.send_core(b).start()
 
     def stage_one(self, b):
         place, half, total, core_in = self.place, self.half, self.total, self.core_in
@@ -726,7 +747,7 @@
     return [pltpu.SemaphoreType.DMA((KINDS, PIECES)), pltpu.SemaphoreType.DMA((KINDS, PIECES))]
 
 
-def product_scatter(left, weight, transposed, stats, epilogue, owned, outs, gathered, collective_id):
+def product_scatter(left, weight, transposed, stats, epilogue, owned, outs, gathered, collective_id, fillers=()):
     tokens = left.shape[0] // 8
     rows = tokens // PIECES
     left = left.reshape(8, PIECES, rows, left.shape[1])
@@ -737,22 +758,46 @@
         refs = list(refs)
         left_ref, weight_ref = refs.pop(0), refs.pop(0)
         own_refs = [refs.pop(0) for _ in owned]
+        extra_in = [[refs.pop(0) for _ in f.arrays] for f in fillers]
         out_refs = [refs.pop(0) for _ in outs]
         full_ref = refs.pop(0) if gathered else None
+        extra_out = [refs.pop(0) for _ in fillers]
         place = Place()
         sems = (refs.pop(0), refs.pop(0))
         scatter.bind(place, sems, left_ref, weight_ref, refs[:count])
+        refs = refs[count:]
+        own_bufs = [refs.pop(0) for _ in owned]
+        out_bufs = [refs.pop(0) for _ in outs]
+        own_sem, out_sem = refs.pop(0), refs.pop(0)
+        own_copies = [
+            pltpu.make_async_copy(ref, buf, own_sem.at[i]) for i, (ref, buf) in enumerate(zip(own_refs, own_bufs))
+        ]
+
+        def out_copies(b):
+            return [
+                pltpu.make_async_copy(buf.at[b], ref.at[b], out_sem.at[i, b])
+                for i, (buf, ref) in enumerate(zip(out_bufs, out_refs))
+            ]
+
         scatter.start_loads()
+        for copy in own_copies:
+            copy.start()
+        for f, ins, out in zip(fillers, extra_in, extra_out):
+            f.bind(ins, out, refs[: len(f.scratch)])
+            refs = refs[len(f.scratch) :]
+            f.start()
         greet(place)
         if gathered:
-            n_buf, keep_sem = refs[count:]
+            n_buf, keep_sem = refs
             gather = Gather(place, n_buf, full_ref, sems, keep_sem)
 
         def end(b):
             result, stat = scatter.stage_three(b)
-            written, sent = epilogue(result, stat, *[r[b] for r in own_refs])
-            for ref, value in zip(out_refs, written):
-                ref[b] = value
+            written, sent = epilogue(result, stat, *[r[b] for r in own_bufs])
+            for buf, value in zip(out_bufs, written):
+                buf[b] = value
+            for copy in out_copies(b):
+                copy.start()
             if gathered:
                 n_buf[b] = sent
                 gather.start(b)
@@ -764,6 +809,14 @@
             guarded(scatter.stage_one, step - 1)
             guarded(scatter.produce, step)
             guarded(scatter.stage_two, step - 3)
+            for f in fillers:
+                f.step(step)
+
+            @pl.when(step == 5)
+            def _():
+                for copy in own_copies:
+                    copy.wait()
+
             guarded(end, step - 5)
             if gathered:
                 guarded(gather.forward, step - 7)
@@ -775,18 +828,34 @@
                 gather.finish(b)
                 gather.drain(b)
             scatter.drain(b)
-
-    any_spec, vmem = pl.BlockSpec(memory_space=pl.ANY), pl.BlockSpec(memory_space=pltpu.VMEM)
+            for copy in out_copies(b):
+                copy.wait()
+
+        for f in fillers:
+            f.end()
+
+    any_spec = ANY_SPEC
     out_shape = [jax.ShapeDtypeStruct((PIECES, rows, c), d) for c, d in outs]
-    out_specs = [vmem] * len(outs)
+    out_specs = [any_spec] * len(outs)
     scratch = plane_sems() + scatter.scratch()
+    scratch += [pltpu.VMEM((PIECES, rows, o.shape[1]), o.dtype) for o in owned]
+    scratch += [pltpu.VMEM(o.shape, o.dtype) for o in out_shape]
+    scratch += [pltpu.SemaphoreType.DMA((len(owned),)), pltpu.SemaphoreType.DMA((len(outs), PIECES))]
     if gathered:
         out_shape.append(jax.ShapeDtypeStruct((8, PIECES, rows, gathered), BF))
         out_specs.append(any_spec)
+    args = [left, weight] + [o.reshape(PIECES, rows, o.shape[1]) for o in owned]
+    in_specs = [any_spec, any_spec] + [any_spec] * len(owned)
+    for f in fillers:
+        args, in_specs = args + f.arrays, in_specs + [any_spec] * len(f.arrays)
+        out_shape.append(f.out_shape)
+        out_specs.append(any_spec)
+        scratch += f.scratch
+    if gathered:
         scratch += [pltpu.VMEM((PIECES, rows, gathered), BF), pltpu.SemaphoreType.DMA((PIECES,))]
     results = pl.pallas_call(
         kernel,
-        in_specs=[any_spec, any_spec] + [vmem] * len(owned),
+        in_specs=in_specs,
         out_specs=out_specs,
         out_shape=out_shape,
         scratch_shapes=scratch,
@@ -799,16 +868,90 @@
             transcendentals=0,
         ),
         name="product_scatter",
-    )(left, weight, *[o.reshape(PIECES, rows, o.shape[1]) for o in owned])
+    )(*args)
     flat = [r.reshape(tokens, r.shape[2]) for r in results[: len(outs)]]
     if gathered:
-        flat.append(results[-1].reshape(8 * tokens, gathered))
-    return flat
+        flat.append(results[len(outs)].reshape(8 * tokens, gathered))
+    return flat + list(results[len(outs) + (1 if gathered else 0) :])
+
+
+class GradProduct:
+    BLOCK = 256
+
+    def __init__(self, left, right, by_right, first):
+        self.left, self.right, self.by_right, self.first = left, right, by_right, first
+        whole, streamed = (left, right) if by_right else (right, left)
+        self.tokens, self.blocks = left.shape[0], streamed.shape[1] // self.BLOCK
+        depth, width = left.shape[1], right.shape[1]
+        block = (depth, self.BLOCK) if by_right else (self.BLOCK, width)
+        self.arrays = [whole, streamed]
+        self.out_shape = jax.ShapeDtypeStruct((depth, width), BF)
+        self.scratch = [
+            pltpu.VMEM(whole.shape, BF),
+            pltpu.VMEM((2, self.tokens, self.BLOCK), BF),
+            pltpu.VMEM((2,) + block, BF),
+            pltpu.SemaphoreType.DMA((1,)),
+            pltpu.SemaphoreType.DMA((2,)),
+            pltpu.SemaphoreType.DMA((2,)),
+        ]
+
+    def plain(self):
+        return tn(self.left, self.right).astype(BF)
+
+    def bind(self, ins, out, refs):
+        self.whole_ref, self.streamed_ref = ins
+        self.out = out
+        self.w_buf, self.s_buf, self.o_buf, self.w_sem, self.s_sem, self.o_sem = refs
+
+    def columns(self, b):
+        return pl.ds(pl.multiple_of(b * self.BLOCK, self.BLOCK), self.BLOCK)
+
+    def load(self, b):
+        return pltpu.make_async_copy(self.streamed_ref.at[:, self.columns(b)], self.s_buf.at[b % 2], self.s_sem.at[b % 2])
+
+    def store(self, b):
+        to = self.out.at[:, self.columns(b)] if self.by_right else self.out.at[self.columns(b)]
+        return pltpu.make_async_copy(self.o_buf.at[b % 2], to, self.o_sem.at[b % 2])
+
+    def whole_copy(self):
+        return pltpu.make_async_copy(self.whole_ref, self.w_buf, self.w_sem.at[0])
+
+    def start(self):
+        self.whole_copy().start(priority=1)
+        self.load(0).start(priority=1)
+        self.load(1).start(priority=1)
+
+    def step(self, step):
+        b = step - self.first
+
+        @pl.when(b == 0)
+        def _():
+            self.whole_copy().wait()
+
+        @pl.when((b >= 0) & (b < self.blocks))
+        def _():
+            self.load(b).wait()
+
+            @pl.when(b >= 2)
+            def _():
+                self.store(b - 2).wait()
+
+            streamed, whole = self.s_buf[b % 2], self.w_buf[...]
+            product = tn(whole, streamed) if self.by_right else tn(streamed, whole)
+            self.o_buf[b % 2] = product.astype(BF)
+            self.store(b).start(priority=1)
+
+        @pl.when((b >= 0) & (b + 2 < self.blocks))
+        def _():
+            self.load(b + 2).start(priority=1)
+
+    def end(self):
+        self.store(self.blocks - 2).wait()
+        self.store(self.blocks - 1).wait()
 
 
 def mixer_specs(tokens, heads, reverse):
-    width, unroll = heads * 128, UNROLL if reverse else UNROLL_FORWARD
-    span = unroll * BLOCK
+    width, span = heads * 128, UNROLL * BLOCK
     steps = tokens // span
 
     def at(i):
@@ -818,7 +961,7 @@
         steps,
         pl.BlockSpec((span, 3 * width), lambda i, *_: (at(i), 0)),
         pl.BlockSpec((1, width), lambda i, *_: (0, 0)),
-        pl.BlockSpec((unroll, heads, 128, 128), lambda i, *_: (at(i), 0, 0, 0)),
+        pl.BlockSpec((UNROLL, heads, 128, 128), lambda i, *_: (at(i), 0, 0, 0)),
         lambda columns: pl.BlockSpec((span, columns), lambda i, *_: (at(i), 0)),
     )
 
@@ -832,17 +975,22 @@
     def kernel(cut_ref, live_ref, n_ref, w_ref, gap_ref, *refs):
         if not together:
             return mixer_forward_kernel(heads, cut_ref, live_ref, n_ref, w_ref, gap_ref, *refs)
-        own_ref, pieces_ref, mixed_ref, kept_ref, qfi_ref, full_ref, rows_ref, state, send, recv, local, w_send, w_recv, w_local = refs
+        (own_ref, pieces_ref, mixed_ref, kept_ref, qfi_ref, full_ref, rows_ref, state, own_buf, pieces_buf, send, recv, local,
+         w_send, w_recv, w_local) = refs
         place = Place()
-        gather = Gather(place, own_ref, full_ref, (send, recv), local)
+        gather = Gather(place, own_buf, full_ref, (send, recv), local)
+        loads = [
+            pltpu.make_async_copy(own_ref, own_buf, local.at[0]),
+            pltpu.make_async_copy(pieces_ref, pieces_buf, w_local.at[0]),
+        ]
 
         def exchange(j):
             core = place.core
             here = pltpu.make_async_copy(
-                pieces_ref.at[core * per_rank + j], rows_ref.at[j, core], w_local.at[j]
+                pieces_buf.at[core * per_rank + j], rows_ref.at[j, core], w_local.at[j]
             )
             there = pltpu.make_async_remote_copy(
-                src_ref=pieces_ref.at[(1 - core) * per_rank + j], dst_ref=rows_ref.at[j, core],
+                src_ref=pieces_buf.at[(1 - core) * per_rank + j], dst_ref=rows_ref.at[j, core],
                 send_sem=w_send.at[j], recv_sem=w_recv.at[j], device_id=place.device(0, 0, 1), device_id_type=MESH,
             )
             back = rows_ref.at[j, 1 - core]
@@ -854,8 +1002,12 @@
 
         @pl.when(pl.program_id(0) == 0)
         def _():
+            for load in loads:
+                load.start()
             greet(place)
-            pl.loop(0, PIECES)(gather.start)
+            for load in loads:
+                load.wait()
+            pl.loop(0, EARLY)(gather.start)
             for j in range(per_rank):
                 here, there, _ = exchange(j)
                 here.start()
@@ -865,10 +1017,15 @@
             heads, cut_ref, live_ref, n_ref, w_ref, gap_ref, mixed_ref, kept_ref, qfi_ref, state
         )
 
+        for b in range(EARLY):
+            @pl.when(pl.program_id(0) == min(steps - 1, (8 + 7 * b) // 4))
+            def _():
+                gather.forward(b)
+
         @pl.when(pl.program_id(0) == steps - 1)
         def _():
-            for stage in (gather.forward, gather.forward_last, gather.finish, gather.drain):
-                pl.loop(0, PIECES)(stage)
+            for stage in (gather.forward_last, gather.finish, gather.drain):
+                pl.loop(0, EARLY)(stage)
             for j in range(per_rank):
                 here, there, arrival = exchange(j)
                 here.wait()
@@ -895,6 +1052,7 @@
             jax.ShapeDtypeStruct((8,) + own.shape, own.dtype),
             jax.ShapeDtypeStruct((per_rank, 2, w_rows, model), BF),
         ]
+        scratch = scratch + [pltpu.VMEM(own.shape, BF), pltpu.VMEM(out_pieces.shape, BF)]
         scratch = scratch + plane_sems() + [pltpu.SemaphoreType.DMA((PIECES,))]
         scratch = scratch + [pltpu.SemaphoreType.DMA((per_rank,))] * 3
         params = pltpu.CompilerParams(
@@ -916,15 +1074,90 @@
     )(cut, live, *args)
     mixed, kept, qfi = results[:3]
     if together:
-        return mixed, kept, qfi, results[3].reshape(tokens, own.shape[2]), results[4].reshape(width, model)
+        return mixed, kept, qfi, results[3], results[4].reshape(width, model)
     return mixed, kept, qfi, lax.all_gather(own, "seq", axis=0, tiled=True), None
 
 
-def mixer_backward(cut, live, qfi, gap, kept, grad, left, weight, epilogue, owned, collective_id):
+def mixer_backward(cut, live, qfi, gap, kept, grad, parts, grad_out, per_rank, collective_id):
     tokens, heads = qfi.shape[0], gap.shape[1] // 128
     width = heads * 128
     steps, qfi_spec, gap_spec, kept_spec, block = mixer_specs(tokens, heads, True)
     together = lax.axis_size("seq") == 8
+    planes = lax.axis_size("dp")
+
+    def kernel(cut_ref, live_ref, qfi_ref, gap_ref, kept_ref, grad_ref, *refs):
+        if not together:
+            return mixer_backward_kernel(heads, cut_ref, live_ref, qfi_ref, gap_ref, kept_ref, grad_ref, *refs)
+        (parts_ref, og_ref, out_ref, gap_out_ref, swapped_ref, sum_ref, state, parts_buf, og_buf, by_plane, landed,
+         send, recv, local, c_send, c_recv, z_send, z_recv, load_sem) = refs
+        place, step = Place(), pl.program_id(0)
+        core = place.core
+        loads = [
+            pltpu.make_async_copy(parts_ref, parts_buf, load_sem.at[0]),
+            pltpu.make_async_copy(og_ref, og_buf, load_sem.at[1]),
+        ]
+
+        def over_core(j):
+            there = by_plane.at[core * per_rank + j]
+            back = by_plane.at[(1 - core) * per_rank + j]
+            return [
+                pltpu.make_async_remote_copy(
+                    src_ref=src, dst_ref=dst, send_sem=c_send.at[j], recv_sem=c_recv.at[j],
+                    device_id=place.device(0, 0, 1), device_id_type=MESH,
+                )
+                for src, dst in ((og_buf.at[j, 1 - core], there), (back, back))
+            ]
+
+        def over_planes(hop):
+            plane = lax.rem(place.plane + hop, planes)
+            back = landed.at[planes - hop - 1]
+            return [
+                pltpu.make_async_remote_copy(
+                    src_ref=src, dst_ref=dst, send_sem=z_send.at[hop - 1], recv_sem=z_recv.at[hop - 1],
+                    device_id=(plane, place.me), device_id_type=MESH,
+                )
+                for src, dst in ((by_plane.at[plane], landed.at[planes - hop - 1]), (back, back))
+            ]
+
+        swaps = functools.partial(swap_pairs, place, [parts_buf], [swapped_ref], send, recv, local)
+
+        @pl.when(step == 0)
+        def _():
+            for load in loads:
+                load.start()
+            greet_column_and_plane(place, planes)
+            for load in loads:
+                load.wait()
+            for j in range(per_rank):
+                over_core(j)[0].start()
+                by_plane[core * per_rank + j] = og_buf[j, core]
+            for copy, _ in swaps():
+                copy.start()
+
+        @pl.when(step == 1)
+        def _():
+            for j in range(per_rank):
+                there, arrival = over_core(j)
+                there.wait_send()
+                arrival.wait_recv()
+            for hop in range(1, planes):
+                over_planes(hop)[0].start()
+
+        mixer_backward_kernel(
+            heads, cut_ref, live_ref, qfi_ref, gap_ref, kept_ref, grad_ref, out_ref, gap_out_ref, state
+        )
+
+        @pl.when(step == steps - 1)
+        def _():
+            swap_waits(swaps())
+            total = by_plane[place.plane].astype(F32)
+            for hop in range(1, planes):
+                there, arrival = over_planes(hop)
+                there.wait_send()
+                arrival.wait_recv()
+                total += landed[planes - hop - 1].astype(F32)
+            sum_ref[...] = total
+
     in_specs = [qfi_spec, gap_spec, kept_spec, block(width)]
     out_specs = [block(3 * width), gap_spec]
     out_shape = [jax.ShapeDtypeStruct((tokens, 3 * width), BF), jax.ShapeDtypeStruct((1, width), F32)]
@@ -932,63 +1165,31 @@
     args = [qfi, gap, kept, grad]
     params = pltpu.CompilerParams(vmem_limit_bytes=VMEM_LIMIT)
     if together:
-        rows = tokens // 8 // PIECES
-        left = left.reshape(8, PIECES, rows, left.shape[1])
-        scatter = Scatter(left.shape, weight.shape, False, False)
-        model = weight.shape[1]
-        stride = max(1, (steps - 2) // PIECES)
-        any_spec = pl.BlockSpec(memory_space=pl.ANY)
-        whole = pl.BlockSpec((PIECES, rows, model), lambda i, *_: (0, 0, 0), pipeline_mode=pl.Buffered(1))
-        in_specs = in_specs + [any_spec, any_spec, whole]
-        args = args + [left, weight, owned.reshape(PIECES, rows, model)]
-        out_specs = out_specs + [whole]
-        out_shape = out_shape + [jax.ShapeDtypeStruct((PIECES, rows, model), BF)]
-        scratch = scratch + plane_sems() + scatter.scratch()
+        rows, model = grad_out.shape[2:]
+        in_specs, args = in_specs + [ANY_SPEC] * 2, args + [parts, grad_out]
+        out_specs = out_specs + [ANY_SPEC, pl.BlockSpec((rows, model), lambda i, *_: (0, 0))]
+        out_shape = out_shape + [
+            jax.ShapeDtypeStruct(parts.shape, BF),
+            jax.ShapeDtypeStruct((rows, model), F32),
+        ]
+        scratch = scratch + [
+            pltpu.VMEM(parts.shape, BF),
+            pltpu.VMEM(grad_out.shape, BF),
+            pltpu.VMEM((planes, rows, model), BF),
+            pltpu.VMEM((planes - 1, rows, model), BF),
+            pltpu.SemaphoreType.DMA((1, 7)),
+            pltpu.SemaphoreType.DMA((1, 7)),
+            pltpu.SemaphoreType.DMA((1,)),
+            pltpu.SemaphoreType.DMA((per_rank,)),
+            pltpu.SemaphoreType.DMA((per_rank,)),
+            pltpu.SemaphoreType.DMA((planes - 1,)),
+            pltpu.SemaphoreType.DMA((planes - 1,)),
+            pltpu.SemaphoreType.DMA((2,)),
+        ]
         params = pltpu.CompilerParams(
             vmem_limit_bytes=VMEM_LIMIT, collective_id=collective_id, has_side_effects=True
         )
-
-    def kernel(cut_ref, live_ref, qfi_ref, gap_ref, kept_ref, grad_ref, *refs):
-        if not together:
-            out_ref, gap_out_ref, state = refs
-            mixer_backward_kernel(
-                heads, cut_ref, live_ref, qfi_ref, gap_ref, kept_ref, grad_ref, out_ref, gap_out_ref, state
-            )
-            return
-        left_ref, weight_ref, owned_ref, out_ref, gap_out_ref, sum_ref, state, send, recv = refs[:9]
-        place, step = Place(), pl.program_id(0)
-        scatter.bind(place, (send, recv), left_ref, weight_ref, refs[9:])
-
-        @pl.when(step == 0)
-        def _():
-            scatter.start_loads()
-            greet(place)
-            scatter.weight_copy().wait()
-
-        def end(b):
-            result, _ = scatter.stage_three(b)
-            sum_ref[b] = epilogue(result, None, owned_ref[b])[0][0]
-
-        def phases(at):
-            for body, first in ((scatter.stage_one, 2), (scatter.produce, 0), (scatter.stage_two, 8), (end, 12)):
-                @pl.when((at >= first) & (lax.rem(at - first, stride) == 0) & (at < first + stride * PIECES))
-                def _():
-                    body((at - first) // stride)
-
-        phases(step)
-        mixer_backward_kernel(
-            heads, cut_ref, live_ref, qfi_ref, gap_ref, kept_ref, grad_ref, out_ref, gap_out_ref, state
-        )
-
-        @pl.when(step == steps - 1)
-        def _():
-            @pl.loop(steps, stride * (PIECES - 1) + 13)
-            def _(late):
-                phases(late)
-
-            pl.loop(0, PIECES)(scatter.drain)
-
-    results = pl.pallas_call(
+    return pl.pallas_call(
         kernel,
         grid_spec=pltpu.PrefetchScalarGridSpec(
             num_scalar_prefetch=2, grid=(steps,), in_specs=in_specs, out_specs=out_specs, scratch_shapes=scratch
@@ -1000,13 +1201,9 @@
         ),
         name="mixer_backward",
     )(cut, live, *args)
-    if together:
-        return results[0], results[1], results[2].reshape(tokens // 8, model)
-    (summed,) = product_all(left, weight, False, False, epilogue, [owned], [(weight.shape[1], BF)], 0, collective_id)
-    return results[0], results[1], summed
-
-
-def feed_forward_kernel(units, n_ref, g_ref, gu_ref, down_ref, units_ref, grad_ref, gate_w, up_w):
+
+
+def feed_forward_kernel(units, n_ref, gu_ref, units_ref, act_ref, slope_ref, gate_w, up_w):
     @pl.when(pl.program_id(0) == 0)
     def _():
         gate_w[...] = gu_ref[:, :units]
@@ -1014,33 +1211,108 @@
 
     n = n_ref[...]
     gate, up = nn(n, gate_w[...]), nn(n, up_w[...])
-    d_units = nt(g_ref[...], down_ref[...])
     sig = jax.nn.sigmoid(gate)
     act = gate * sig
     units_ref[...] = (act * up).astype(BF)
-    grad_ref[:, :units] = (d_units * up * sig * (1.0 + gate * (1.0 - sig))).astype(BF)
-    grad_ref[:, units:] = (d_units * act).astype(BF)
-
-
-def feed_forward(n2, grad, gu, down):
+    act_ref[...] = act.astype(BF)
+    slope_ref[...] = (up * sig * (1.0 + gate * (1.0 - sig))).astype(BF)
+
+
+def feed_backward_kernel(units, g_ref, down_ref, act_ref, slope_ref, grad_ref):
+    d_units = nt(g_ref[...], down_ref[...])
+    grad_ref[:, :units] = (d_units * slope_ref[...].astype(F32)).astype(BF)
+    grad_ref[:, units:] = (d_units * act_ref[...].astype(F32)).astype(BF)
+
+
+def fixed_block(shape):
+    return pl.BlockSpec(shape, lambda i: (0, 0), pipeline_mode=pl.Buffered(1))
+
+
+def row_block(columns):
+    return pl.BlockSpec((512, columns), lambda i: (i, 0))
+
+
+def feed_forward(n2, gu, own, full, collective_id):
     tokens, model = n2.shape
+    units = gu.shape[1] // 2
+    steps = tokens // 512
+    together = lax.axis_size("seq") == 8
+
+    def kernel(n_ref, gu_ref, *refs):
+        if not together:
+            return feed_forward_kernel(units, n_ref, gu_ref, *refs)
+        own_ref, _, units_ref, act_ref, slope_ref, full_ref, gate_w, up_w, own_buf, send, recv, local = refs
+        place, step = Place(), pl.program_id(0)
+        gather = Gather(place, own_buf, full_ref, (send, recv), local)
+
+        @pl.when(step == 0)
+        def _():
+            load = pltpu.make_async_copy(own_ref, own_buf, local.at[0])
+            load.start()
+            greet(place)
+            load.wait()
+            pl.loop(EARLY, PIECES)(gather.start)
+
+        feed_forward_kernel(units, n_ref, gu_ref, units_ref, act_ref, slope_ref, gate_w, up_w)
+
+        @pl.when(step == min(3, steps - 1))
+        def _():
+            pl.loop(EARLY, PIECES)(gather.forward)
+
+        @pl.when(step == steps - 1)
+        def _():
+            for stage in (gather.forward_last, gather.finish, gather.drain):
+                pl.loop(EARLY, PIECES)(stage)
+
+    in_specs, args = [row_block(model), fixed_block(gu.shape)], [n2, gu]
+    out_specs = [row_block(units)] * 3
+    out_shape = [jax.ShapeDtypeStruct((tokens, units), d) for d in (BF, BF, BF)]
+    scratch = [pltpu.VMEM((model, units), BF), pltpu.VMEM((model, units), BF)]
+    params, aliases = pltpu.CompilerParams(vmem_limit_bytes=VMEM_LIMIT), {}
+    if together:
+        own = own.reshape(PIECES, own.shape[0] // PIECES, own.shape[1])
+        in_specs, args = in_specs + [ANY_SPEC] * 2, args + [own, full]
+        out_specs = out_specs + [ANY_SPEC]
+        out_shape = out_shape + [jax.ShapeDtypeStruct(full.shape, full.dtype)]
+        scratch = scratch + [pltpu.VMEM(own.shape, BF)] + plane_sems() + [pltpu.SemaphoreType.DMA((PIECES,))]
+        params = pltpu.CompilerParams(
+            vmem_limit_bytes=VMEM_LIMIT, collective_id=collective_id, has_side_effects=True
+        )
+        aliases = {3: 3}
+    results = pl.pallas_call(
+        kernel,
+        grid=(steps,),
+        in_specs=in_specs,
+        out_specs=out_specs,
+        out_shape=out_shape,
+        scratch_shapes=scratch,
+        compiler_params=params,
+        input_output_aliases=aliases,
+        cost_estimate=pl.CostEstimate(
+            flops=4 * tokens * model * units, bytes_accessed=4 * tokens * model, transcendentals=tokens * units
+        ),
+        name="feed_forward",
+    )(*args)
+    if together:
+        return results[0], results[1], results[2], results[3].reshape(tokens, model)
+    return results[0], results[1], results[2], full
+
+
+def feed_backward(grad, down, act, slope):
+    tokens, model = grad.shape
     units = down.shape[0]
-    span = 512
-    fixed = lambda shape: pl.BlockSpec(shape, lambda i: (0, 0), pipeline_mode=pl.Buffered(1))
-    block = lambda columns: pl.BlockSpec((span, columns), lambda i: (i, 0))
     return pl.pallas_call(
-        functools.partial(feed_forward_kernel, units),
-        grid=(tokens // span,),
-        in_specs=[block(model), block(model), fixed(gu.shape), fixed(down.shape)],
-        out_specs=[block(units), block(2 * units)],
-        out_shape=[jax.ShapeDtypeStruct((tokens, units), BF), jax.ShapeDtypeStruct((tokens, 2 * units), BF)],
-        scratch_shapes=[pltpu.VMEM((model, units), BF), pltpu.VMEM((model, units), BF)],
+        functools.partial(feed_backward_kernel, units),
+        grid=(tokens // 512,),
+        in_specs=[row_block(model), fixed_block(down.shape), row_block(units), row_block(units)],
+        out_specs=row_block(2 * units),
+        out_shape=jax.ShapeDtypeStruct((tokens, 2 * units), BF),
         compiler_params=pltpu.CompilerParams(vmem_limit_bytes=VMEM_LIMIT),
         cost_estimate=pl.CostEstimate(
-            flops=6 * tokens * model * units, bytes_accessed=4 * tokens * model, transcendentals=tokens * units
+            flops=2 * tokens * model * units, bytes_accessed=8 * tokens * model, transcendentals=0
         ),
-        name="feed_forward",
-    )(n2, grad, gu, down)
+        name="feed_backward",
+    )(grad, down, act, slope)
 
 
 def gather_dp(v):
@@ -1055,9 +1327,9 @@
     return lax.all_to_all(v, "seq", split_axis=0, concat_axis=0, tiled=True)
 
 
-def product_all(left, weight, transposed, stats, epilogue, owned, outs, gathered, collective_id):
+def product_all(left, weight, transposed, stats, epilogue, owned, outs, gathered, collective_id, fillers=()):
     if lax.axis_size("seq") == 8:
-        return product_scatter(left, weight, transposed, stats, epilogue, owned, outs, gathered, collective_id)
+        return product_scatter(left, weight, transposed, stats, epilogue, owned, outs, gathered, collective_id, fillers)
     depth = left.shape[1] - (EXTRA if stats else 0)
     product = (nt if transposed else nn)(left[:, :depth], weight).astype(BF)
     result = lax.psum_scatter(product, "seq", scatter_dimension=0, tiled=True).astype(F32)
@@ -1066,7 +1338,8 @@
         stat = lax.psum_scatter(left[:, depth:].astype(F32), "seq", scatter_dimension=0, tiled=True)
     written, sent = epilogue(result, stat, *owned)
     written = [w.astype(d) for w, (_, d) in zip(written, outs)]
-    return written + ([lax.all_gather(sent, "seq", axis=0, tiled=True)] if gathered else [])
+    written += [lax.all_gather(sent, "seq", axis=0, tiled=True)] if gathered else []
+    return written + [f.plain() for f in fillers]
 
 
 def split_lanes(v):
@@ -1162,7 +1435,6 @@
         n1, gu_swapped = gather_plane(x16, w_gate, w_up, gain_f, planes, 2)
     qfi_full = gather_dp(qfi_swapped.reshape(ranks * rows, 3 * channels))
     gu_full = gather_dp(gu_swapped.reshape(ranks * rows, 2 * units))
-    down_own = gather_dp(w_down)
     gap_own = gap_own.reshape(1, channels).astype(F32)
     segment = ids[:, 0].reshape(tokens // BLOCK, BLOCK)
     live = jnp.sum(ids[:, 1]).reshape(1)
@@ -1184,16 +1456,25 @@
         normed = middle * inverse_rms(row_mean(middle * middle))
         return [middle, jnp.broadcast_to(factor_o, (x.shape[0], EXTRA))], normed.astype(BF)
 
+    mixed, w_down_late = order(mixed, w_down)
+    down_own = gather_dp(w_down_late)
     middle, factor_o, n2 = product_all(
         mixed, out_own, False, True, after_output, [x16], [(model, F32), (EXTRA, F32)], model, 4
     )
-    hidden_units, d_gu = feed_forward(n2, grad_all, gu_full, down_own)
+    hidden_units, act, slope, grad_all = feed_forward(n2, gu_full, og16, grad_all, 10)
+    def after_down(result, stat, middle):
+        return [(middle + result).astype(BF)], None
+
     grad_down = tn(hidden_units, grad_all).astype(BF)
     down_sum = scatter_dp(grad_down)
-    n2, _ = order(n2, grad_down)
-    grad_gu = tn(n2, d_gu).astype(BF)
+    act, _ = order(act, grad_down)
+    d_gu = feed_backward(grad_all, down_own, act, slope)
+    block_out, grad_gu = product_all(
+        hidden_units, down_own, False, False, after_down, [middle], [(model, BF)], 0, 6,
+        (GradProduct(n2, d_gu, False, 0),),
+    )
     gu_sum = scatter_dp(grad_gu)
-    d_gu, _ = order(d_gu, grad_gu)
+    d_gu, grad_gu = order(d_gu, grad_gu)
 
     def after_ffn(result, stat, middle, og16, x16, factor_o):
         factor_o = factor_o[:, :1]
@@ -1211,22 +1492,23 @@
     beta = jnp.sum(d_attn[:, model:].astype(F32), axis=1, keepdims=True)
     d_attn = d_attn[:, :model]
 
-    def after_down(result, stat, middle):
-        return [(middle + result).astype(BF)], None
-
     mixed = mixed[:, :channels]
     grad_out = tn(mixed, d_attn).astype(BF)
     d_mixed = (nt(d_attn, out_own) - beta * mixed.astype(F32)).astype(BF)
     grad_out, d_mixed = order(grad_out, d_mixed)
-    out_back = grad_out.reshape(per_rank, span, rows, model).transpose(1, 0, 2, 3)
-    out_sum = scatter_dp(swap_group(out_back).reshape(planes * rows, model))
-    d_qfi, gap_grad, block_out = mixer_backward(
-        cut, live, qfi, gap_own, kept, d_mixed, hidden_units, down_own, after_down, middle, 6
-    )
+    if plain:
+        d_qfi, gap_grad = mixer_backward(cut, live, qfi, gap_own, kept, d_mixed, None, None, per_rank, 6)
+        out_back = grad_out.reshape(per_rank, span, rows, model).transpose(1, 0, 2, 3)
+        out_rows = scatter_dp(swap_group(out_back).reshape(planes * rows, model)).astype(F32)
+        gu_rows = swap_seq(gu_sum).reshape(ranks, rows, 2 * units)
+    else:
+        d_qfi, gap_grad, gu_rows, out_rows = mixer_backward(
+            cut, live, qfi, gap_own, kept, d_mixed, gu_sum.reshape(ranks, rows, 2 * units),
+            grad_out.reshape(per_rank, span, rows, model), per_rank, 9,
+        )
     grad_qfi = tn(n1, d_qfi).astype(BF)
-    grad_qfi, d_qfi, gu_sum = order(grad_qfi, d_qfi, gu_sum)
+    grad_qfi, d_qfi = order(grad_qfi, d_qfi)
     qfi_sum = scatter_dp(grad_qfi)
-    gu_rows = swap_seq(gu_sum).reshape(ranks, rows, 2 * units)
 
     def after_mixer(result, stat, x16, d_middle):
         x = x16.astype(F32)
@@ -1236,12 +1518,11 @@
 
     (hidden_grad,) = product_all(d_qfi, qfi_full, True, False, after_mixer, [x16, d_middle], [(model, BF)], 0, 7)
 
-    hidden_grad, qfi_sum, gap_grad = order(hidden_grad, qfi_sum, gap_grad)
+    hidden_grad, gu_rows, down_sum, out_rows, gap_grad = order(hidden_grad, gu_rows, down_sum, out_rows, gap_grad)
 
     def rowdot(w, g):
         return jnp.sum(w.astype(F32) * g, axis=1)
 
-    out_rows = out_sum.astype(F32)
     g_out_gain = rowdot(w_output, out_rows)
     if plain:
         gu_rows = gu_rows.astype(F32)
@@ -1255,12 +1536,12 @@
         g_attn_gain = sum(rowdot(w, g) for w, g in zip(mixer_weights, parts))
         g_query, g_forget, g_input = [gain_a * g for g in parts]
     else:
+        (g_gate, g_up), g_ffn_gain = finish((w_gate, w_up), gain_f, gu_rows, unit_moves(units, planes, ranks))
         gap_tile = jnp.broadcast_to(gap_grad, (8, channels))
-        g_query, g_forget, g_input, g_attn_gain, gap_all, g_gate, g_up, g_ffn_gain = exit_plane(
-            qfi_sum.reshape(ranks, rows, 3 * channels), mixer_weights, gain_a, gap_tile,
-            gu_rows, (w_gate, w_up), gain_f, per_rank, groups, planes, 8,
+        qfi_rows, gap_all = exit_plane(qfi_sum.reshape(ranks, rows, 3 * channels), gap_tile, planes, 8)
+        (g_query, g_forget, g_input), g_attn_gain = finish(
+            mixer_weights, gain_a, qfi_rows, head_moves(head, per_rank, groups, span)
         )
-        g_attn_gain, g_ffn_gain = g_attn_gain[:, 0], g_ffn_gain[:, 0]
         plane, me = lax.axis_index("dp"), lax.axis_index("seq")
         at = lax.rem(plane, per_rank) * head + lax.rem(me, 2) * rows
         from_core = jnp.sum(gap_all[:, :, 0], axis=0)

time: 662 us -> 621 us (0.938)
  matrix products: 59.7 us -> 38.8 us
  local copies, waits for them, and re-layouts: 15.5 us -> 8.74 us
    pallas_call x5 -> x9, Pallas kernels: 327 us -> 382 us  [the longest x4 312 us: product_scatter(): pl.pallas_call(kernel, in_specs=in_specs, out_specs=out_specs, out_shape=...]
    pallas_call x1, Pallas kernels: 64.5 us -> 28.5 us  [mixer_backward(): pl.pallas_call(kernel, grid_spec=pltpu.PrefetchScalarGridSpec(num_scalar_...]
    pallas_call x1, Pallas kernels: 64 us -> 42.9 us  [mixer_forward(): pl.pallas_call(kernel, grid_spec=pltpu.PrefetchScalarGridSpec(num_scalar_...]
    dot_general x5 -> x4, matrix products: 59.7 us -> 38.8 us  [dot(): return lax.dot_general(a, b, (dims, ((), ())), preferred_element_type=F32)]
    unnamed x38 -> x25, local copies, waits for them, and re-layouts: 8.89 us -> 2.25 us
  transfers between devices with their start and end apart: 9 -> 7, of which waited for: 0 -> 1; matrix products, arithmetic and copies ran while one was open for 10% -> 6% of each run, Pallas kernels for 74% -> 80%
where the time goes in v4:
time: 621 us; the launch traced here: 616 us
  Pallas kernels  539 us (87%)
  matrix products  38.8 us (6%)
  between operations  14.7 us (2%)
  other arithmetic  12.6 us (2%)
  local copies, waits for them, and re-layouts  8.74 us (1%)
    pallas_call x4, Pallas kernels, product_scatter(): pl.pallas_call(kernel, in_specs=in_specs, out_specs=out_specs, out_shape=...  312 us
    pallas_call x1, Pallas kernels, gather_plane(): pl.pallas_call(kernel, in_specs=[VMEM_SPEC] * 4, out_specs=[ANY_SPEC] * 2...  65.5 us
    pallas_call x1, Pallas kernels, mixer_forward(): pl.pallas_call(kernel, grid_spec=pltpu.PrefetchScalarGridSpec(num_scalar_...  42.9 us
    dot_general x4, matrix products, dot(): return lax.dot_general(a, b, (dims, ((), ())), preferred_element_type=F32)  38.8 us
    pallas_call x1, Pallas kernels, feed_forward(): pl.pallas_call(kernel, grid=(steps,), in_specs=in_specs, out_specs=out_sp...  32.6 us
    pallas_call x1, Pallas kernels, mixer_backward(): pl.pallas_call(kernel, grid_spec=pltpu.PrefetchScalarGridSpec(num_scalar_...  28.5 us
    pallas_call x1, Pallas kernels, enter_plane(): pl.pallas_call(kernel, in_specs=[VMEM_SPEC] * 4 + [ANY_SPEC] * 2, out_spe...  19.7 us
    pallas_call x1, Pallas kernels, feed_backward(): pl.pallas_call(functools.partial(feed_backward_kernel, units), grid=(toke...  15.4 us
  transfers between devices with their start and end apart: 7, of which 1 were waited for; matrix products, arithmetic and copies ran while one was open for 6% of the time, Pallas kernels for 80%

profile of v4, /device:TPU:0, one launch (start us, length us, event | category | flops | bytes accessed | tf_op | source)
XLA Modules:
  0.0 616.0 jit_solution(17256002858955544849)
XLA Ops:
  7.9 1.8 fusion.14
  12.4 1.3 pad.9.gap_ref
  13.7 19.7 %enter_plane.1 = (bf16[8,64,768]{2,1,0:T(8,128)(2,1)}, s32[8,8,384]{2,1,0:T(8,128)}, bf16[4,2,16,128]{3,2,1,0:T(8,128)(2,1)}) custom-call(bf16[64,2048]{1,0:T(8,128)(2,1)} %refs_2_.2, bf16[64,2048]{1,0:T(8,128)(2,1)} %refs_3_.2, bf16[64,2048]{1,0:T(8,128)(2,1)} %refs_4_.1, f32[64,1]{1,0:T(8,128)} %copy.29.gain_ref.refs_1_, s32[8,384]{1,0:T(8,128)} %pad.8.ids_ref, ...), custom_call_target="tpu_custom_call" | custom-call | tf_op jit(solution)/shard_map/enter_plane/pallas_call | solution.py:435
  34.8 65.5 %gather_plane.1 = (bf16[8,5,64,2048]{3,2,1,0:T(8,128)(2,1)}, bf16[8,64,1408]{2,1,0:T(8,128)(2,1)}) custom-call(bf16[5,64,2048]{2,1,0:T(8,128)(2,1)} %bitcast.46, bf16[64,5632]{1,0:T(8,128)(2,1)} %refs_2_.3, bf16[64,5632]{1,0:T(8,128)(2,1)} %refs_3_.3, f32[64,1]{1,0:T(8,128)} %copy.31.gain_ref.refs_1_), custom_call_target="tpu_custom_call" | custom-call | tf_op jit(solution)/shard_map/gather_plane/pallas_call | solution.py:492
  100.4 1.6 slice_reduce_fusion
  105.6 42.9 %mixer_forward.1 = (bf16[2560,384]{1,0:T(8,128)(2,1)}, bf16[40,2,128,128]{3,2,1,0:T(8,128)(2,1)}, f32[2560,768]{1,0:T(8,128)}, bf16[8,5,64,2048]{3,2,1,0:T(8,128)(2,1)}, bf16[2,2,64,2048]{3,2,1,0:T(8,128)(2,1)}) custom-call(s32[40]{0:T(128)} %convert_reduce_fusion.1.cut_ref, s32[1]{0:T(128)} %bitcast.4.live_ref, bf16[2560,2048]{1,0:T(8,128)(2,1)} %bitcast.63, ...), custom_call_target="tpu_custom_call" | custom-call | flops 8891924480 | bytes 314572800 | tf_op jit(solution)/shard_map/mixer_forward/pallas_call | solution.py:1061
  149.1 98.3 %product_scatter.4 = (f32[5,64,2048]{2,1,0:T(8,128)}, f32[5,64,128]{2,1,0:T(8,128)}, bf16[8,5,64,2048]{3,2,1,0:T(8,128)(2,1)}) custom-call(bf16[8,5,64,384]{3,2,1,0:T(8,128)(2,1)} %bitcast.75, bf16[256,2048]{1,0:T(8,128)(2,1)} %bitcast.76, bf16[5,64,2048]{2,1,0:T(8,128)(2,1)} %bitcast.47), custom_call_target="tpu_custom_call" | custom-call | flops 2684354560 | bytes 314572800 | tf_op jit(solution)/shard_map/product_scatter/pallas_call | solution.py:856
  247.4 32.6 %feed_forward.1 = (bf16[2560,704]{1,0:T(8,128)(2,1)}, bf16[2560,704]{1,0:T(8,128)(2,1)}, bf16[2560,704]{1,0:T(8,128)(2,1)}, bf16[8,5,64,2048]{3,2,1,0:T(8,128)(2,1)}) custom-call(bf16[2560,2048]{1,0:T(8,128)(2,1)} %bitcast.72, bf16[2048,1408]{1,0:T(8,128)(2,1)} %all-gather.8.cloned.1.call-done.gu_ref.refs_1_, ...), custom_call_target="tpu_custom_call", output_to_operand_aliasing={{3}: (3, {})} | custom-call | flops 14763950080 | bytes 20971520 | tf_op jit(solution)/shard_map/feed_forward/pallas_call | solution.py:1282
  280.0 12.7 %convolution_convert_fusion.1 = bf16[704,2048]{1,0:T(8,128)(2,1)} fusion(bf16[2560,704]{1,0:T(8,128)(2,1)} %get-tuple-element.76, bf16[2560,2048]{1,0:T(8,128)(2,1)} %bitcast.41), kind=kOutput, calls=%fused_computation.7 | convolution fusion | flops 7383416832 | bytes 16973824 | tf_op jit(solution)/shard_map/dot_general | solution.py:20
  293.0 15.4 %feed_backward.1.refs_3_ = bf16[2560,1408]{1,0:T(8,128)(2,1)} custom-call(bf16[2560,2048]{1,0:T(8,128)(2,1)} %bitcast.42, bf16[704,2048]{1,0:T(8,128)(2,1)} %all-gather.10.cloned.1.call-done.down_ref.refs_1_, bf16[2560,704]{1,0:T(8,128)(2,1)} %get-tuple-element.81.act_ref, bf16[2560,704]{1,0:T(8,128)(2,1)} %get-tuple-element.82.slope_ref), custom_call_target="tpu_custom_call" | custom-call | flops 7381975040 | bytes 41943040 | tf_op jit(solution)/shard_map/feed_backward/pallas_call | solution.py:1304
  308.4 55.6 %product_scatter.5 = (bf16[5,64,2048]{2,1,0:T(8,128)(2,1)}, bf16[2048,1408]{1,0:T(8,128)(2,1)}) custom-call(bf16[8,5,64,704]{3,2,1,0:T(8,128)(2,1)} %bitcast.74, bf16[704,2048]{1,0:T(8,128)(2,1)} %all-gather.10.cloned.1.call-done.down_ref.refs_1_, f32[5,64,2048]{2,1,0:T(8,128)} %get-tuple-element.78.refs_2_, bf16[2560,1408]{1,0:T(8,128)(2,1)} %feed_backward.1.refs_3_, ...), custom_call_target="tpu_custom_call" | custom-call | flops 7381975040 | bytes 183500800 | tf_op jit(solution)/shard_map/product_scatter/pallas_call | solution.py:856
  364.3 103.4 %product_scatter.6 = (f32[5,64,2048]{2,1,0:T(8,128)}, bf16[8,5,64,2176]{3,2,1,0:T(8,128)(2,1)}) custom-call(bf16[8,5,64,1408]{3,2,1,0:T(8,128)(2,1)} %bitcast.43, bf16[2048,1408]{1,0:T(8,128)(2,1)} %all-gather.8.cloned.1.call-done.gu_ref.refs_1_, f32[5,64,2048]{2,1,0:T(8,128)} %get-tuple-element.78.refs_2_, bf16[5,64,2048]{2,1,0:T(8,128)(2,1)} %bitcast.68, ...), custom_call_target="tpu_custom_call" | custom-call | flops 14763950080 | bytes 314572800 | tf_op jit(solution)/shard_map/product_scatter/pallas_call | solution.py:856
  467.8 1.5 convert_reduce_fusion
  469.3 8.0 %fusion.10 = bf16[256,2048]{1,0:T(8,128)(2,1)} fusion(bf16[2560,2176]{1,0:T(8,128)(2,1)} %bitcast.56, bf16[2560,384]{1,0:T(8,128)(2,1)S(1)} %copy-done.6), kind=kOutput, calls=%fused_computation.8 | convolution fusion | flops 2684878848 | bytes 12845056 | tf_op jit(solution)/shard_map/dot_general | solution.py:20
  477.4 4.3 fusion.7.grad_ref
  481.7 28.5 %mixer_backward.1 = (bf16[2560,768]{1,0:T(8,128)(2,1)}, f32[1,256]{1,0:T(1,128)}, bf16[8,64,1408]{2,1,0:T(8,128)(2,1)}, f32[64,2048]{1,0:T(8,128)}) custom-call(s32[40]{0:T(128)} %convert_reduce_fusion.1.cut_ref, s32[1]{0:T(128)} %bitcast.4.live_ref, f32[2560,768]{1,0:T(8,128)} %get-tuple-element.84.qfi_ref, f32[1,256]{1,0:T(1,128)} %reshape.128.gap_ref, ...), custom_call_target="tpu_custom_call" | custom-call | flops 2013265920 | bytes 18350080 | tf_op jit(solution)/shard_map/mixer_backward/pallas_call | solution.py:1192
  510.2 13.8 %convolution_convert_fusion = bf16[2048,768]{1,0:T(8,128)(2,1)} fusion(bf16[2560,2048]{1,0:T(8,128)(2,1)} %bitcast.64, bf16[2560,768]{1,0:T(8,128)(2,1)} %get-tuple-element.94), kind=kOutput, calls=%fused_computation.6 | convolution fusion | flops 8054636544 | bytes 17563648 | tf_op jit(solution)/shard_map/dot_general | solution.py:20
  524.1 54.3 %product_scatter.7 = bf16[5,64,2048]{2,1,0:T(8,128)(2,1)} custom-call(bf16[8,5,64,768]{3,2,1,0:T(8,128)(2,1)} %bitcast.65, bf16[2048,768]{1,0:T(8,128)(2,1)} %all-gather.6.cloned.1.call-done.w_ref.refs_1_, bf16[5,64,2048]{2,1,0:T(8,128)(2,1)} %bitcast.49, f32[5,64,2048]{2,1,0:T(8,128)} %get-tuple-element.95.refs_3_), custom_call_target="tpu_custom_call" | custom-call | flops 8053063680 | bytes 183500800 | tf_op jit(solution)/shard_map/product_scatter/pallas_call | solution.py:856
  578.4 4.5 finish.3
  582.9 1.3 convert_element_type.55
  584.2 1.5 broadcast_multiply_fusion
  585.7 1.2 reduce-scatter.8.cloned.1.call-done
  587.5 15.0 %exit_plane.1 = (bf16[8,64,768]{2,1,0:T(8,128)(2,1)}, f32[4,2,8,256]{3,2,1,0:T(8,128)}) custom-call(bf16[8,64,768]{2,1,0:T(8,128)(2,1)} %bitcast.53, f32[8,256]{1,0:T(8,128)} %broadcast_in_dim.33.gap_ref), custom_call_target="tpu_custom_call" | custom-call | tf_op jit(solution)/shard_map/exit_plane/pallas_call | solution.py:533
  602.5 2.9 finish.2
  (64 shorter events, 13.8 us)
Async XLA Ops:
  7.2 98.4 %all-gather.12.cloned.1.call-start = ((), (), s32[]{:S(2)}) async-start(), calls=%async_computation.9 | async-start | bytes 1310720 | tf_op jit(solution)/shard_map/all_gather | solution.py:1412
  9.7 95.9 %all-gather.6.cloned.1.call-start = ((), (), s32[]{:S(2)}) async-start(), calls=%async_computation.3 | async-start | bytes 3932160 | tf_op jit(solution)/shard_map/all_gather | solution.py:1319
  33.4 214.0 %all-gather.8.cloned.1.call-start = ((), (), s32[]{:S(2)}) async-start(), calls=%async_computation.4 | async-start | bytes 7208960 | tf_op jit(solution)/shard_map/all_gather | solution.py:1319
  100.4 192.6 %all-gather.10.cloned.1.call-start = ((), (), s32[]{:S(2)}) async-start(), calls=%async_computation.5 | async-start | bytes 3604480 | tf_op jit(solution)/shard_map/all_gather | solution.py:1319
  148.5 319.3 %reduce-scatter.4.cloned.1.call-start = ((), (), s32[]{:S(2)}) async-start(), calls=%async_computation.6 | async-start | bytes 3604480 | tf_op jit(solution)/shard_map/reduce_scatter | solution.py:1323
  292.8 188.9 %reduce-scatter.6.cloned.1.call-start = ((), (), s32[]{:S(2)}) async-start(), calls=%async_computation.7 | async-start | bytes 7208960 | tf_op jit(solution)/shard_map/reduce_scatter | solution.py:1323
  364.1 222.8 %reduce-scatter.8.cloned.1.call-start = ((), (), s32[]{:S(2)}) async-start(), calls=%async_computation.8 | async-start | bytes 3932160 | tf_op jit(solution)/shard_map/reduce_scatter | solution.py:1323
  364.3 104.9 %copy-start.6 = (bf16[2560,384]{1,0:T(8,128)(2,1)S(1)}, bf16[2560,384]{1,0:T(8,128)(2,1)}, u32[]{:S(2)}) copy-start(bf16[2560,384]{1,0:T(8,128)(2,1)} %get-tuple-element.71) | copy-start | bytes 5898244
  467.8 9.6 %slice-start = ((s8[11141120]{0:T(1024)(128)(4,1)}), s8[4194304]{0:T(1024)(128)(4,1)S(1)}, s32[]{:S(2)}) async-start(s8[11141120]{0:T(1024)(128)(4,1)} %bitcast.57), calls=%async_computation.10 | async-start | bytes 8388608
  469.3 8.1 %slice-start.1 = ((s8[11141120]{0:T(1024)(128)(4,1)}), s8[4194304]{0:T(1024)(128)(4,1)S(1)}, s32[]{:S(2)}) async-start(s8[11141120]{0:T(1024)(128)(4,1)} %bitcast.57), calls=%async_computation.11 | async-start | bytes 8388608
  469.3 8.0 %slice-start.2 = ((s8[11141120]{0:T(1024)(128)(4,1)}), s8[2752512]{0:T(1024)(128)(4,1)S(1)}, s32[]{:S(2)}) async-start(s8[11141120]{0:T(1024)(128)(4,1)} %bitcast.57), calls=%async_computation.12 | async-start | bytes 5505024
  469.3 8.0 %copy-start.7 = (bf16[2,2,64,2048]{3,2,1,0:T(8,128)(2,1)S(1)}, bf16[2,2,64,2048]{3,2,1,0:T(8,128)(2,1)}, u32[]{:S(2)}) copy-start(bf16[2,2,64,2048]{3,2,1,0:T(8,128)(2,1)} %get-tuple-element.72) | copy-start | bytes 3145732
  578.3 4.6 copy-start.3
  578.3 5.8 copy-start.2
  578.4 5.8 copy-start.4
  578.4 8.5 %copy-start.5 = (f32[1,256]{1,0:T(1,128)S(1)}, f32[1,256]{1,0:T(1,128)}, u32[]{:S(2)}) copy-start(f32[1,256]{1,0:T(1,128)} %get-tuple-element.102) | copy-start | bytes 3076
  582.9 23.9 %copy-start = (bf16[5,64,2048]{2,1,0:T(8,128)(2,1)S(1)}, bf16[5,64,2048]{2,1,0:T(8,128)(2,1)}, u32[]{:S(2)}) copy-start(bf16[5,64,2048]{2,1,0:T(8,128)(2,1)} %get-tuple-element.83) | copy-start | bytes 3932164
  584.2 23.7 %copy-start.1 = (bf16[5,64,2048]{2,1,0:T(8,128)(2,1)S(1)}, bf16[5,64,2048]{2,1,0:T(8,128)(2,1)}, u32[]{:S(2)}) copy-start(bf16[5,64,2048]{2,1,0:T(8,128)(2,1)} %product_scatter.7) | copy-start | bytes 3932164
Sparse Core Ops, SparseCore 0:
  10.2 31.2 all-gather.11
  43.0 62.4 all-gather.5
  107.1 105.3 all-gather.7
  213.9 57.4 all-gather.9
  292.9 54.3 reduce-scatter.3
  364.2 100.5 reduce-scatter.5
  524.2 62.6 reduce-scatter.7

commit v5 on v4

--- a/solution.py
+++ b/solution.py
@@ -75,7 +75,7 @@
     return allowed, inherits, tail, whole
 
 
-def mixer_forward_kernel(heads, cut_ref, live_ref, n_ref, w_ref, gap_ref, mixed_ref, kept_ref, qfi_ref, state):
+def mixer_forward_kernel(heads, blocks, cut_ref, n_ref, w_ref, gap_ref, mixed_ref, kept_ref, qfi_ref, state):
     step = pl.program_id(0)
     width = heads * 128
 
@@ -89,7 +89,7 @@
         chunk = step * UNROLL + u
         rows = slice(u * BLOCK, (u + 1) * BLOCK)
         at = lax.broadcasted_iota(jnp.int32, (BLOCK, 1), 0) + chunk * BLOCK
-        live = (at < live_ref[0]).astype(F32)
+        live = (at < cut_ref[0, blocks]).astype(F32)
         query_pre, sig_q, sig_nf, key, value = chunk_prep(qfi_ref[rows, :], gap_ref[...], live, width)
         query = query_pre * sig_q
         total = split_sum(lower, jnp.log1p(-key))
@@ -98,7 +98,7 @@
         scaled_q = (query * jnp.exp(total - centre)).astype(BF)
         scaled_k = (key * jnp.exp(centre - total)).astype(BF)
         value_low = value.astype(BF)
-        allowed, inherits, tail, whole = chunk_masks(cut_ref[chunk])
+        allowed, inherits, tail, whole = chunk_masks(cut_ref[chunk // blocks, lax.rem(chunk, blocks)])
         value_tail = (value * tail).astype(BF)
         e_centre = jnp.exp(centre)
         e_rest = jnp.exp(ending - centre)
@@ -120,7 +120,7 @@
         mixed_ref[rows, width:] = jnp.where(lane == 0, high, jnp.where(lane == 1, square - high, 0.0)).astype(BF)
 
 
-def mixer_backward_kernel(heads, cut_ref, live_ref, qfi_ref, gap_ref, kept_ref, grad_ref, out_ref, gap_out_ref, state):
+def mixer_backward_kernel(heads, blocks, cut_ref, qfi_ref, gap_ref, kept_ref, grad_ref, out_ref, gap_out_ref, state):
     step = pl.program_id(0)
     last = pl.num_programs(0) - 1
     width = heads * 128
@@ -136,7 +136,7 @@
         chunk = (last - step) * UNROLL + u
         rows = slice(u * BLOCK, (u + 1) * BLOCK)
         at = lax.broadcasted_iota(jnp.int32, (BLOCK, 1), 0) + chunk * BLOCK
-        live = (at < live_ref[0]).astype(F32)
+        live = (at < cut_ref[0, blocks]).astype(F32)
         gap = gap_ref[...]
         query_pre, sig_q, sig_nf, key, value = chunk_prep(qfi_ref[rows, :], gap, live, width)
         query = query_pre * sig_q
@@ -148,7 +148,7 @@
         scaled_q = (query * e_q).astype(BF)
         scaled_k = (key * e_k).astype(BF)
         value_low = value.astype(BF)
-        allowed, inherits, tail, whole = chunk_masks(cut_ref[chunk])
+        allowed, inherits, tail, whole = chunk_masks(cut_ref[chunk // blocks, lax.rem(chunk, blocks)])
         value_tail = (value * tail).astype(BF)
         grad = grad_ref[rows, :]
         grad_in = (grad.astype(F32) * inherits).astype(BF)
@@ -193,8 +193,9 @@
 
 MESH = pl.DeviceIdType.MESH
 PIECES = 5
-EARLY = 3
+EARLY = 4
 TILE = 1024
+CHUNK = 32
 VMEM_LIMIT = 60 * 1024 * 1024
 (S_X, S_Y, S_CORE, S_DIAG_Y, S_DIAG_X, S_CORE_X, S_CORE_Y, S_CORE_D, R_CORE, R_X, R_Y, R_LAST_Y, R_LAST_X, KINDS) = range(14)
 
@@ -389,130 +390,183 @@
     pl.semaphore_wait(barrier, len(devices))
 
 
-def enter_plane(weights, gain, ids, gap, per_rank, groups, planes, collective_id):
+class Line:
+    def __init__(self, place, planes, full, sems):
+        self.p, self.planes, self.full, self.sems = place, planes, full, sems
+
+    def copy(self, way, plane, to, hop):
+        send, recv = self.sems
+        block = self.full.at[plane]
+        return pltpu.make_async_remote_copy(
+            src_ref=block, dst_ref=block, send_sem=send.at[way, hop], recv_sem=recv.at[way, hop],
+            device_id=(to, self.p.me), device_id_type=MESH,
+        )
+
+    def each(self, hop, arriving, body):
+        plane, last = self.p.plane, self.planes - 1
+        if arriving:
+            conditions = (plane - hop >= 0, plane + hop <= last)
+        else:
+            conditions = ((plane - hop >= 0) & (plane + 1 <= last), (plane + hop <= last) & (plane >= 1))
+        for way, condition in enumerate(conditions):
+            @pl.when(condition)
+            def _():
+                block = plane - hop if way == 0 else plane + hop
+                to = lax.rem(plane + (1 if way == 0 else last), self.planes)
+                body(self.copy(way, block, to, hop - 1 if arriving else hop))
+
+    def start(self, hop):
+        self.each(hop, False, lambda copy: copy.start())
+
+    def arrive(self, hop):
+        self.each(hop, True, lambda copy: copy.wait_recv())
+
+    def drain(self):
+        for hop in range(self.planes - 1):
+            self.each(hop, False, lambda copy: copy.wait_send())
+
+
+def enter_plane(weights, gain, x, unit_weights, unit_gain, ids, gap, per_rank, groups, planes, collective_id):
     rows, model = weights[0].shape
     head = model // (8 * per_rank)
     channels = per_rank * head
     span = 8 // groups
-
-    def kernel(q_ref, f_ref, i_ref, gain_ref, ids_ref, gap_ref, out_ref, ids_out, gap_out, part, *sems):
-        send, recv, local, gap_send, gap_recv = sems
+    tokens = x.shape[0]
+    x_rows = tokens // PIECES
+    every_unit = unit_weights[0].shape[1]
+    units_in = every_unit // (8 * planes)
+    units = units_in * planes
+    x = x.reshape(PIECES, x_rows, model)
+    blocks = tokens // BLOCK
+
+    def kernel(q_ref, f_ref, i_ref, gain_ref, x_ref, gate_ref, up_ref, unit_gain_ref, ids_ref, gap_ref,
+               qfi_out, full, unit_out, cut_out, gap_out,
+               part, normed, unit_part, ids_in, gap_in, *sems):
+        (swap_send, swap_recv, swap_local, send, recv, local, gap_send, gap_recv, z_send, z_recv) = sems
         place = Place()
         scale = gain_ref[...]
         for w, ref in enumerate((q_ref, f_ref, i_ref)):
-            for a in range(groups):
-                for m in range(span):
-                    for j in range(per_rank):
-                        h = (m * per_rank + j) * groups + a
-                        at = w * channels + j * head
-                        part[a * span + m, :, at : at + head] = fold(scale, ref[:, h * head : (h + 1) * head])
+            for rank, source, target in ((r, t, c) for v, r, c, t in head_moves(head, per_rank, groups, span) if v == w):
+                part[rank, :, target] = fold(scale, ref[:, source])
         greet_column_and_plane(place, planes)
-        copies = swap_starts(place, [part], [out_ref], send, recv, local)
-        gaps = column_spread(place, planes, gap_ref, gap_out, gap_send, gap_recv)
-        own_gap = pltpu.make_async_copy(gap_ref, gap_out.at[place.plane, place.core], local.at[2])
-        own_gap.start()
-        own_ids = pltpu.make_async_copy(ids_ref, ids_out.at[place.me], local.at[1])
-        own_ids.start()
-        ids_copies = []
+        first = swap_starts(
+            place, [part], [qfi_out.at[place.plane]],
+            swap_send.at[pl.ds(0, 1)], swap_recv.at[pl.ds(0, 1)], swap_local.at[pl.ds(0, 1)],
+        )
+        gaps = column_spread(place, planes, gap_ref, gap_in, gap_send, gap_recv)
+        gap_in[place.plane, place.core] = gap_ref[...]
+        ids_in[place.me] = ids_ref[...]
+        id_pairs = []
         for k, flips in enumerate(FLIPS):
-            there = ids_out.at[place.rank(*flips)]
-            made = [
+            there = ids_in.at[place.rank(*flips)]
+            id_pairs.append(tuple(
                 pltpu.make_async_remote_copy(
-                    src_ref=src, dst_ref=dst, send_sem=send.at[1, k], recv_sem=recv.at[1, k],
+                    src_ref=src, dst_ref=dst, send_sem=swap_send.at[1, k], recv_sem=swap_recv.at[1, k],
                     device_id=place.device(*flips), device_id_type=MESH,
                 )
-                for src, dst in ((ids_ref, ids_out.at[place.me]), (there, there))
-            ]
-            made[0].start()
-            ids_copies.append(made)
-        swap_waits(copies)
-        for copy, arrival in ids_copies + gaps:
+                for src, dst in ((ids_ref, ids_in.at[place.me]), (there, there))
+            ))
+            id_pairs[-1][0].start()
+
+        gather = Gather(place, normed, full, (send, recv), local)
+
+        @pl.loop(0, PIECES)
+        def _(b):
+            value = x_ref[b].astype(F32)
+            normed[b] = (value * inverse_rms(row_mean(value * value))).astype(BF)
+            gather.start(b)
+
+        line = Line(place, planes, qfi_out, (z_send, z_recv))
+        swap_waits(first)
+        line.start(0)
+        unit_scale = unit_gain_ref[...]
+        for side, ref in enumerate((gate_ref, up_ref)):
+            for _, rank, target, source in (move for move in unit_moves(units, planes, 8) if move[0] == side):
+                unit_part[rank, :, target] = fold(unit_scale, ref[:, source])
+        for copy, arrival in id_pairs + gaps:
             copy.wait_send()
             arrival.wait_recv()
-        own_gap.wait()
-        own_ids.wait()
-
-    return pl.pallas_call(
+        segment = ids_in[:, 0, :].astype(F32)
+        live = jnp.sum(ids_in[:, 1, :tokens].astype(F32))
+        lane = lax.broadcasted_iota(jnp.int32, (8, EXTRA), 1)
+        parts = [segment[:, c * BLOCK : (c + 1) * BLOCK] for c in range(blocks)]
+        ends = [jnp.max(p, axis=1, keepdims=True) for p in parts]
+        begin = jnp.min(parts[0], axis=1, keepdims=True)
+        before = jnp.concatenate([begin[:1], ends[-1][:-1]], axis=0)
+        result = jnp.where(lane == blocks, live, 0.0)
+        for c in range(blocks):
+            stay = jnp.sum((parts[c] == before).astype(F32), axis=1, keepdims=True)
+            result = jnp.where(lane == c, stay, result)
+            before = ends[c]
+        cut_out[...] = result.astype(jnp.int32)
+        for j in range(per_rank):
+            for c in range(span):
+                at = (j * span + c) * rows
+                gap_out[:, at : at + rows] = gap_in[place.core * per_rank + j, c, :1, :rows].astype(F32)
+        unit_copies = []
+
+        def rest():
+            pl.loop(3, PIECES)(gather.forward)
+            unit_copies.extend(swap_starts(
+                place, [unit_part], [unit_out],
+                swap_send.at[pl.ds(2, 1)], swap_recv.at[pl.ds(2, 1)], swap_local.at[pl.ds(1, 1)],
+            ))
+
+        stages = [lambda: pl.loop(0, 3)(gather.forward), rest, lambda: pl.loop(0, PIECES)(gather.forward_last)]
+        for hop in range(1, planes):
+            if hop <= len(stages):
+                stages[hop - 1]()
+            line.arrive(hop)
+            if hop < planes - 1:
+                line.start(hop)
+        for stage in stages[planes - 1 :]:
+            stage()
+        pl.loop(0, PIECES)(gather.finish)
+        swap_waits(unit_copies)
+        line.drain()
+        pl.loop(0, PIECES)(gather.drain)
+
+    qfi, full, unit_rows, cut, gap = pl.pallas_call(
         kernel,
-        in_specs=[VMEM_SPEC] * 4 + [ANY_SPEC] * 2,
-        out_specs=[ANY_SPEC] * 3,
+        in_specs=[VMEM_SPEC] * 10,
+        out_specs=[ANY_SPEC] * 3 + [VMEM_SPEC] * 2,
         out_shape=[
-            jax.ShapeDtypeStruct((8, rows, 3 * channels), BF),
-            jax.ShapeDtypeStruct((8,) + ids.shape, ids.dtype),
-            jax.ShapeDtypeStruct((planes, 2) + gap.shape, gap.dtype),
+            jax.ShapeDtypeStruct((planes, 8, rows, 3 * channels), BF),
+            jax.ShapeDtypeStruct((8, PIECES, x_rows, model), BF),
+            jax.ShapeDtypeStruct((8, rows, 2 * units), BF),
+            jax.ShapeDtypeStruct((8, EXTRA), jnp.int32),
+            jax.ShapeDtypeStruct((1, channels), F32),
         ],
         scratch_shapes=[
             pltpu.VMEM((8, rows, 3 * channels), BF),
-            pltpu.SemaphoreType.DMA((2, 7)),
-            pltpu.SemaphoreType.DMA((2, 7)),
-            pltpu.SemaphoreType.DMA((3,)),
+            pltpu.VMEM((PIECES, x_rows, model), BF),
+            pltpu.VMEM((8, rows, 2 * units), BF),
+            pltpu.VMEM((8,) + ids.shape, ids.dtype),
+            pltpu.VMEM((planes, 2) + gap.shape, gap.dtype),
+            pltpu.SemaphoreType.DMA((3, 7)),
+            pltpu.SemaphoreType.DMA((3, 7)),
+            pltpu.SemaphoreType.DMA((2,)),
+            pltpu.SemaphoreType.DMA((KINDS, PIECES)),
+            pltpu.SemaphoreType.DMA((KINDS, PIECES)),
+            pltpu.SemaphoreType.DMA((PIECES,)),
             pltpu.SemaphoreType.DMA((2 * planes - 1,)),
             pltpu.SemaphoreType.DMA((2 * planes - 1,)),
+            pltpu.SemaphoreType.DMA((2, planes)),
+            pltpu.SemaphoreType.DMA((2, planes)),
         ],
         compiler_params=pltpu.CompilerParams(
             collective_id=collective_id, has_side_effects=True, vmem_limit_bytes=VMEM_LIMIT
         ),
+        cost_estimate=pl.CostEstimate(flops=0, bytes_accessed=200 * tokens * model, transcendentals=0),
         name="enter_plane",
-    )(*weights, gain, ids, gap)
-
-
-def gather_plane(x, w_gate, w_up, gain, planes, collective_id):
-    tokens, width = x.shape
-    rows = tokens // PIECES
-    w_rows, every_unit = w_gate.shape
-    units_in = every_unit // (8 * planes)
-    units = units_in * planes
-    x = x.reshape(PIECES, rows, width)
-
-    def kernel(x_ref, gate_ref, up_ref, gain_ref, full, out_ref, normed, part, *sems):
-        send, recv, local, swap_send, swap_recv, swap_local = sems
-        place = Place()
-        gather = Gather(place, normed, full, (send, recv), local)
-        value = x_ref[0].astype(F32)
-        normed[0] = (value * inverse_rms(row_mean(value * value))).astype(BF)
-        greet_all(place)
-        gather.start(0)
-        for b in range(1, PIECES):
-            value = x_ref[b].astype(F32)
-            normed[b] = (value * inverse_rms(row_mean(value * value))).astype(BF)
-            gather.start(b)
-        scale = gain_ref[...]
-        for side, ref in enumerate((gate_ref, up_ref)):
-            for i in range(planes):
-                for s in range(8):
-                    at = (i * 8 + s) * units_in
-                    to = side * units + i * units_in
-                    part[s, :, to : to + units_in] = fold(scale, ref[:, at : at + units_in])
-        copies = swap_starts(place, [part], [out_ref], swap_send, swap_recv, swap_local)
-        for stage in (gather.forward, gather.forward_last, gather.finish):
-            pl.loop(0, PIECES)(stage)
-        swap_waits(copies)
-        pl.loop(0, PIECES)(gather.drain)
-
-    full, swapped = pl.pallas_call(
-        kernel,
-        in_specs=[VMEM_SPEC] * 4,
-        out_specs=[ANY_SPEC] * 2,
-        out_shape=[
-            jax.ShapeDtypeStruct((8, PIECES, rows, width), BF),
-            jax.ShapeDtypeStruct((8, w_rows, 2 * units), BF),
-        ],
-        scratch_shapes=[
-            pltpu.VMEM((PIECES, rows, width), BF),
-            pltpu.VMEM((8, w_rows, 2 * units), BF),
-            pltpu.SemaphoreType.DMA((KINDS, PIECES)),
-            pltpu.SemaphoreType.DMA((KINDS, PIECES)),
-            pltpu.SemaphoreType.DMA((PIECES,)),
-            pltpu.SemaphoreType.DMA((1, 7)),
-            pltpu.SemaphoreType.DMA((1, 7)),
-            pltpu.SemaphoreType.DMA((1,)),
-        ],
-        compiler_params=pltpu.CompilerParams(
-            collective_id=collective_id, has_side_effects=True, vmem_limit_bytes=VMEM_LIMIT
-        ),
-        name="gather_plane",
-    )(x, w_gate, w_up, gain)
-    return full.reshape(8 * tokens, width), swapped
+    )(*weights, gain, x, *unit_weights, unit_gain, ids, gap)
+    return (
+        qfi.reshape(model, 3 * channels),
+        full.reshape(8 * tokens, model),
+        unit_rows,
+        cut,
+        gap,
+    )
 
 
 def exit_plane(summed, gap_grad, planes, collective_id):
@@ -639,7 +693,7 @@
             pltpu.VMEM((PIECES, rows, right), BF),
             pltpu.VMEM((PIECES, rows, right), BF),
             pltpu.SemaphoreType.DMA((PIECES,)),
-            pltpu.SemaphoreType.DMA((1,)),
+            pltpu.SemaphoreType.DMA((2,)),
         ]
 
     def bind(self, place, sems, left_ref, weight_ref, refs):
@@ -648,8 +702,12 @@
          self.keep_a, self.keep_b, self.last_y_out, self.last_y_in, self.last_x_out,
          self.last_x_in, self.load_sem, self.w_sem) = refs
 
-    def weight_copy(self):
-        return pltpu.make_async_copy(self.weight_ref, self.w_buf, self.w_sem.at[0])
+    def weight_copy(self, t):
+        tile = min(TILE, self.width)
+        at = pl.ds(t * tile, tile)
+        if self.transposed:
+            return pltpu.make_async_copy(self.weight_ref.at[at], self.w_buf.at[at], self.w_sem.at[t])
+        return pltpu.make_async_copy(self.weight_ref.at[:, at], self.w_buf.at[:, at], self.w_sem.at[t])
 
     def start_loads(self):
         core = self.place.core
@@ -660,7 +718,8 @@
                         self.left_ref.at[at, b], self.x_buf.at[b, side + j], self.load_sem.at[b]
                     ).start()
             if b == 0:
-                self.weight_copy().start()
+                for t in range(self.width // min(TILE, self.width)):
+                    self.weight_copy(t).start()
 
     def send_core(self, b):
         return remote(self.core_out.at[b], self.core_in.at[b], self.sems, R_CORE, b, self.place.device(0, 0, 1))
@@ -688,6 +747,10 @@
             return out.reshape(4, rows, tile), at
 
         for t in range(width // tile):
+            @pl.when(b == 0)
+            def _():
+                self.weight_copy(t).wait()
+
             out, at = product(0, t)
             self.core_out[b, :, :, at] = out.astype(BF)
         if self.stats:
@@ -699,38 +762,60 @@
         if self.stats:
             self.total[:, :, width:] = self.x_buf[b, 4:, :, depth:].astype(F32)
 
+    def by_chunks(self, body):
+        @pl.loop(0, self.rows // CHUNK)
+        def _(r):
+            body(pl.ds(pl.multiple_of(r * CHUNK, CHUNK), CHUNK))
+
     def stage_one(self, b):
         place, half, total, core_in = self.place, self.half, self.total, self.core_in
         self.send_core(b).wait_recv()
-        for i in range(2):
-            go, stay = 2 * i + 1 - place.x, 2 * i + place.x
-            self.x_out[b, i] = (total[go, :, :half] + core_in[b, go, :, :half].astype(F32)).astype(BF)
-            self.keep_a[b, i] = total[stay, :, :half] + core_in[b, stay, :, :half].astype(F32)
+
+        def for_x(r):
+            for i in range(2):
+                go, stay = 2 * i + 1 - place.x, 2 * i + place.x
+                self.x_out[b, i, r] = (total[go, r, :half] + core_in[b, go, r, :half].astype(F32)).astype(BF)
+                self.keep_a[b, i, r] = total[stay, r, :half] + core_in[b, stay, r, :half].astype(F32)
+
+        def for_y(r):
+            for i in range(2):
+                go, stay = 2 * (1 - place.y) + i, 2 * place.y + i
+                self.y_out[b, i, r] = (total[go, r, half:] + core_in[b, go, r, half:].astype(F32)).astype(BF)
+                self.keep_b[b, i, r] = total[stay, r, half:] + core_in[b, stay, r, half:].astype(F32)
+
+        self.by_chunks(for_x)
         self.send_x(b).start()
-        for i in range(2):
-            go, stay = 2 * (1 - place.y) + i, 2 * place.y + i
-            self.y_out[b, i] = (total[go, :, half:] + core_in[b, go, :, half:].astype(F32)).astype(BF)
-            self.keep_b[b, i] = total[stay, :, half:] + core_in[b, stay, :, half:].astype(F32)
+        self.by_chunks(for_y)
         self.send_y(b).start()
 
     def stage_two(self, b):
+        go_y, go_x = 1 - self.place.y, 1 - self.place.x
+
+        def low(r):
+            self.last_y_out[b, r] = (self.keep_a[b, go_y, r] + self.x_in[b, go_y, r].astype(F32)).astype(BF)
+
+        def high(r):
+            self.last_x_out[b, r] = (self.keep_b[b, go_x, r] + self.y_in[b, go_x, r].astype(F32)).astype(BF)
+
         self.send_x(b).wait_recv()
-        go = 1 - self.place.y
-        self.last_y_out[b] = (self.keep_a[b, go] + self.x_in[b, go].astype(F32)).astype(BF)
+        self.by_chunks(low)
         self.send_last_y(b).start()
         self.send_y(b).wait_recv()
-        go = 1 - self.place.x
-        self.last_x_out[b] = (self.keep_b[b, go] + self.y_in[b, go].astype(F32)).astype(BF)
+        self.by_chunks(high)
         self.send_last_x(b).start()
 
-    def stage_three(self, b):
+    def stage_three(self, b, body):
         self.send_last_y(b).wait_recv()
         self.send_last_x(b).wait_recv()
         y, x = self.place.y, self.place.x
-        low = self.keep_a[b, y] + self.x_in[b, y].astype(F32) + self.last_y_in[b].astype(F32)
-        high = self.keep_b[b, x] + self.y_in[b, x].astype(F32) + self.last_x_in[b].astype(F32)
-        result = jnp.concatenate([low, high[:, : self.half]], axis=1)
-        return result, (high[:, self.half :] if self.stats else None)
+
+        def end(r):
+            low = self.keep_a[b, y, r] + self.x_in[b, y, r].astype(F32) + self.last_y_in[b, r].astype(F32)
+            high = self.keep_b[b, x, r] + self.y_in[b, x, r].astype(F32) + self.last_x_in[b, r].astype(F32)
+            result = jnp.concatenate([low, high[:, : self.half]], axis=1)
+            body(r, result, high[:, self.half :] if self.stats else None)
+
+        self.by_chunks(end)
 
     def drain(self, b):
         for copy in (self.send_core, self.send_x, self.send_y, self.send_last_y, self.send_last_x):
@@ -792,18 +877,18 @@
             gather = Gather(place, n_buf, full_ref, sems, keep_sem)
 
         def end(b):
-            result, stat = scatter.stage_three(b)
-            written, sent = epilogue(result, stat, *[r[b] for r in own_bufs])
-            for buf, value in zip(out_bufs, written):
-                buf[b] = value
+            def rows_done(r, result, stat):
+                written, sent = epilogue(result, stat, *[o[b, r] for o in own_bufs])
+                for buf, value in zip(out_bufs, written):
+                    buf[b, r] = value
+                if gathered:
+                    n_buf[b, r] = sent
+
+            scatter.stage_three(b, rows_done)
             for copy in out_copies(b):
                 copy.start()
             if gathered:
-                n_buf[b] = sent
                 gather.start(b)
-
-        scatter.weight_copy().wait()
-
         @pl.loop(0, PIECES + (9 if gathered else 5))
         def _(step):
             guarded(scatter.stage_one, step - 1)
@@ -966,15 +1051,16 @@
     )
 
 
-def mixer_forward(cut, live, n1, weight, gap, own, out_pieces, per_rank, collective_id):
+def mixer_forward(cut, n1, weight, gap, own, out_pieces, per_rank, collective_id):
     tokens, heads = n1.shape[0], gap.shape[1] // 128
     width = heads * 128
+    blocks = tokens // BLOCK // lax.axis_size("seq")
     steps, qfi_spec, gap_spec, kept_spec, block = mixer_specs(tokens, heads, False)
     together = lax.axis_size("seq") == 8
 
-    def kernel(cut_ref, live_ref, n_ref, w_ref, gap_ref, *refs):
+    def kernel(cut_ref, n_ref, w_ref, gap_ref, *refs):
         if not together:
-            return mixer_forward_kernel(heads, cut_ref, live_ref, n_ref, w_ref, gap_ref, *refs)
+            return mixer_forward_kernel(heads, blocks, cut_ref, n_ref, w_ref, gap_ref, *refs)
         (own_ref, pieces_ref, mixed_ref, kept_ref, qfi_ref, full_ref, rows_ref, state, own_buf, pieces_buf, send, recv, local,
          w_send, w_recv, w_local) = refs
         place = Place()
@@ -1013,8 +1099,12 @@
                 here.start()
                 there.start()
 
+        @pl.when(pl.program_id(0) == steps - 1)
+        def _():
+            pl.loop(0, EARLY)(gather.forward_last)
+
         mixer_forward_kernel(
-            heads, cut_ref, live_ref, n_ref, w_ref, gap_ref, mixed_ref, kept_ref, qfi_ref, state
+            heads, blocks, cut_ref, n_ref, w_ref, gap_ref, mixed_ref, kept_ref, qfi_ref, state
         )
 
         for b in range(EARLY):
@@ -1024,7 +1114,7 @@
 
         @pl.when(pl.program_id(0) == steps - 1)
         def _():
-            for stage in (gather.forward_last, gather.finish, gather.drain):
+            for stage in (gather.finish, gather.drain):
                 pl.loop(0, EARLY)(stage)
             for j in range(per_rank):
                 here, there, arrival = exchange(j)
@@ -1061,7 +1151,7 @@
     results = pl.pallas_call(
         kernel,
         grid_spec=pltpu.PrefetchScalarGridSpec(
-            num_scalar_prefetch=2, grid=(steps,), in_specs=in_specs, out_specs=out_specs, scratch_shapes=scratch
+            num_scalar_prefetch=1, grid=(steps,), in_specs=in_specs, out_specs=out_specs, scratch_shapes=scratch
         ),
         out_shape=out_shape,
         compiler_params=params,
@@ -1071,23 +1161,24 @@
             transcendentals=tokens * width * 6,
         ),
         name="mixer_forward",
-    )(cut, live, *args)
+    )(cut, *args)
     mixed, kept, qfi = results[:3]
     if together:
         return mixed, kept, qfi, results[3], results[4].reshape(width, model)
     return mixed, kept, qfi, lax.all_gather(own, "seq", axis=0, tiled=True), None
 
 
-def mixer_backward(cut, live, qfi, gap, kept, grad, parts, grad_out, per_rank, collective_id):
+def mixer_backward(cut, qfi, gap, kept, grad, parts, grad_out, per_rank, collective_id):
     tokens, heads = qfi.shape[0], gap.shape[1] // 128
     width = heads * 128
+    blocks = tokens // BLOCK // lax.axis_size("seq")
     steps, qfi_spec, gap_spec, kept_spec, block = mixer_specs(tokens, heads, True)
     together = lax.axis_size("seq") == 8
     planes = lax.axis_size("dp")
 
-    def kernel(cut_ref, live_ref, qfi_ref, gap_ref, kept_ref, grad_ref, *refs):
+    def kernel(cut_ref, qfi_ref, gap_ref, kept_ref, grad_ref, *refs):
         if not together:
-            return mixer_backward_kernel(heads, cut_ref, live_ref, qfi_ref, gap_ref, kept_ref, grad_ref, *refs)
+            return mixer_backward_kernel(heads, blocks, cut_ref, qfi_ref, gap_ref, kept_ref, grad_ref, *refs)
         (parts_ref, og_ref, out_ref, gap_out_ref, swapped_ref, sum_ref, state, parts_buf, og_buf, by_plane, landed,
          send, recv, local, c_send, c_recv, z_send, z_recv, load_sem) = refs
         place, step = Place(), pl.program_id(0)
@@ -1144,7 +1235,7 @@
                 over_planes(hop)[0].start()
 
         mixer_backward_kernel(
-            heads, cut_ref, live_ref, qfi_ref, gap_ref, kept_ref, grad_ref, out_ref, gap_out_ref, state
+            heads, blocks, cut_ref, qfi_ref, gap_ref, kept_ref, grad_ref, out_ref, gap_out_ref, state
         )
 
         @pl.when(step == steps - 1)
@@ -1192,7 +1283,7 @@
     return pl.pallas_call(
         kernel,
         grid_spec=pltpu.PrefetchScalarGridSpec(
-            num_scalar_prefetch=2, grid=(steps,), in_specs=in_specs, out_specs=out_specs, scratch_shapes=scratch
+            num_scalar_prefetch=1, grid=(steps,), in_specs=in_specs, out_specs=out_specs, scratch_shapes=scratch
         ),
         out_shape=out_shape,
         compiler_params=params,
@@ -1200,7 +1291,7 @@
             flops=tokens * width * 128 * 24, bytes_accessed=tokens * width * 28, transcendentals=tokens * width * 6
         ),
         name="mixer_backward",
-    )(cut, live, *args)
+    )(cut, *args)
 
 
 def feed_forward_kernel(units, n_ref, gu_ref, units_ref, act_ref, slope_ref, gate_w, up_w):
@@ -1218,10 +1309,55 @@
     slope_ref[...] = (up * sig * (1.0 + gate * (1.0 - sig))).astype(BF)
 
 
-def feed_backward_kernel(units, g_ref, down_ref, act_ref, slope_ref, grad_ref):
-    d_units = nt(g_ref[...], down_ref[...])
+def add_up(total, product, out_ref):
+    step = pl.program_id(0)
+
+    @pl.when(step == 0)
+    def _():
+        total[...] = product
+
+    @pl.when(step > 0)
+    def _():
+        total[...] += product
+
+    @pl.when(step == pl.num_programs(0) - 1)
+    def _():
+        out_ref[...] = total[...].astype(BF)
+
+
+def feed_backward_kernel(units, g_ref, units_ref, down_ref, act_ref, slope_ref, grad_ref, down_grad_ref, g_all, u_all, sem, u_sem):
+    step, steps = pl.program_id(0), pl.num_programs(0)
+    blocks, rows, model = g_all.shape
+    u_copy = pltpu.make_async_copy(units_ref, u_all, u_sem.at[0])
+
+    def load(b):
+        return pltpu.make_async_copy(g_ref.at[b], g_all.at[b], sem.at[b])
+
+    @pl.when(step == 0)
+    def _():
+        for b in range(blocks):
+            load(b).start()
+        u_copy.start()
+
+    load(step).wait()
+    d_units = nt(g_all[step], down_ref[...])
     grad_ref[:, :units] = (d_units * slope_ref[...].astype(F32)).astype(BF)
     grad_ref[:, units:] = (d_units * act_ref[...].astype(F32)).astype(BF)
+
+    @pl.when(step == steps - 1)
+    def _():
+        u_copy.wait()
+        for at in range(0, model, 1024):
+            cols = slice(at, at + 1024)
+            down_grad_ref[:, cols] = tn(u_all[...], g_all[:, :, cols].reshape(blocks * rows, 1024)).astype(BF)
+
+
+def output_backward_kernel(model, width, d_ref, mixed_ref, out_ref, d_mixed_ref, grad_ref, total):
+    d_attn = d_ref[:, :model]
+    mixed = mixed_ref[:, :width]
+    beta = jnp.sum(d_ref[:, model:].astype(F32), axis=1, keepdims=True)
+    d_mixed_ref[...] = (nt(d_attn, out_ref[...]) - beta * mixed.astype(F32)).astype(BF)
+    add_up(total, tn(mixed, d_attn), grad_ref)
 
 
 def fixed_block(shape):
@@ -1253,15 +1389,19 @@
             load.wait()
             pl.loop(EARLY, PIECES)(gather.start)
 
-        feed_forward_kernel(units, n_ref, gu_ref, units_ref, act_ref, slope_ref, gate_w, up_w)
-
-        @pl.when(step == min(3, steps - 1))
+        @pl.when(step == min(2, steps - 1))
         def _():
             pl.loop(EARLY, PIECES)(gather.forward)
 
         @pl.when(step == steps - 1)
         def _():
-            for stage in (gather.forward_last, gather.finish, gather.drain):
+            pl.loop(EARLY, PIECES)(gather.forward_last)
+
+        feed_forward_kernel(units, n_ref, gu_ref, units_ref, act_ref, slope_ref, gate_w, up_w)
+
+        @pl.when(step == steps - 1)
+        def _():
+            for stage in (gather.finish, gather.drain):
                 pl.loop(EARLY, PIECES)(stage)
 
     in_specs, args = [row_block(model), fixed_block(gu.shape)], [n2, gu]
@@ -1298,21 +1438,45 @@
     return results[0], results[1], results[2], full
 
 
-def feed_backward(grad, down, act, slope):
+def feed_backward(grad, down, hidden_units, act, slope):
     tokens, model = grad.shape
     units = down.shape[0]
+    blocks = tokens // 512
     return pl.pallas_call(
         functools.partial(feed_backward_kernel, units),
-        grid=(tokens // 512,),
-        in_specs=[row_block(model), fixed_block(down.shape), row_block(units), row_block(units)],
-        out_specs=row_block(2 * units),
-        out_shape=jax.ShapeDtypeStruct((tokens, 2 * units), BF),
+        grid=(blocks,),
+        in_specs=[ANY_SPEC, ANY_SPEC, fixed_block(down.shape)] + [row_block(units)] * 2,
+        out_specs=[row_block(2 * units), fixed_block(down.shape)],
+        out_shape=[jax.ShapeDtypeStruct((tokens, 2 * units), BF), jax.ShapeDtypeStruct(down.shape, BF)],
+        scratch_shapes=[
+            pltpu.VMEM((blocks, 512, model), BF),
+            pltpu.VMEM((tokens, units), BF),
+            pltpu.SemaphoreType.DMA((blocks,)),
+            pltpu.SemaphoreType.DMA((1,)),
+        ],
         compiler_params=pltpu.CompilerParams(vmem_limit_bytes=VMEM_LIMIT),
         cost_estimate=pl.CostEstimate(
-            flops=2 * tokens * model * units, bytes_accessed=8 * tokens * model, transcendentals=0
+            flops=4 * tokens * model * units, bytes_accessed=8 * tokens * model, transcendentals=0
         ),
         name="feed_backward",
-    )(grad, down, act, slope)
+    )(grad.reshape(blocks, 512, model), hidden_units, down, act, slope)
+
+
+def output_backward(d_attn, mixed, weight):
+    tokens, (width, model) = mixed.shape[0], weight.shape
+    return pl.pallas_call(
+        functools.partial(output_backward_kernel, model, width),
+        grid=(tokens // 512,),
+        in_specs=[row_block(d_attn.shape[1]), row_block(mixed.shape[1]), fixed_block(weight.shape)],
+        out_specs=[row_block(width), fixed_block(weight.shape)],
+        out_shape=[jax.ShapeDtypeStruct((tokens, width), BF), jax.ShapeDtypeStruct(weight.shape, BF)],
+        scratch_shapes=[pltpu.VMEM(weight.shape, F32)],
+        compiler_params=pltpu.CompilerParams(vmem_limit_bytes=VMEM_LIMIT),
+        cost_estimate=pl.CostEstimate(
+            flops=4 * tokens * model * width, bytes_accessed=3 * tokens * model, transcendentals=0
+        ),
+        name="output_backward",
+    )(d_attn, mixed, weight)
 
 
 def gather_dp(v):
@@ -1412,39 +1576,34 @@
     out_pieces = lax.all_gather(fold(gain_o, w_output), "dp", axis=0)
     if plain:
         qfi_part = jnp.concatenate([to_heads(fold(gain_a, w)) for w in mixer_weights], axis=2)
-        qfi_swapped = swap_seq(qfi_part)
+        qfi_full = gather_dp(swap_seq(qfi_part).reshape(ranks * rows, 3 * channels))
         gu_part = jnp.concatenate([to_units(fold(gain_f, w)) for w in (w_gate, w_up)], axis=2)
         gu_swapped = swap_seq(gu_part)
         x = x16.astype(F32)
         normed = (x * inverse_rms(row_mean(x * x))).astype(BF)
         n1 = lax.all_gather(normed, "seq", axis=0, tiled=True)
         gap_pieces = lax.all_gather(gate_gap, "dp", axis=0)
-        gap_own = swap_group(own_rows(gap_pieces)).transpose(1, 0, 2)
+        gap_own = swap_group(own_rows(gap_pieces)).transpose(1, 0, 2).reshape(1, channels).astype(F32)
         ids = lax.all_gather(ids, "seq", axis=0)
+        segment = ids[:, 0].reshape(tokens // BLOCK, BLOCK)
+        live = jnp.sum(ids[:, 1]).reshape(1)
+        ends = segment[:, -1]
+        before = jnp.concatenate([segment[:1, 0], ends[:-1]])
+        cut = jnp.sum((segment == before[:, None]).astype(jnp.int32), axis=1).reshape(ranks, -1)
+        cut = jnp.concatenate([cut, jnp.broadcast_to(live, (ranks, 1))], axis=1)
+        cut = jnp.pad(cut, ((0, 0), (0, EXTRA - cut.shape[1])))
     else:
         wide = -(-row_tokens // 128) * 128
         ids = jnp.pad(ids, ((0, 6), (0, wide - row_tokens)))
         gap_tile = jnp.pad(gate_gap[None], ((0, 15), (0, 128 - rows)))
-        qfi_swapped, ids, gap_all = enter_plane(
-            mixer_weights, gain_a, ids, gap_tile, per_rank, groups, planes, 1
+        qfi_full, n1, gu_swapped, cut, gap_own = enter_plane(
+            mixer_weights, gain_a, x16, (w_gate, w_up), gain_f, ids, gap_tile, per_rank, groups, planes, 1
         )
-        ids = ids[:, :2, :row_tokens]
-        mine = lax.rem(lax.axis_index("seq"), 2) * per_rank
-        gap_own = lax.dynamic_slice_in_dim(gap_all[:, :, 0, :rows], mine, per_rank, axis=0)
-        x16, qfi_swapped = order(x16, qfi_swapped)
-        n1, gu_swapped = gather_plane(x16, w_gate, w_up, gain_f, planes, 2)
-    qfi_full = gather_dp(qfi_swapped.reshape(ranks * rows, 3 * channels))
     gu_full = gather_dp(gu_swapped.reshape(ranks * rows, 2 * units))
-    gap_own = gap_own.reshape(1, channels).astype(F32)
-    segment = ids[:, 0].reshape(tokens // BLOCK, BLOCK)
-    live = jnp.sum(ids[:, 1]).reshape(1)
-    ends = segment[:, -1]
-    before = jnp.concatenate([segment[:1, 0], ends[:-1]])
-    cut = jnp.sum((segment == before[:, None]).astype(jnp.int32), axis=1)
 
     og16 = out_grad[0]
     mixed, kept, qfi, grad_all, out_own = mixer_forward(
-        cut, live, n1, qfi_full, gap_own, og16, out_pieces, per_rank, 3
+        cut, n1, qfi_full, gap_own, og16, out_pieces, per_rank, 3
     )
     if plain:
         out_own = swap_group(own_rows(out_pieces)).transpose(1, 0, 2, 3).reshape(channels, model)
@@ -1465,10 +1624,8 @@
     def after_down(result, stat, middle):
         return [(middle + result).astype(BF)], None
 
-    grad_down = tn(hidden_units, grad_all).astype(BF)
+    d_gu, grad_down = feed_backward(grad_all, down_own, hidden_units, act, slope)
     down_sum = scatter_dp(grad_down)
-    act, _ = order(act, grad_down)
-    d_gu = feed_backward(grad_all, down_own, act, slope)
     block_out, grad_gu = product_all(
         hidden_units, down_own, False, False, after_down, [middle], [(model, BF)], 0, 6,
         (GradProduct(n2, d_gu, False, 0),),
@@ -1489,21 +1646,16 @@
         d_gu, gu_full, True, False, after_ffn, [middle, og16, x16, factor_o], [(model, F32)], model + EXTRA, 5
     )
     d_attn, down_sum = order(d_attn, down_sum)
-    beta = jnp.sum(d_attn[:, model:].astype(F32), axis=1, keepdims=True)
-    d_attn = d_attn[:, :model]
-
-    mixed = mixed[:, :channels]
-    grad_out = tn(mixed, d_attn).astype(BF)
-    d_mixed = (nt(d_attn, out_own) - beta * mixed.astype(F32)).astype(BF)
+    d_mixed, grad_out = output_backward(d_attn, mixed, out_own)
     grad_out, d_mixed = order(grad_out, d_mixed)
     if plain:
-        d_qfi, gap_grad = mixer_backward(cut, live, qfi, gap_own, kept, d_mixed, None, None, per_rank, 6)
+        d_qfi, gap_grad = mixer_backward(cut, qfi, gap_own, kept, d_mixed, None, None, per_rank, 6)
         out_back = grad_out.reshape(per_rank, span, rows, model).transpose(1, 0, 2, 3)
         out_rows = scatter_dp(swap_group(out_back).reshape(planes * rows, model)).astype(F32)
         gu_rows = swap_seq(gu_sum).reshape(ranks, rows, 2 * units)
     else:
         d_qfi, gap_grad, gu_rows, out_rows = mixer_backward(
-            cut, live, qfi, gap_own, kept, d_mixed, gu_sum.reshape(ranks, rows, 2 * units),
+            cut, qfi, gap_own, kept, d_mixed, gu_sum.reshape(ranks, rows, 2 * units),
             grad_out.reshape(per_rank, span, rows, model), per_rank, 9,
         )
     grad_qfi = tn(n1, d_qfi).astype(BF)

time: 621 us -> 605 us (0.974)
  matrix products: 38.8 us -> 13.6 us
  Pallas kernels: 539 us -> 550 us
    dot_general x4 -> x1, matrix products: 38.8 us -> 13.6 us  [dot(): return lax.dot_general(a, b, (dims, ((), ())), preferred_element_type=F32)]
    pallas_call x3, Pallas kernels: 101 us -> 119 us  [the longest x1 83.9 us: enter_plane(): pl.pallas_call(kernel, in_specs=[VMEM_SPEC] * 10, out_specs=[ANY_SPEC] *...]
  transfers between devices with their start and end apart: 7 -> 6, of which waited for: 1 -> 1; matrix products, arithmetic and copies ran while one was open for 6% -> 1% of each run, Pallas kernels for 80% -> 81%
where the time goes in v5:
time: 605 us; the launch traced here: 595 us
  Pallas kernels  550 us (91%)
  between operations  14.7 us (2%)
  matrix products  13.6 us (2%)
  other arithmetic  8.08 us (1%)
  local copies, waits for them, and re-layouts  6.6 us (1%)
    pallas_call x4, Pallas kernels, product_scatter(): pl.pallas_call(kernel, in_specs=in_specs, out_specs=out_specs, out_shape=...  308 us
    pallas_call x1, Pallas kernels, enter_plane(): pl.pallas_call(kernel, in_specs=[VMEM_SPEC] * 10, out_specs=[ANY_SPEC] *...  83.9 us
    pallas_call x1, Pallas kernels, mixer_forward(): pl.pallas_call(kernel, grid_spec=pltpu.PrefetchScalarGridSpec(num_scalar_...  45.4 us
    pallas_call x1, Pallas kernels, mixer_backward(): pl.pallas_call(kernel, grid_spec=pltpu.PrefetchScalarGridSpec(num_scalar_...  27.9 us
    pallas_call x1, Pallas kernels, feed_forward(): pl.pallas_call(kernel, grid=(steps,), in_specs=in_specs, out_specs=out_sp...  27.1 us
    pallas_call x1, Pallas kernels, feed_backward(): pl.pallas_call(functools.partial(feed_backward_kernel, units), grid=(bloc...  24.2 us
    pallas_call x1, Pallas kernels, exit_plane(): pl.pallas_call(kernel, in_specs=[ANY_SPEC] * 2, out_specs=[ANY_SPEC] * 2,...  14.7 us
    dot_general x1, matrix products, dot(): return lax.dot_general(a, b, (dims, ((), ())), preferred_element_type=F32)  13.6 us
  transfers between devices with their start and end apart: 6, of which 1 were waited for; matrix products, arithmetic and copies ran while one was open for 1% of the time, Pallas kernels for 81%

profile of v5, /device:TPU:0, one launch (start us, length us, event | category | flops | bytes accessed | tf_op | source)
XLA Modules:
  0.0 595.2 jit_solution(13847799469477480709)
XLA Ops:
  7.9 1.8 fusion
  11.7 0.7 copy.30.unit_gain_ref.refs_1_
  12.5 0.7 pad_add_fusion
  13.8 1.3 pad.9.gap_ref
  15.0 83.9 %enter_plane.1 = (bf16[4,8,64,768]{3,2,1,0:T(8,128)(2,1)}, bf16[8,5,64,2048]{3,2,1,0:T(8,128)(2,1)}, bf16[8,64,1408]{2,1,0:T(8,128)(2,1)}, s32[8,128]{1,0:T(8,128)}, f32[1,256]{1,0:T(1,128)}) custom-call(bf16[64,2048]{1,0:T(8,128)(2,1)} %refs_2_.2, bf16[64,2048]{1,0:T(8,128)(2,1)} %refs_3_.2, bf16[64,2048]{1,0:T(8,128)(2,1)} %refs_4_.1, ...), custom_call_target="tpu_custom_call" | custom-call | bytes 131072000 | tf_op jit(solution)/shard_map/enter_plane/pallas_call | solution.py:529
  99.1 45.4 %mixer_forward.1 = (bf16[2560,384]{1,0:T(8,128)(2,1)}, bf16[40,2,128,128]{3,2,1,0:T(8,128)(2,1)}, f32[2560,768]{1,0:T(8,128)}, bf16[8,5,64,2048]{3,2,1,0:T(8,128)(2,1)}, bf16[2,2,64,2048]{3,2,1,0:T(8,128)(2,1)}) custom-call(s32[8,128]{1,0:T(8,128)} %get-tuple-element.65.cut_ref, bf16[2560,2048]{1,0:T(8,128)(2,1)} %bitcast.46, bf16[2048,768]{1,0:T(8,128)(2,1)} %bitcast.49, ...), custom_call_target="tpu_custom_call" | custom-call | flops 8891924480 | bytes 314572800 | tf_op jit(solution)/shard_map/mixer_forward/pallas_call | solution.py:1151
  144.8 96.8 %product_scatter.4 = (f32[5,64,2048]{2,1,0:T(8,128)}, f32[5,64,128]{2,1,0:T(8,128)}, bf16[8,5,64,2048]{3,2,1,0:T(8,128)(2,1)}) custom-call(bf16[8,5,64,384]{3,2,1,0:T(8,128)(2,1)} %bitcast.63, bf16[256,2048]{1,0:T(8,128)(2,1)} %bitcast.64, bf16[5,64,2048]{2,1,0:T(8,128)(2,1)} %bitcast.37), custom_call_target="tpu_custom_call" | custom-call | flops 2684354560 | bytes 314572800 | tf_op jit(solution)/shard_map/product_scatter/pallas_call | solution.py:941
  241.6 27.1 %feed_forward.1 = (bf16[2560,704]{1,0:T(8,128)(2,1)}, bf16[2560,704]{1,0:T(8,128)(2,1)}, bf16[2560,704]{1,0:T(8,128)(2,1)}, bf16[8,5,64,2048]{3,2,1,0:T(8,128)(2,1)}) custom-call(bf16[2560,2048]{1,0:T(8,128)(2,1)} %bitcast.58, bf16[2048,1408]{1,0:T(8,128)(2,1)} %all-gather.5.cloned.1.call-done.gu_ref.refs_1_, ...), custom_call_target="tpu_custom_call", output_to_operand_aliasing={{3}: (3, {})} | custom-call | flops 14763950080 | bytes 20971520 | tf_op jit(solution)/shard_map/feed_forward/pallas_call | solution.py:1422
  268.8 24.2 %feed_backward.1 = (bf16[2560,1408]{1,0:T(8,128)(2,1)}, bf16[704,2048]{1,0:T(8,128)(2,1)}) custom-call(bf16[5,512,2048]{2,1,0:T(8,128)(2,1)} %bitcast.60, bf16[2560,704]{1,0:T(8,128)(2,1)} %get-tuple-element.75.units_ref, bf16[704,2048]{1,0:T(8,128)(2,1)} %all-gather.7.cloned.1.call-done.down_ref.refs_1_, bf16[2560,704]{1,0:T(8,128)(2,1)} %get-tuple-element.79.act_ref, ...), custom_call_target="tpu_custom_call" | custom-call | flops 14763950080 | bytes 41943040 | tf_op jit(solution)/shard_map/feed_backward/pallas_call | solution.py:1445
  293.3 55.7 %product_scatter.5 = (bf16[5,64,2048]{2,1,0:T(8,128)(2,1)}, bf16[2048,1408]{1,0:T(8,128)(2,1)}) custom-call(bf16[8,5,64,704]{3,2,1,0:T(8,128)(2,1)} %bitcast.62, bf16[704,2048]{1,0:T(8,128)(2,1)} %all-gather.7.cloned.1.call-done.down_ref.refs_1_, f32[5,64,2048]{2,1,0:T(8,128)} %get-tuple-element.77.refs_2_, bf16[2560,1408]{1,0:T(8,128)(2,1)} %get-tuple-element.86.refs_3_, ...), custom_call_target="tpu_custom_call" | custom-call | flops 7381975040 | bytes 183500800 | tf_op jit(solution)/shard_map/product_scatter/pallas_call | solution.py:941
  349.1 101.6 %product_scatter.6 = (f32[5,64,2048]{2,1,0:T(8,128)}, bf16[8,5,64,2176]{3,2,1,0:T(8,128)(2,1)}) custom-call(bf16[8,5,64,1408]{3,2,1,0:T(8,128)(2,1)} %bitcast.61, bf16[2048,1408]{1,0:T(8,128)(2,1)} %all-gather.5.cloned.1.call-done.gu_ref.refs_1_, f32[5,64,2048]{2,1,0:T(8,128)} %get-tuple-element.77.refs_2_, bf16[5,64,2048]{2,1,0:T(8,128)(2,1)} %bitcast.53, ...), custom_call_target="tpu_custom_call" | custom-call | flops 14763950080 | bytes 314572800 | tf_op jit(solution)/shard_map/product_scatter/pallas_call | solution.py:941
  450.7 11.3 %output_backward.1 = (bf16[2560,256]{1,0:T(8,128)(2,1)}, bf16[256,2048]{1,0:T(8,128)(2,1)}) custom-call(bf16[2560,2176]{1,0:T(8,128)(2,1)} %bitcast.57, bf16[2560,384]{1,0:T(8,128)(2,1)} %get-tuple-element.70.mixed_ref, bf16[256,2048]{1,0:T(8,128)(2,1)} %bitcast.65), custom_call_target="tpu_custom_call" | custom-call | flops 5368709120 | bytes 15728640 | tf_op jit(solution)/shard_map/output_backward/pallas_call | solution.py:1467
  462.0 27.9 %mixer_backward.1 = (bf16[2560,768]{1,0:T(8,128)(2,1)}, f32[1,256]{1,0:T(1,128)}, bf16[8,64,1408]{2,1,0:T(8,128)(2,1)}, f32[64,2048]{1,0:T(8,128)}) custom-call(s32[8,128]{1,0:T(8,128)} %get-tuple-element.65.cut_ref, f32[2560,768]{1,0:T(8,128)} %get-tuple-element.83.qfi_ref, f32[1,256]{1,0:T(1,128)} %get-tuple-element.68.gap_ref, ...), custom_call_target="tpu_custom_call" | custom-call | flops 2013265920 | bytes 18350080 | tf_op jit(solution)/shard_map/mixer_backward/pallas_call | solution.py:1283
  489.9 13.6 %convolution_convert_fusion = bf16[2048,768]{1,0:T(8,128)(2,1)} fusion(bf16[2560,2048]{1,0:T(8,128)(2,1)} %bitcast.47, bf16[2560,768]{1,0:T(8,128)(2,1)} %get-tuple-element.96), kind=kOutput, calls=%fused_computation | convolution fusion | flops 8054636544 | bytes 17563648 | tf_op jit(solution)/shard_map/dot_general | solution.py:20
  503.6 53.8 %product_scatter.7 = bf16[5,64,2048]{2,1,0:T(8,128)(2,1)} custom-call(bf16[8,5,64,768]{3,2,1,0:T(8,128)(2,1)} %bitcast.48, bf16[2048,768]{1,0:T(8,128)(2,1)} %bitcast.50, bf16[5,64,2048]{2,1,0:T(8,128)(2,1)} %bitcast.39, f32[5,64,2048]{2,1,0:T(8,128)} %get-tuple-element.97.refs_3_), custom_call_target="tpu_custom_call" | custom-call | flops 8053063680 | bytes 183500800 | tf_op jit(solution)/shard_map/product_scatter/pallas_call | solution.py:941
  557.4 4.5 finish.3
  562.0 1.3 convert_element_type.24
  563.2 1.5 broadcast_multiply_fusion
  564.7 1.5 reduce-scatter.8.cloned.1.call-done
  566.8 14.7 %exit_plane.1 = (bf16[8,64,768]{2,1,0:T(8,128)(2,1)}, f32[4,2,8,256]{3,2,1,0:T(8,128)}) custom-call(bf16[8,64,768]{2,1,0:T(8,128)(2,1)} %bitcast.43, f32[8,256]{1,0:T(8,128)} %broadcast_in_dim.31.gap_ref), custom_call_target="tpu_custom_call" | custom-call | tf_op jit(solution)/shard_map/exit_plane/pallas_call | solution.py:587
  581.5 2.9 finish.2
  584.4 0.9 slice_reduce_fusion
  585.8 1.1 copy.36
  586.9 1.1 copy.37
  (36 shorter events, 5.3 us)
Async XLA Ops:
  7.2 91.9 %all-gather.9.cloned.1.call-start = ((), (), s32[]{:S(2)}) async-start(), calls=%async_computation.8 | async-start | bytes 1310720 | tf_op jit(solution)/shard_map/all_gather | solution.py:1576
  9.7 231.9 %all-gather.5.cloned.1.call-start = ((), (), s32[]{:S(2)}) async-start(), calls=%async_computation.3 | async-start | bytes 7208960 | tf_op jit(solution)/shard_map/all_gather | solution.py:1483
  99.0 169.8 %all-gather.7.cloned.1.call-start = ((), (), s32[]{:S(2)}) async-start(), calls=%async_computation.4 | async-start | bytes 3604480 | tf_op jit(solution)/shard_map/all_gather | solution.py:1483
  144.5 306.2 %reduce-scatter.4.cloned.1.call-start = ((), (), s32[]{:S(2)}) async-start(), calls=%async_computation.5 | async-start | bytes 3604480 | tf_op jit(solution)/shard_map/reduce_scatter | solution.py:1487
  293.0 169.0 %reduce-scatter.6.cloned.1.call-start = ((), (), s32[]{:S(2)}) async-start(), calls=%async_computation.6 | async-start | bytes 7208960 | tf_op jit(solution)/shard_map/reduce_scatter | solution.py:1487
  349.0 217.2 %reduce-scatter.8.cloned.1.call-start = ((), (), s32[]{:S(2)}) async-start(), calls=%async_computation.7 | async-start | bytes 3932160 | tf_op jit(solution)/shard_map/reduce_scatter | solution.py:1487
  557.4 4.6 copy-start.3
  557.4 5.8 copy-start.2
  557.4 5.8 copy-start.4
  557.4 8.8 %copy-start.5 = (f32[1,256]{1,0:T(1,128)S(1)}, f32[1,256]{1,0:T(1,128)}, u32[]{:S(2)}) copy-start(f32[1,256]{1,0:T(1,128)} %get-tuple-element.104) | copy-start | bytes 3076
  562.0 23.9 %copy-start = (bf16[5,64,2048]{2,1,0:T(8,128)(2,1)S(1)}, bf16[5,64,2048]{2,1,0:T(8,128)(2,1)}, u32[]{:S(2)}) copy-start(bf16[5,64,2048]{2,1,0:T(8,128)(2,1)} %get-tuple-element.82) | copy-start | bytes 3932164
  563.2 23.7 %copy-start.1 = (bf16[5,64,2048]{2,1,0:T(8,128)(2,1)S(1)}, bf16[5,64,2048]{2,1,0:T(8,128)(2,1)}, u32[]{:S(2)}) copy-start(bf16[5,64,2048]{2,1,0:T(8,128)(2,1)} %product_scatter.7) | copy-start | bytes 3932164
Sparse Core Ops, SparseCore 0:
  10.2 33.6 all-gather.8
  99.1 105.6 all-gather.4
  206.4 57.4 all-gather.6
  293.2 54.6 reduce-scatter.3
  350.0 102.0 reduce-scatter.5
  503.6 62.5 reduce-scatter.7

commit v6 on v5

--- a/solution.py
+++ b/solution.py
@@ -483,6 +483,10 @@
         for side, ref in enumerate((gate_ref, up_ref)):
             for _, rank, target, source in (move for move in unit_moves(units, planes, 8) if move[0] == side):
                 unit_part[rank, :, target] = fold(unit_scale, ref[:, source])
+        unit_copies = swap_starts(
+            place, [unit_part], [unit_out],
+            swap_send.at[pl.ds(2, 1)], swap_recv.at[pl.ds(2, 1)], swap_local.at[pl.ds(1, 1)],
+        )
         for copy, arrival in id_pairs + gaps:
             copy.wait_send()
             arrival.wait_recv()
@@ -503,16 +507,8 @@
             for c in range(span):
                 at = (j * span + c) * rows
                 gap_out[:, at : at + rows] = gap_in[place.core * per_rank + j, c, :1, :rows].astype(F32)
-        unit_copies = []
-
-        def rest():
-            pl.loop(3, PIECES)(gather.forward)
-            unit_copies.extend(swap_starts(
-                place, [unit_part], [unit_out],
-                swap_send.at[pl.ds(2, 1)], swap_recv.at[pl.ds(2, 1)], swap_local.at[pl.ds(1, 1)],
-            ))
-
-        stages = [lambda: pl.loop(0, 3)(gather.forward), rest, lambda: pl.loop(0, PIECES)(gather.forward_last)]
+        stages = [lambda: pl.loop(0, 3)(gather.forward), lambda: pl.loop(3, PIECES)(gather.forward)]
+        stages += [lambda: pl.loop(0, PIECES)(gather.forward_last)]
         for hop in range(1, planes):
             if hop <= len(stages):
                 stages[hop - 1]()
@@ -693,7 +689,7 @@
             pltpu.VMEM((PIECES, rows, right), BF),
             pltpu.VMEM((PIECES, rows, right), BF),
             pltpu.SemaphoreType.DMA((PIECES,)),
-            pltpu.SemaphoreType.DMA((2,)),
+            pltpu.SemaphoreType.DMA((1,)),
         ]
 
     def bind(self, place, sems, left_ref, weight_ref, refs):
@@ -702,12 +698,8 @@
          self.keep_a, self.keep_b, self.last_y_out, self.last_y_in, self.last_x_out,
          self.last_x_in, self.load_sem, self.w_sem) = refs
 
-    def weight_copy(self, t):
-        tile = min(TILE, self.width)
-        at = pl.ds(t * tile, tile)
-        if self.transposed:
-            return pltpu.make_async_copy(self.weight_ref.at[at], self.w_buf.at[at], self.w_sem.at[t])
-        return pltpu.make_async_copy(self.weight_ref.at[:, at], self.w_buf.at[:, at], self.w_sem.at[t])
+    def weight_copy(self):
+        return pltpu.make_async_copy(self.weight_ref, self.w_buf, self.w_sem.at[0])
 
     def start_loads(self):
         core = self.place.core
@@ -718,8 +710,7 @@
                         self.left_ref.at[at, b], self.x_buf.at[b, side + j], self.load_sem.at[b]
                     ).start()
             if b == 0:
-                for t in range(self.width // min(TILE, self.width)):
-                    self.weight_copy(t).start()
+                self.weight_copy().start()
 
     def send_core(self, b):
         return remote(self.core_out.at[b], self.core_in.at[b], self.sems, R_CORE, b, self.place.device(0, 0, 1))
@@ -747,10 +738,6 @@
             return out.reshape(4, rows, tile), at
 
         for t in range(width // tile):
-            @pl.when(b == 0)
-            def _():
-                self.weight_copy(t).wait()
-
             out, at = product(0, t)
             self.core_out[b, :, :, at] = out.astype(BF)
         if self.stats:
@@ -889,6 +876,8 @@
                 copy.start()
             if gathered:
                 gather.start(b)
+        scatter.weight_copy().wait()
+
         @pl.loop(0, PIECES + (9 if gathered else 5))
         def _(step):
             guarded(scatter.stage_one, step - 1)
@@ -1325,31 +1314,12 @@
         out_ref[...] = total[...].astype(BF)
 
 
-def feed_backward_kernel(units, g_ref, units_ref, down_ref, act_ref, slope_ref, grad_ref, down_grad_ref, g_all, u_all, sem, u_sem):
-    step, steps = pl.program_id(0), pl.num_programs(0)
-    blocks, rows, model = g_all.shape
-    u_copy = pltpu.make_async_copy(units_ref, u_all, u_sem.at[0])
-
-    def load(b):
-        return pltpu.make_async_copy(g_ref.at[b], g_all.at[b], sem.at[b])
-
-    @pl.when(step == 0)
-    def _():
-        for b in range(blocks):
-            load(b).start()
-        u_copy.start()
-
-    load(step).wait()
-    d_units = nt(g_all[step], down_ref[...])
+def feed_backward_kernel(units, g_ref, down_ref, units_ref, act_ref, slope_ref, grad_ref, down_grad_ref, total):
+    grad = g_ref[...]
+    d_units = nt(grad, down_ref[...])
     grad_ref[:, :units] = (d_units * slope_ref[...].astype(F32)).astype(BF)
     grad_ref[:, units:] = (d_units * act_ref[...].astype(F32)).astype(BF)
-
-    @pl.when(step == steps - 1)
-    def _():
-        u_copy.wait()
-        for at in range(0, model, 1024):
-            cols = slice(at, at + 1024)
-            down_grad_ref[:, cols] = tn(u_all[...], g_all[:, :, cols].reshape(blocks * rows, 1024)).astype(BF)
+    add_up(total, tn(units_ref[...], grad), down_grad_ref)
 
 
 def output_backward_kernel(model, width, d_ref, mixed_ref, out_ref, d_mixed_ref, grad_ref, total):
@@ -1441,25 +1411,19 @@
 def feed_backward(grad, down, hidden_units, act, slope):
     tokens, model = grad.shape
     units = down.shape[0]
-    blocks = tokens // 512
     return pl.pallas_call(
         functools.partial(feed_backward_kernel, units),
-        grid=(blocks,),
-        in_specs=[ANY_SPEC, ANY_SPEC, fixed_block(down.shape)] + [row_block(units)] * 2,
+        grid=(tokens // 512,),
+        in_specs=[row_block(model), fixed_block(down.shape)] + [row_block(units)] * 3,
         out_specs=[row_block(2 * units), fixed_block(down.shape)],
         out_shape=[jax.ShapeDtypeStruct((tokens, 2 * units), BF), jax.ShapeDtypeStruct(down.shape, BF)],
-        scratch_shapes=[
-            pltpu.VMEM((blocks, 512, model), BF),
-            pltpu.VMEM((tokens, units), BF),
-            pltpu.SemaphoreType.DMA((blocks,)),
-            pltpu.SemaphoreType.DMA((1,)),
-        ],
+        scratch_shapes=[pltpu.VMEM(down.shape, F32)],
         compiler_params=pltpu.CompilerParams(vmem_limit_bytes=VMEM_LIMIT),
         cost_estimate=pl.CostEstimate(
             flops=4 * tokens * model * units, bytes_accessed=8 * tokens * model, transcendentals=0
         ),
         name="feed_backward",
-    )(grad.reshape(blocks, 512, model), hidden_units, down, act, slope)
+    )(grad, down, hidden_units, act, slope)
 
 
 def output_backward(d_attn, mixed, weight):

time: 605 us -> 598 us (0.988); the launches traced: 595 us -> 597 us
  no operation moved by 1% of the time
where the time goes in v6:
time: 598 us; the launch traced here: 597 us
  Pallas kernels  552 us (92%)
  between operations  14.3 us (2%)
  matrix products  13.6 us (2%)
  other arithmetic  8.08 us (1%)
  local copies, waits for them, and re-layouts  6.6 us (1%)
    pallas_call x4, Pallas kernels, product_scatter(): pl.pallas_call(kernel, in_specs=in_specs, out_specs=out_specs, out_shape=...  309 us
    pallas_call x1, Pallas kernels, enter_plane(): pl.pallas_call(kernel, in_specs=[VMEM_SPEC] * 10, out_specs=[ANY_SPEC] *...  83.9 us
    pallas_call x1, Pallas kernels, mixer_forward(): pl.pallas_call(kernel, grid_spec=pltpu.PrefetchScalarGridSpec(num_scalar_...  45.4 us
    pallas_call x1, Pallas kernels, mixer_backward(): pl.pallas_call(kernel, grid_spec=pltpu.PrefetchScalarGridSpec(num_scalar_...  27.9 us
    pallas_call x1, Pallas kernels, feed_forward(): pl.pallas_call(kernel, grid=(steps,), in_specs=in_specs, out_specs=out_sp...  27 us
    pallas_call x1, Pallas kernels, feed_backward(): pl.pallas_call(functools.partial(feed_backward_kernel, units), grid=(toke...  25.4 us
    pallas_call x1, Pallas kernels, exit_plane(): pl.pallas_call(kernel, in_specs=[ANY_SPEC] * 2, out_specs=[ANY_SPEC] * 2,...  14.9 us
    dot_general x1, matrix products, dot(): return lax.dot_general(a, b, (dims, ((), ())), preferred_element_type=F32)  13.6 us
  transfers between devices with their start and end apart: 6, of which 1 were waited for; matrix products, arithmetic and copies ran while one was open for 1% of the time, Pallas kernels for 81%

profile of v6, /device:TPU:0, one launch (start us, length us, event | category | flops | bytes accessed | tf_op | source)
XLA Modules:
  0.0 597.1 jit_solution(1550782788969362327)
XLA Ops:
  7.9 1.8 fusion
  10.4 0.7 copy.29.gain_ref.refs_1_
  11.7 0.7 copy.30.unit_gain_ref.refs_1_
  13.8 1.3 pad.9.gap_ref
  15.0 83.9 %enter_plane.1 = (bf16[4,8,64,768]{3,2,1,0:T(8,128)(2,1)}, bf16[8,5,64,2048]{3,2,1,0:T(8,128)(2,1)}, bf16[8,64,1408]{2,1,0:T(8,128)(2,1)}, s32[8,128]{1,0:T(8,128)}, f32[1,256]{1,0:T(1,128)}) custom-call(bf16[64,2048]{1,0:T(8,128)(2,1)} %refs_2_.2, bf16[64,2048]{1,0:T(8,128)(2,1)} %refs_3_.2, bf16[64,2048]{1,0:T(8,128)(2,1)} %refs_4_.1, ...), custom_call_target="tpu_custom_call" | custom-call | bytes 131072000 | tf_op jit(solution)/shard_map/enter_plane/pallas_call | solution.py:525
  99.1 45.4 %mixer_forward.1 = (bf16[2560,384]{1,0:T(8,128)(2,1)}, bf16[40,2,128,128]{3,2,1,0:T(8,128)(2,1)}, f32[2560,768]{1,0:T(8,128)}, bf16[8,5,64,2048]{3,2,1,0:T(8,128)(2,1)}, bf16[2,2,64,2048]{3,2,1,0:T(8,128)(2,1)}) custom-call(s32[8,128]{1,0:T(8,128)} %get-tuple-element.65.cut_ref, bf16[2560,2048]{1,0:T(8,128)(2,1)} %bitcast.46, bf16[2048,768]{1,0:T(8,128)(2,1)} %bitcast.49, ...), custom_call_target="tpu_custom_call" | custom-call | flops 8891924480 | bytes 314572800 | tf_op jit(solution)/shard_map/mixer_forward/pallas_call | solution.py:1140
  144.8 96.8 %product_scatter.4 = (f32[5,64,2048]{2,1,0:T(8,128)}, f32[5,64,128]{2,1,0:T(8,128)}, bf16[8,5,64,2048]{3,2,1,0:T(8,128)(2,1)}) custom-call(bf16[8,5,64,384]{3,2,1,0:T(8,128)(2,1)} %bitcast.63, bf16[256,2048]{1,0:T(8,128)(2,1)} %bitcast.64, bf16[5,64,2048]{2,1,0:T(8,128)(2,1)} %bitcast.37), custom_call_target="tpu_custom_call" | custom-call | flops 2684354560 | bytes 314572800 | tf_op jit(solution)/shard_map/product_scatter/pallas_call | solution.py:930
  241.6 27.0 %feed_forward.1 = (bf16[2560,704]{1,0:T(8,128)(2,1)}, bf16[2560,704]{1,0:T(8,128)(2,1)}, bf16[2560,704]{1,0:T(8,128)(2,1)}, bf16[8,5,64,2048]{3,2,1,0:T(8,128)(2,1)}) custom-call(bf16[2560,2048]{1,0:T(8,128)(2,1)} %bitcast.58, bf16[2048,1408]{1,0:T(8,128)(2,1)} %all-gather.5.cloned.1.call-done.gu_ref.refs_1_, ...), custom_call_target="tpu_custom_call", output_to_operand_aliasing={{3}: (3, {})} | custom-call | flops 14763950080 | bytes 20971520 | tf_op jit(solution)/shard_map/feed_forward/pallas_call | solution.py:1392
  268.7 25.4 %feed_backward.1 = (bf16[2560,1408]{1,0:T(8,128)(2,1)}, bf16[704,2048]{1,0:T(8,128)(2,1)}) custom-call(bf16[2560,2048]{1,0:T(8,128)(2,1)} %bitcast.60, bf16[704,2048]{1,0:T(8,128)(2,1)} %all-gather.7.cloned.1.call-done.down_ref.refs_1_, bf16[2560,704]{1,0:T(8,128)(2,1)} %get-tuple-element.75.units_ref, bf16[2560,704]{1,0:T(8,128)(2,1)} %get-tuple-element.79.act_ref, ...), custom_call_target="tpu_custom_call" | custom-call | flops 14763950080 | bytes 41943040 | tf_op jit(solution)/shard_map/feed_backward/pallas_call | solution.py:1414
  294.1 55.7 %product_scatter.5 = (bf16[5,64,2048]{2,1,0:T(8,128)(2,1)}, bf16[2048,1408]{1,0:T(8,128)(2,1)}) custom-call(bf16[8,5,64,704]{3,2,1,0:T(8,128)(2,1)} %bitcast.62, bf16[704,2048]{1,0:T(8,128)(2,1)} %all-gather.7.cloned.1.call-done.down_ref.refs_1_, f32[5,64,2048]{2,1,0:T(8,128)} %get-tuple-element.77.refs_2_, bf16[2560,1408]{1,0:T(8,128)(2,1)} %get-tuple-element.86.refs_3_, ...), custom_call_target="tpu_custom_call" | custom-call | flops 7381975040 | bytes 183500800 | tf_op jit(solution)/shard_map/product_scatter/pallas_call | solution.py:930
  350.1 102.7 %product_scatter.6 = (f32[5,64,2048]{2,1,0:T(8,128)}, bf16[8,5,64,2176]{3,2,1,0:T(8,128)(2,1)}) custom-call(bf16[8,5,64,1408]{3,2,1,0:T(8,128)(2,1)} %bitcast.61, bf16[2048,1408]{1,0:T(8,128)(2,1)} %all-gather.5.cloned.1.call-done.gu_ref.refs_1_, f32[5,64,2048]{2,1,0:T(8,128)} %get-tuple-element.77.refs_2_, bf16[5,64,2048]{2,1,0:T(8,128)(2,1)} %bitcast.53, ...), custom_call_target="tpu_custom_call" | custom-call | flops 14763950080 | bytes 314572800 | tf_op jit(solution)/shard_map/product_scatter/pallas_call | solution.py:930
  452.8 11.2 %output_backward.1 = (bf16[2560,256]{1,0:T(8,128)(2,1)}, bf16[256,2048]{1,0:T(8,128)(2,1)}) custom-call(bf16[2560,2176]{1,0:T(8,128)(2,1)} %bitcast.57, bf16[2560,384]{1,0:T(8,128)(2,1)} %get-tuple-element.70.mixed_ref, bf16[256,2048]{1,0:T(8,128)(2,1)} %bitcast.65), custom_call_target="tpu_custom_call" | custom-call | flops 5368709120 | bytes 15728640 | tf_op jit(solution)/shard_map/output_backward/pallas_call | solution.py:1431
  464.0 27.9 %mixer_backward.1 = (bf16[2560,768]{1,0:T(8,128)(2,1)}, f32[1,256]{1,0:T(1,128)}, bf16[8,64,1408]{2,1,0:T(8,128)(2,1)}, f32[64,2048]{1,0:T(8,128)}) custom-call(s32[8,128]{1,0:T(8,128)} %get-tuple-element.65.cut_ref, f32[2560,768]{1,0:T(8,128)} %get-tuple-element.83.qfi_ref, f32[1,256]{1,0:T(1,128)} %get-tuple-element.68.gap_ref, ...), custom_call_target="tpu_custom_call" | custom-call | flops 2013265920 | bytes 18350080 | tf_op jit(solution)/shard_map/mixer_backward/pallas_call | solution.py:1272
  492.0 13.6 %convolution_convert_fusion = bf16[2048,768]{1,0:T(8,128)(2,1)} fusion(bf16[2560,2048]{1,0:T(8,128)(2,1)} %bitcast.47, bf16[2560,768]{1,0:T(8,128)(2,1)} %get-tuple-element.96), kind=kOutput, calls=%fused_computation | convolution fusion | flops 8054636544 | bytes 17563648 | tf_op jit(solution)/shard_map/dot_general | solution.py:20
  505.6 54.0 %product_scatter.7 = bf16[5,64,2048]{2,1,0:T(8,128)(2,1)} custom-call(bf16[8,5,64,768]{3,2,1,0:T(8,128)(2,1)} %bitcast.48, bf16[2048,768]{1,0:T(8,128)(2,1)} %bitcast.50, bf16[5,64,2048]{2,1,0:T(8,128)(2,1)} %bitcast.39, f32[5,64,2048]{2,1,0:T(8,128)} %get-tuple-element.97.refs_3_), custom_call_target="tpu_custom_call" | custom-call | flops 8053063680 | bytes 183500800 | tf_op jit(solution)/shard_map/product_scatter/pallas_call | solution.py:930
  559.7 4.5 finish.3
  564.2 1.3 convert_element_type.24
  565.4 1.5 broadcast_multiply_fusion
  567.0 1.4 reduce-scatter.8.cloned.1.call-done
  568.9 14.9 %exit_plane.1 = (bf16[8,64,768]{2,1,0:T(8,128)(2,1)}, f32[4,2,8,256]{3,2,1,0:T(8,128)}) custom-call(bf16[8,64,768]{2,1,0:T(8,128)(2,1)} %bitcast.43, f32[8,256]{1,0:T(8,128)} %broadcast_in_dim.31.gap_ref), custom_call_target="tpu_custom_call" | custom-call | tf_op jit(solution)/shard_map/exit_plane/pallas_call | solution.py:583
  583.8 2.9 finish.2
  586.7 0.9 slice_reduce_fusion
  588.2 1.1 copy.36
  589.2 1.1 copy.37
  (36 shorter events, 5.3 us)
Async XLA Ops:
  7.2 91.9 %all-gather.9.cloned.1.call-start = ((), (), s32[]{:S(2)}) async-start(), calls=%async_computation.8 | async-start | bytes 1310720 | tf_op jit(solution)/shard_map/all_gather | solution.py:1540
  9.7 231.9 %all-gather.5.cloned.1.call-start = ((), (), s32[]{:S(2)}) async-start(), calls=%async_computation.3 | async-start | bytes 7208960 | tf_op jit(solution)/shard_map/all_gather | solution.py:1447
  99.0 169.7 %all-gather.7.cloned.1.call-start = ((), (), s32[]{:S(2)}) async-start(), calls=%async_computation.4 | async-start | bytes 3604480 | tf_op jit(solution)/shard_map/all_gather | solution.py:1447
  144.5 308.3 %reduce-scatter.4.cloned.1.call-start = ((), (), s32[]{:S(2)}) async-start(), calls=%async_computation.5 | async-start | bytes 3604480 | tf_op jit(solution)/shard_map/reduce_scatter | solution.py:1451
  294.1 170.0 %reduce-scatter.6.cloned.1.call-start = ((), (), s32[]{:S(2)}) async-start(), calls=%async_computation.6 | async-start | bytes 7208960 | tf_op jit(solution)/shard_map/reduce_scatter | solution.py:1451
  349.8 218.5 %reduce-scatter.8.cloned.1.call-start = ((), (), s32[]{:S(2)}) async-start(), calls=%async_computation.7 | async-start | bytes 3932160 | tf_op jit(solution)/shard_map/reduce_scatter | solution.py:1451
  559.6 4.6 copy-start.3
  559.6 5.8 copy-start.2
  559.6 5.8 copy-start.4
  559.6 8.7 %copy-start.5 = (f32[1,256]{1,0:T(1,128)S(1)}, f32[1,256]{1,0:T(1,128)}, u32[]{:S(2)}) copy-start(f32[1,256]{1,0:T(1,128)} %get-tuple-element.104) | copy-start | bytes 3076
  564.2 24.0 %copy-start = (bf16[5,64,2048]{2,1,0:T(8,128)(2,1)S(1)}, bf16[5,64,2048]{2,1,0:T(8,128)(2,1)}, u32[]{:S(2)}) copy-start(bf16[5,64,2048]{2,1,0:T(8,128)(2,1)} %get-tuple-element.82) | copy-start | bytes 3932164
  565.4 23.8 %copy-start.1 = (bf16[5,64,2048]{2,1,0:T(8,128)(2,1)S(1)}, bf16[5,64,2048]{2,1,0:T(8,128)(2,1)}, u32[]{:S(2)}) copy-start(bf16[5,64,2048]{2,1,0:T(8,128)(2,1)} %product_scatter.7) | copy-start | bytes 3932164
Sparse Core Ops, SparseCore 0:
  10.2 33.6 all-gather.8
  99.1 105.6 all-gather.4
  206.4 57.4 all-gather.6
  294.2 54.8 reduce-scatter.3
  351.2 102.0 reduce-scatter.5
  505.7 62.5 reduce-scatter.7

commit v7 on v6

--- a/solution.py
+++ b/solution.py
@@ -689,7 +689,7 @@
             pltpu.VMEM((PIECES, rows, right), BF),
             pltpu.VMEM((PIECES, rows, right), BF),
             pltpu.SemaphoreType.DMA((PIECES,)),
-            pltpu.SemaphoreType.DMA((1,)),
+            pltpu.SemaphoreType.DMA((2,)),
         ]
 
     def bind(self, place, sems, left_ref, weight_ref, refs):
@@ -698,8 +698,12 @@
          self.keep_a, self.keep_b, self.last_y_out, self.last_y_in, self.last_x_out,
          self.last_x_in, self.load_sem, self.w_sem) = refs
 
-    def weight_copy(self):
-        return pltpu.make_async_copy(self.weight_ref, self.w_buf, self.w_sem.at[0])
+    def weight_copy(self, t):
+        tile = min(TILE, self.width)
+        at = pl.ds(t * tile, tile)
+        if self.transposed:
+            return pltpu.make_async_copy(self.weight_ref.at[at], self.w_buf.at[at], self.w_sem.at[t])
+        return pltpu.make_async_copy(self.weight_ref.at[:, at], self.w_buf.at[:, at], self.w_sem.at[t])
 
     def start_loads(self):
         core = self.place.core
@@ -710,7 +714,8 @@
                         self.left_ref.at[at, b], self.x_buf.at[b, side + j], self.load_sem.at[b]
                     ).start()
             if b == 0:
-                self.weight_copy().start()
+                for t in range(self.width // min(TILE, self.width)):
+                    self.weight_copy(t).start()
 
     def send_core(self, b):
         return remote(self.core_out.at[b], self.core_in.at[b], self.sems, R_CORE, b, self.place.device(0, 0, 1))
@@ -738,6 +743,10 @@
             return out.reshape(4, rows, tile), at
 
         for t in range(width // tile):
+            @pl.when(b == 0)
+            def _():
+                self.weight_copy(t).wait()
+
             out, at = product(0, t)
             self.core_out[b, :, :, at] = out.astype(BF)
         if self.stats:
@@ -876,8 +885,6 @@
                 copy.start()
             if gathered:
                 gather.start(b)
-        scatter.weight_copy().wait()
-
         @pl.loop(0, PIECES + (9 if gathered else 5))
         def _(step):
             guarded(scatter.stage_one, step - 1)

time: 598 us -> 597 us (level)
  no operation moved by 1% of the time
where the time goes in v7:
time: 597 us; the launch traced here: 596 us
  Pallas kernels  551 us (92%)
  between operations  14.3 us (2%)
  matrix products  13.6 us (2%)
  other arithmetic  8.08 us (1%)
  local copies, waits for them, and re-layouts  6.6 us (1%)
    pallas_call x4, Pallas kernels, product_scatter(): pl.pallas_call(kernel, in_specs=in_specs, out_specs=out_specs, out_shape=...  308 us
    pallas_call x1, Pallas kernels, enter_plane(): pl.pallas_call(kernel, in_specs=[VMEM_SPEC] * 10, out_specs=[ANY_SPEC] *...  83.9 us
    pallas_call x1, Pallas kernels, mixer_forward(): pl.pallas_call(kernel, grid_spec=pltpu.PrefetchScalarGridSpec(num_scalar_...  45.4 us
    pallas_call x1, Pallas kernels, mixer_backward(): pl.pallas_call(kernel, grid_spec=pltpu.PrefetchScalarGridSpec(num_scalar_...  27.9 us
    pallas_call x1, Pallas kernels, feed_forward(): pl.pallas_call(kernel, grid=(steps,), in_specs=in_specs, out_specs=out_sp...  27.1 us
    pallas_call x1, Pallas kernels, feed_backward(): pl.pallas_call(functools.partial(feed_backward_kernel, units), grid=(toke...  25.4 us
    pallas_call x1, Pallas kernels, exit_plane(): pl.pallas_call(kernel, in_specs=[ANY_SPEC] * 2, out_specs=[ANY_SPEC] * 2,...  14.7 us
    dot_general x1, matrix products, dot(): return lax.dot_general(a, b, (dims, ((), ())), preferred_element_type=F32)  13.6 us
  transfers between devices with their start and end apart: 6, of which 1 were waited for; matrix products, arithmetic and copies ran while one was open for 1% of the time, Pallas kernels for 81%

profile of v7, /device:TPU:0, one launch (start us, length us, event | category | flops | bytes accessed | tf_op | source)
XLA Modules:
  0.0 596.0 jit_solution(6364868810705259886)
XLA Ops:
  7.9 1.8 fusion
  10.4 0.7 copy.29.gain_ref.refs_1_
  11.7 0.7 copy.30.unit_gain_ref.refs_1_
  13.8 1.3 pad.9.gap_ref
  15.0 83.9 %enter_plane.1 = (bf16[4,8,64,768]{3,2,1,0:T(8,128)(2,1)}, bf16[8,5,64,2048]{3,2,1,0:T(8,128)(2,1)}, bf16[8,64,1408]{2,1,0:T(8,128)(2,1)}, s32[8,128]{1,0:T(8,128)}, f32[1,256]{1,0:T(1,128)}) custom-call(bf16[64,2048]{1,0:T(8,128)(2,1)} %refs_2_.2, bf16[64,2048]{1,0:T(8,128)(2,1)} %refs_3_.2, bf16[64,2048]{1,0:T(8,128)(2,1)} %refs_4_.1, ...), custom_call_target="tpu_custom_call" | custom-call | bytes 131072000 | tf_op jit(solution)/shard_map/enter_plane/pallas_call | solution.py:525
  99.1 45.4 %mixer_forward.1 = (bf16[2560,384]{1,0:T(8,128)(2,1)}, bf16[40,2,128,128]{3,2,1,0:T(8,128)(2,1)}, f32[2560,768]{1,0:T(8,128)}, bf16[8,5,64,2048]{3,2,1,0:T(8,128)(2,1)}, bf16[2,2,64,2048]{3,2,1,0:T(8,128)(2,1)}) custom-call(s32[8,128]{1,0:T(8,128)} %get-tuple-element.65.cut_ref, bf16[2560,2048]{1,0:T(8,128)(2,1)} %bitcast.46, bf16[2048,768]{1,0:T(8,128)(2,1)} %bitcast.49, ...), custom_call_target="tpu_custom_call" | custom-call | flops 8891924480 | bytes 314572800 | tf_op jit(solution)/shard_map/mixer_forward/pallas_call | solution.py:1147
  144.8 96.8 %product_scatter.4 = (f32[5,64,2048]{2,1,0:T(8,128)}, f32[5,64,128]{2,1,0:T(8,128)}, bf16[8,5,64,2048]{3,2,1,0:T(8,128)(2,1)}) custom-call(bf16[8,5,64,384]{3,2,1,0:T(8,128)(2,1)} %bitcast.63, bf16[256,2048]{1,0:T(8,128)(2,1)} %bitcast.64, bf16[5,64,2048]{2,1,0:T(8,128)(2,1)} %bitcast.37), custom_call_target="tpu_custom_call" | custom-call | flops 2684354560 | bytes 314572800 | tf_op jit(solution)/shard_map/product_scatter/pallas_call | solution.py:937
  241.6 27.1 %feed_forward.1 = (bf16[2560,704]{1,0:T(8,128)(2,1)}, bf16[2560,704]{1,0:T(8,128)(2,1)}, bf16[2560,704]{1,0:T(8,128)(2,1)}, bf16[8,5,64,2048]{3,2,1,0:T(8,128)(2,1)}) custom-call(bf16[2560,2048]{1,0:T(8,128)(2,1)} %bitcast.58, bf16[2048,1408]{1,0:T(8,128)(2,1)} %all-gather.5.cloned.1.call-done.gu_ref.refs_1_, ...), custom_call_target="tpu_custom_call", output_to_operand_aliasing={{3}: (3, {})} | custom-call | flops 14763950080 | bytes 20971520 | tf_op jit(solution)/shard_map/feed_forward/pallas_call | solution.py:1399
  268.8 25.4 %feed_backward.1 = (bf16[2560,1408]{1,0:T(8,128)(2,1)}, bf16[704,2048]{1,0:T(8,128)(2,1)}) custom-call(bf16[2560,2048]{1,0:T(8,128)(2,1)} %bitcast.60, bf16[704,2048]{1,0:T(8,128)(2,1)} %all-gather.7.cloned.1.call-done.down_ref.refs_1_, bf16[2560,704]{1,0:T(8,128)(2,1)} %get-tuple-element.75.units_ref, bf16[2560,704]{1,0:T(8,128)(2,1)} %get-tuple-element.79.act_ref, ...), custom_call_target="tpu_custom_call" | custom-call | flops 14763950080 | bytes 41943040 | tf_op jit(solution)/shard_map/feed_backward/pallas_call | solution.py:1421
  294.5 55.6 %product_scatter.5 = (bf16[5,64,2048]{2,1,0:T(8,128)(2,1)}, bf16[2048,1408]{1,0:T(8,128)(2,1)}) custom-call(bf16[8,5,64,704]{3,2,1,0:T(8,128)(2,1)} %bitcast.62, bf16[704,2048]{1,0:T(8,128)(2,1)} %all-gather.7.cloned.1.call-done.down_ref.refs_1_, f32[5,64,2048]{2,1,0:T(8,128)} %get-tuple-element.77.refs_2_, bf16[2560,1408]{1,0:T(8,128)(2,1)} %get-tuple-element.86.refs_3_, ...), custom_call_target="tpu_custom_call" | custom-call | flops 7381975040 | bytes 183500800 | tf_op jit(solution)/shard_map/product_scatter/pallas_call | solution.py:937
  350.2 101.7 %product_scatter.6 = (f32[5,64,2048]{2,1,0:T(8,128)}, bf16[8,5,64,2176]{3,2,1,0:T(8,128)(2,1)}) custom-call(bf16[8,5,64,1408]{3,2,1,0:T(8,128)(2,1)} %bitcast.61, bf16[2048,1408]{1,0:T(8,128)(2,1)} %all-gather.5.cloned.1.call-done.gu_ref.refs_1_, f32[5,64,2048]{2,1,0:T(8,128)} %get-tuple-element.77.refs_2_, bf16[5,64,2048]{2,1,0:T(8,128)(2,1)} %bitcast.53, ...), custom_call_target="tpu_custom_call" | custom-call | flops 14763950080 | bytes 314572800 | tf_op jit(solution)/shard_map/product_scatter/pallas_call | solution.py:937
  451.9 11.3 %output_backward.1 = (bf16[2560,256]{1,0:T(8,128)(2,1)}, bf16[256,2048]{1,0:T(8,128)(2,1)}) custom-call(bf16[2560,2176]{1,0:T(8,128)(2,1)} %bitcast.57, bf16[2560,384]{1,0:T(8,128)(2,1)} %get-tuple-element.70.mixed_ref, bf16[256,2048]{1,0:T(8,128)(2,1)} %bitcast.65), custom_call_target="tpu_custom_call" | custom-call | flops 5368709120 | bytes 15728640 | tf_op jit(solution)/shard_map/output_backward/pallas_call | solution.py:1438
  463.2 27.9 %mixer_backward.1 = (bf16[2560,768]{1,0:T(8,128)(2,1)}, f32[1,256]{1,0:T(1,128)}, bf16[8,64,1408]{2,1,0:T(8,128)(2,1)}, f32[64,2048]{1,0:T(8,128)}) custom-call(s32[8,128]{1,0:T(8,128)} %get-tuple-element.65.cut_ref, f32[2560,768]{1,0:T(8,128)} %get-tuple-element.83.qfi_ref, f32[1,256]{1,0:T(1,128)} %get-tuple-element.68.gap_ref, ...), custom_call_target="tpu_custom_call" | custom-call | flops 2013265920 | bytes 18350080 | tf_op jit(solution)/shard_map/mixer_backward/pallas_call | solution.py:1279
  491.1 13.6 %convolution_convert_fusion = bf16[2048,768]{1,0:T(8,128)(2,1)} fusion(bf16[2560,2048]{1,0:T(8,128)(2,1)} %bitcast.47, bf16[2560,768]{1,0:T(8,128)(2,1)} %get-tuple-element.96), kind=kOutput, calls=%fused_computation | convolution fusion | flops 8054636544 | bytes 17563648 | tf_op jit(solution)/shard_map/dot_general | solution.py:20
  504.7 53.7 %product_scatter.7 = bf16[5,64,2048]{2,1,0:T(8,128)(2,1)} custom-call(bf16[8,5,64,768]{3,2,1,0:T(8,128)(2,1)} %bitcast.48, bf16[2048,768]{1,0:T(8,128)(2,1)} %bitcast.50, bf16[5,64,2048]{2,1,0:T(8,128)(2,1)} %bitcast.39, f32[5,64,2048]{2,1,0:T(8,128)} %get-tuple-element.97.refs_3_), custom_call_target="tpu_custom_call" | custom-call | flops 8053063680 | bytes 183500800 | tf_op jit(solution)/shard_map/product_scatter/pallas_call | solution.py:937
  558.5 4.5 finish.3
  563.0 1.3 convert_element_type.24
  564.3 1.5 broadcast_multiply_fusion
  565.8 1.7 reduce-scatter.8.cloned.1.call-done
  568.1 14.7 %exit_plane.1 = (bf16[8,64,768]{2,1,0:T(8,128)(2,1)}, f32[4,2,8,256]{3,2,1,0:T(8,128)}) custom-call(bf16[8,64,768]{2,1,0:T(8,128)(2,1)} %bitcast.43, f32[8,256]{1,0:T(8,128)} %broadcast_in_dim.31.gap_ref), custom_call_target="tpu_custom_call" | custom-call | tf_op jit(solution)/shard_map/exit_plane/pallas_call | solution.py:583
  582.8 2.9 finish.2
  585.6 0.9 slice_reduce_fusion
  587.1 1.1 copy.36
  588.1 1.1 copy.37
  (36 shorter events, 5.3 us)
Async XLA Ops:
  7.2 91.9 %all-gather.9.cloned.1.call-start = ((), (), s32[]{:S(2)}) async-start(), calls=%async_computation.8 | async-start | bytes 1310720 | tf_op jit(solution)/shard_map/all_gather | solution.py:1547
  9.7 231.9 %all-gather.5.cloned.1.call-start = ((), (), s32[]{:S(2)}) async-start(), calls=%async_computation.3 | async-start | bytes 7208960 | tf_op jit(solution)/shard_map/all_gather | solution.py:1454
  99.0 169.8 %all-gather.7.cloned.1.call-start = ((), (), s32[]{:S(2)}) async-start(), calls=%async_computation.4 | async-start | bytes 3604480 | tf_op jit(solution)/shard_map/all_gather | solution.py:1454
  144.5 307.4 %reduce-scatter.4.cloned.1.call-start = ((), (), s32[]{:S(2)}) async-start(), calls=%async_computation.5 | async-start | bytes 3604480 | tf_op jit(solution)/shard_map/reduce_scatter | solution.py:1458
  294.2 169.0 %reduce-scatter.6.cloned.1.call-start = ((), (), s32[]{:S(2)}) async-start(), calls=%async_computation.6 | async-start | bytes 7208960 | tf_op jit(solution)/shard_map/reduce_scatter | solution.py:1458
  350.1 217.3 %reduce-scatter.8.cloned.1.call-start = ((), (), s32[]{:S(2)}) async-start(), calls=%async_computation.7 | async-start | bytes 3932160 | tf_op jit(solution)/shard_map/reduce_scatter | solution.py:1458
  558.4 4.6 copy-start.3
  558.4 5.8 copy-start.2
  558.4 5.8 copy-start.4
  558.5 9.0 %copy-start.5 = (f32[1,256]{1,0:T(1,128)S(1)}, f32[1,256]{1,0:T(1,128)}, u32[]{:S(2)}) copy-start(f32[1,256]{1,0:T(1,128)} %get-tuple-element.104) | copy-start | bytes 3076
  563.0 24.1 %copy-start = (bf16[5,64,2048]{2,1,0:T(8,128)(2,1)S(1)}, bf16[5,64,2048]{2,1,0:T(8,128)(2,1)}, u32[]{:S(2)}) copy-start(bf16[5,64,2048]{2,1,0:T(8,128)(2,1)} %get-tuple-element.82) | copy-start | bytes 3932164
  564.3 23.9 %copy-start.1 = (bf16[5,64,2048]{2,1,0:T(8,128)(2,1)S(1)}, bf16[5,64,2048]{2,1,0:T(8,128)(2,1)}, u32[]{:S(2)}) copy-start(bf16[5,64,2048]{2,1,0:T(8,128)(2,1)} %product_scatter.7) | copy-start | bytes 3932164
Sparse Core Ops, SparseCore 0:
  10.2 33.6 all-gather.8
  99.1 105.6 all-gather.4
  206.4 57.4 all-gather.6
  294.3 54.6 reduce-scatter.3
  351.1 102.0 reduce-scatter.5
  504.8 62.5 reduce-scatter.7
